TPU v7x, 32 devices: a whole 2x2x4 slice. The times are simulated.
32 devices in a mesh: tok: 32 (over z, y, x, core).
Axes of the slice: x: 2, y: 2, z: 4, core: 2. Of those that a mesh axis runs over, the one named last changes fastest.
Arguments:
- tokens: bfloat16 [2, 36864, 768], P(None, 'tok'), may hold values from -6 to 6
- segments: int32 [2, 32, 1152], P(None, 'tok'), may hold values from 0 to 23, never falling along the last dimension, each value on 1 to 1024 neighbouring positions
- cotangent: bfloat16 [2, 36864, 768], P(None, 'tok'), may hold values from -6 to 6
- w_proj: bfloat16 [768, 1536], P('tok'), may hold values from -0.21875 to 0.21875
- w_depth: bfloat16 [768, 9], P('tok'), may hold values from -2 to 2
- w_point: bfloat16 [768, 384], P('tok'), may hold values from -0.21875 to 0.21875
- w_kernel: bfloat16 [384, 54], P('tok'), may hold values from -0.4375 to 0.4375
- w_out: bfloat16 [768, 768], P('tok'), may hold values from -0.625 to 0.625
- attn_gain: bfloat16 [768], P('tok'), may hold values from 0.5 to 1.5
- attn_shift: bfloat16 [768], P('tok'), may hold values from -3 to 3
- w_in: bfloat16 [768, 1536], P('tok'), may hold values from -0.3125 to 0.3125
- w_down: bfloat16 [3072, 384], P('tok'), may hold values from -0.21875 to 0.21875
- ffn_gain: bfloat16 [768], P('tok'), may hold values from 0.5 to 1.5
- ffn_shift: bfloat16 [768], P('tok'), may hold values from -3 to 3
Outputs:
- output: bfloat16 [2, 36864, 768], P(None, 'tok')
- grad_tokens: float32 [2, 36864, 768], P(None, 'tok')
- grad_proj: float32 [768, 1536], P('tok')
- grad_depth: float32 [768, 9], P('tok')
- grad_point: float32 [768, 384], P('tok')
- grad_kernel: float32 [384, 54], P('tok')
- grad_out: float32 [768, 768], P('tok')
- grad_attn_gain: float32 [768], P('tok')
- grad_attn_shift: float32 [768], P('tok')
- grad_in: float32 [768, 1536], P('tok')
- grad_down: float32 [3072, 384], P('tok')
- grad_ffn_gain: float32 [768], P('tok')
- grad_ffn_shift: float32 [768], P('tok')
Inputs may be any that keep to these rules, and one draw needn't show every extreme that they name: `segments`: each block of 1152 tokens holds 24 whole sequences, numbered in order and never falling along the block; each sequence has 1 to 1024 tokens, and one in every block has exactly 1024.
All inputs are finite; a program needn't handle non-finite values.
Results may differ from a plain program's by a relative error of at most 0.012.
The roundings to bfloat16 on the way count: a program that leaves them out, or rounds other values in their place, can miss the bound.
Values may be sent and summed in bfloat16 or wider, within the bound.
A program may use at most 384 MiB of HBM per device.

v0:
```python
from functools import partial

import jax
import jax.numpy as jnp
from jax import lax
from jax.sharding import PartitionSpec as P

HEADS = 6
KERNEL = 9


norm_eps = 1e-12


def window_mask(seg_ids):
    n_rows = seg_ids.shape[0]
    reach = KERNEL // 2
    padded = jnp.pad(seg_ids, (reach, reach), constant_values=-1)
    return jnp.stack(
        [padded[offset : offset + n_rows] == seg_ids for offset in range(KERNEL)], 1
    ).astype(jnp.float32)


def window_list(field):
    n_rows = field.shape[0]
    reach = KERNEL // 2
    padded = jnp.pad(field, ((reach, reach), (0, 0)))
    return [padded[offset : offset + n_rows] for offset in range(KERNEL)]


def window_back(pieces):
    n_rows = pieces[0].shape[0]
    reach = KERNEL // 2
    summed = jnp.zeros(pieces[0].shape, jnp.float32)
    for offset, piece in enumerate(pieces):
        padded = jnp.pad(piece, ((reach, reach), (0, 0)))
        first = 2 * reach - offset
        summed = summed + padded[first : first + n_rows]
    return summed


def norm_fwd(values, gain, shift):
    centre = values - jnp.mean(values, -1, keepdims=True)
    inv_std = lax.rsqrt(jnp.mean(centre * centre, -1, keepdims=True) + norm_eps)
    normed = centre * inv_std
    return (normed * gain + shift, normed, inv_std)


def norm_back(grad_normed, normed, inv_std):
    mean_one = jnp.mean(grad_normed, -1, keepdims=True)
    mean_two = jnp.mean(grad_normed * normed, -1, keepdims=True)
    return inv_std * (grad_normed - mean_one - normed * mean_two)


def head_layout(q_rows, k_rows, v_rows, seg_ids):
    n_rows, d_half = q_rows.shape
    head_dim = d_half // HEADS
    n_blocks = max(1, n_rows // 512)
    block_len = n_rows // n_blocks
    q_blocks = q_rows.reshape(n_blocks, block_len, HEADS, head_dim)
    k_heads = k_rows.reshape(n_rows, HEADS, head_dim)
    v_heads = v_rows.reshape(n_rows, HEADS, head_dim)
    s_blocks = seg_ids.reshape(n_blocks, block_len)
    return (q_blocks, k_heads, v_heads, s_blocks, head_dim ** (-0.5))


def masked_scores(q_block, s_block, k_heads, seg_ids, score_scale):
    scores = (
        jnp.einsum("qhd,khd->hqk", q_block, k_heads, preferred_element_type=jnp.float32)
        * score_scale
    )
    return jnp.where((s_block[:, None] == seg_ids[None, :])[None], scores, -1e30)


def attend(q_rows, k_rows, v_rows, seg_ids):
    q_blocks, k_heads, v_heads, s_blocks, score_scale = head_layout(q_rows, k_rows, v_rows, seg_ids)

    def one_block(item):
        q_block, s_block = item
        scores = masked_scores(q_block, s_block, k_heads, seg_ids, score_scale)
        row_max = jnp.max(scores, -1, keepdims=True)
        exp_vals = jnp.exp(scores - row_max)
        row_sum = jnp.sum(exp_vals, -1, keepdims=True)
        probs_low = (exp_vals / row_sum).astype(jnp.bfloat16)
        context = jnp.einsum("hqk,khd->qhd", probs_low, v_heads, preferred_element_type=jnp.float32)
        return (context, (row_max + jnp.log(row_sum))[..., 0])

    context, log_sums = lax.map(one_block, (q_blocks, s_blocks))
    return (context.reshape(q_rows.shape), log_sums)


def attend_back(q_rows, k_rows, v_rows, seg_ids, log_sums, d_context):
    q_blocks, k_heads, v_heads, s_blocks, score_scale = head_layout(q_rows, k_rows, v_rows, seg_ids)
    d_blocks = d_context.reshape(q_blocks.shape)

    def one_block(carry, item):
        d_keys, d_values = carry
        q_block, s_block, lse_block, d_block = item
        scores = masked_scores(q_block, s_block, k_heads, seg_ids, score_scale)
        probs = jnp.exp(scores - lse_block[..., None])
        d_values = d_values + jnp.einsum(
            "hqk,qhd->khd", probs.astype(jnp.bfloat16), d_block, preferred_element_type=jnp.float32
        )
        d_probs = jnp.einsum("qhd,khd->hqk", d_block, v_heads, preferred_element_type=jnp.float32)
        inner_sum = jnp.sum(probs * d_probs, -1, keepdims=True)
        d_scores = (probs * (d_probs - inner_sum)).astype(jnp.bfloat16)
        d_query = (
            jnp.einsum("hqk,khd->qhd", d_scores, k_heads, preferred_element_type=jnp.float32)
            * score_scale
        )
        d_keys = (
            d_keys
            + jnp.einsum("hqk,qhd->khd", d_scores, q_block, preferred_element_type=jnp.float32)
            * score_scale
        )
        return ((d_keys, d_values), d_query)

    zero_heads = jnp.zeros(k_heads.shape, jnp.float32)
    (d_keys, d_values), d_query = lax.scan(
        one_block, (zero_heads, zero_heads), (q_blocks, s_blocks, log_sums, d_blocks)
    )
    return (
        d_query.reshape(q_rows.shape),
        d_keys.reshape(q_rows.shape),
        d_values.reshape(q_rows.shape),
    )


def forward_pass(x_rows, seg_ids, full):
    (
        w_proj,
        w_depth,
        w_point,
        w_kernel,
        w_out,
        attn_gain,
        attn_shift,
        w_in,
        w_down,
        ffn_gain,
        ffn_shift,
    ) = full
    n_rows, d_model = x_rows.shape
    d_half = d_model // 2
    valid = window_mask(seg_ids)
    merged = jnp.dot(x_rows, w_proj, preferred_element_type=jnp.float32).astype(jnp.bfloat16)
    q_rows = merged[:, :d_half]
    k_rows = merged[:, d_half : 2 * d_half]
    v_rows = merged[:, 2 * d_half : 3 * d_half]
    x_full = x_rows.astype(jnp.float32)
    depth_taps = w_depth.astype(jnp.float32)
    x_wins = window_list(x_full)
    depth = jnp.zeros((n_rows, d_model), jnp.float32)
    for offset in range(KERNEL):
        depth = depth + x_wins[offset] * valid[:, offset : offset + 1] * depth_taps[:, offset]
    depth_low = depth.astype(jnp.bfloat16)
    span_key = jnp.dot(depth_low, w_point, preferred_element_type=jnp.float32)
    mixed = (span_key * q_rows.astype(jnp.float32)).astype(jnp.bfloat16)
    logits = jnp.dot(mixed, w_kernel, preferred_element_type=jnp.float32).reshape(
        n_rows, HEADS, KERNEL
    )
    taps = jax.nn.softmax(logits, -1)
    tap_valid = taps * valid[:, None, :]
    c_wins = window_list(merged[:, 3 * d_half :].astype(jnp.float32))
    conv_out = jnp.zeros((n_rows, HEADS, d_half // HEADS), jnp.float32)
    for offset in range(KERNEL):
        conv_out = (
            conv_out
            + c_wins[offset].reshape(n_rows, HEADS, -1) * tap_valid[:, :, offset : offset + 1]
        )
    context, log_sums = attend(q_rows, k_rows, v_rows, seg_ids)
    joined = jnp.concatenate([context, conv_out.reshape(n_rows, d_half)], 1).astype(jnp.bfloat16)
    attended = jnp.dot(joined, w_out, preferred_element_type=jnp.float32)
    hidden, normed_one, inv_one = norm_fwd(
        attended + x_full, attn_gain.astype(jnp.float32), attn_shift.astype(jnp.float32)
    )
    hidden_low = hidden.astype(jnp.bfloat16)
    inner = jnp.einsum(
        "ngi,gio->ngo",
        hidden_low.reshape(n_rows, 2, d_half),
        w_in.reshape(2, d_half, -1),
        preferred_element_type=jnp.float32,
    )
    active = jax.nn.gelu(inner, approximate=False).astype(jnp.bfloat16)
    outer = jnp.einsum(
        "ngh,gho->ngo", active, w_down.reshape(2, -1, d_half), preferred_element_type=jnp.float32
    ).reshape(n_rows, d_model)
    result, normed_two, inv_two = norm_fwd(
        outer + hidden, ffn_gain.astype(jnp.float32), ffn_shift.astype(jnp.float32)
    )
    saved = (
        x_rows,
        seg_ids,
        valid,
        merged,
        depth_low,
        span_key,
        mixed,
        taps,
        tap_valid,
        log_sums,
        joined,
        normed_one,
        inv_one,
        hidden_low,
        inner,
        active,
        normed_two,
        inv_two,
    )
    return (saved, result.astype(jnp.bfloat16))


def backward_pass(saved, cot_rows, full):
    (
        w_proj,
        w_depth,
        w_point,
        w_kernel,
        w_out,
        attn_gain,
        attn_shift,
        w_in,
        w_down,
        ffn_gain,
        ffn_shift,
    ) = full
    (
        x_rows,
        seg_ids,
        valid,
        merged,
        depth_low,
        span_key,
        mixed,
        taps,
        tap_valid,
        log_sums,
        joined,
        normed_one,
        inv_one,
        hidden_low,
        inner,
        active,
        normed_two,
        inv_two,
    ) = saved
    n_rows, d_model = x_rows.shape
    d_half = d_model // 2
    q_rows = merged[:, :d_half]
    k_rows = merged[:, d_half : 2 * d_half]
    v_rows = merged[:, 2 * d_half : 3 * d_half]
    grad_top = cot_rows.astype(jnp.float32)
    g_ffn_gain = jnp.sum(grad_top * normed_two, 0)
    g_ffn_shift = jnp.sum(grad_top, 0)
    d_sum_two = norm_back(grad_top * ffn_gain.astype(jnp.float32), normed_two, inv_two)
    d_outer = d_sum_two.astype(jnp.bfloat16).reshape(n_rows, 2, d_half)
    d_active = jnp.einsum(
        "ngo,gho->ngh", d_outer, w_down.reshape(2, -1, d_half), preferred_element_type=jnp.float32
    )
    g_down = jnp.einsum(
        "ngh,ngo->gho", active, d_outer, preferred_element_type=jnp.float32
    ).reshape(-1, d_half)
    _, gelu_back = jax.vjp(partial(jax.nn.gelu, approximate=False), inner)
    d_inner = gelu_back(d_active)[0].astype(jnp.bfloat16)
    d_hidden = (
        jnp.einsum(
            "ngh,gih->ngi", d_inner, w_in.reshape(2, d_half, -1), preferred_element_type=jnp.float32
        ).reshape(n_rows, d_model)
        + d_sum_two
    )
    g_in = jnp.einsum(
        "ngi,ngh->gih",
        hidden_low.reshape(n_rows, 2, d_half),
        d_inner,
        preferred_element_type=jnp.float32,
    ).reshape(d_model, -1)
    g_attn_gain = jnp.sum(d_hidden * normed_one, 0)
    g_attn_shift = jnp.sum(d_hidden, 0)
    d_residual = norm_back(d_hidden * attn_gain.astype(jnp.float32), normed_one, inv_one)
    d_attn = d_residual.astype(jnp.bfloat16)
    d_joined = jnp.dot(d_attn, w_out.T, preferred_element_type=jnp.float32)
    g_out = jnp.dot(joined.T, d_attn, preferred_element_type=jnp.float32)
    d_context = d_joined[:, :d_half].astype(jnp.bfloat16)
    d_conv = d_joined[:, d_half:].reshape(n_rows, HEADS, -1)
    c_wins = window_list(merged[:, 3 * d_half :].astype(jnp.float32))
    d_taps = (
        jnp.stack(
            [
                jnp.sum(d_conv * c_wins[offset].reshape(n_rows, HEADS, -1), -1)
                for offset in range(KERNEL)
            ],
            -1,
        )
        * valid[:, None, :]
    )
    d_logits = (
        (taps * (d_taps - jnp.sum(taps * d_taps, -1, keepdims=True)))
        .astype(jnp.bfloat16)
        .reshape(n_rows, -1)
    )
    d_conv_vals = window_back(
        [
            (d_conv * tap_valid[:, :, offset : offset + 1]).reshape(n_rows, d_half)
            for offset in range(KERNEL)
        ]
    )
    d_mixed = jnp.dot(d_logits, w_kernel.T, preferred_element_type=jnp.float32)
    g_kernel = jnp.dot(mixed.T, d_logits, preferred_element_type=jnp.float32)
    d_span = (d_mixed * q_rows.astype(jnp.float32)).astype(jnp.bfloat16)
    dq_mixed = d_mixed * span_key
    g_point = jnp.dot(depth_low.T, d_span, preferred_element_type=jnp.float32)
    d_depth = jnp.dot(d_span, w_point.T, preferred_element_type=jnp.float32)
    depth_taps = w_depth.astype(jnp.float32)
    x_wins = window_list(x_rows.astype(jnp.float32))
    g_depth = jnp.stack(
        [
            jnp.sum(d_depth * valid[:, offset : offset + 1] * x_wins[offset], 0)
            for offset in range(KERNEL)
        ],
        1,
    )
    dx_depth = window_back(
        [
            d_depth * valid[:, offset : offset + 1] * depth_taps[:, offset]
            for offset in range(KERNEL)
        ]
    )
    dq_attn, d_keys, d_values = attend_back(q_rows, k_rows, v_rows, seg_ids, log_sums, d_context)
    d_merged = jnp.concatenate([dq_attn + dq_mixed, d_keys, d_values, d_conv_vals], 1).astype(
        jnp.bfloat16
    )
    d_tokens = (
        jnp.dot(d_merged, w_proj.T, preferred_element_type=jnp.float32) + dx_depth + d_residual
    )
    g_proj = jnp.dot(x_rows.T, d_merged, preferred_element_type=jnp.float32)
    grads = (
        g_proj,
        g_depth,
        g_point,
        g_kernel,
        g_out,
        g_attn_gain,
        g_attn_shift,
        g_in,
        g_down,
        g_ffn_gain,
        g_ffn_shift,
    )
    return (d_tokens, grads)


def shards(
    tokens,
    segments,
    cotangent,
    w_proj,
    w_depth,
    w_point,
    w_kernel,
    w_out,
    attn_gain,
    attn_shift,
    w_in,
    w_down,
    ffn_gain,
    ffn_shift,
):
    batches = tokens.shape[0]
    results = []
    input_grads = []
    sharded = None
    for batch in range(batches):
        full = (
            lax.all_gather(w_proj, "tok", axis=0, tiled=True),
            lax.all_gather(w_depth, "tok", axis=0, tiled=True),
            lax.all_gather(w_point, "tok", axis=0, tiled=True),
            lax.all_gather(w_kernel, "tok", axis=0, tiled=True),
            lax.all_gather(w_out, "tok", axis=0, tiled=True),
            lax.all_gather(attn_gain, "tok", axis=0, tiled=True),
            lax.all_gather(attn_shift, "tok", axis=0, tiled=True),
            lax.all_gather(w_in, "tok", axis=0, tiled=True),
            lax.all_gather(w_down, "tok", axis=0, tiled=True),
            lax.all_gather(ffn_gain, "tok", axis=0, tiled=True),
            lax.all_gather(ffn_shift, "tok", axis=0, tiled=True),
        )
        saved, result = forward_pass(tokens[batch], segments[batch, 0], full)
        back_full = (
            lax.all_gather(w_proj, "tok", axis=0, tiled=True),
            lax.all_gather(w_depth, "tok", axis=0, tiled=True),
            lax.all_gather(w_point, "tok", axis=0, tiled=True),
            lax.all_gather(w_kernel, "tok", axis=0, tiled=True),
            lax.all_gather(w_out, "tok", axis=0, tiled=True),
            lax.all_gather(attn_gain, "tok", axis=0, tiled=True),
            lax.all_gather(attn_shift, "tok", axis=0, tiled=True),
            lax.all_gather(w_in, "tok", axis=0, tiled=True),
            lax.all_gather(w_down, "tok", axis=0, tiled=True),
            lax.all_gather(ffn_gain, "tok", axis=0, tiled=True),
            lax.all_gather(ffn_shift, "tok", axis=0, tiled=True),
        )
        d_tokens, grads = backward_pass(saved, cotangent[batch], back_full)
        results.append(result)
        input_grads.append(d_tokens)
        (
            g_proj,
            g_depth,
            g_point,
            g_kernel,
            g_out,
            g_attn_gain,
            g_attn_shift,
            g_in,
            g_down,
            g_ffn_gain,
            g_ffn_shift,
        ) = grads
        owned = (
            lax.psum_scatter(g_proj, "tok", scatter_dimension=0, tiled=True),
            lax.psum_scatter(g_depth, "tok", scatter_dimension=0, tiled=True),
            lax.psum_scatter(g_point, "tok", scatter_dimension=0, tiled=True),
            lax.psum_scatter(g_kernel, "tok", scatter_dimension=0, tiled=True),
            lax.psum_scatter(g_out, "tok", scatter_dimension=0, tiled=True),
            lax.psum_scatter(g_attn_gain, "tok", scatter_dimension=0, tiled=True),
            lax.psum_scatter(g_attn_shift, "tok", scatter_dimension=0, tiled=True),
            lax.psum_scatter(g_in, "tok", scatter_dimension=0, tiled=True),
            lax.psum_scatter(g_down, "tok", scatter_dimension=0, tiled=True),
            lax.psum_scatter(g_ffn_gain, "tok", scatter_dimension=0, tiled=True),
            lax.psum_scatter(g_ffn_shift, "tok", scatter_dimension=0, tiled=True),
        )
        sharded = owned if sharded is None else jax.tree.map(jnp.add, sharded, owned)
    return (
        jnp.stack(results, 0),
        jnp.stack(input_grads, 0),
        sharded[0],
        sharded[1],
        sharded[2],
        sharded[3],
        sharded[4],
        sharded[5],
        sharded[6],
        sharded[7],
        sharded[8],
        sharded[9],
        sharded[10],
    )


def solution(mesh):
    in_specs = (
        P(None, "tok", None),
        P(None, "tok", None),
        P(None, "tok", None),
        P("tok", None),
        P("tok", None),
        P("tok", None),
        P("tok", None),
        P("tok", None),
        P("tok"),
        P("tok"),
        P("tok", None),
        P("tok", None),
        P("tok"),
        P("tok"),
    )
    out_specs = (
        P(None, "tok", None),
        P(None, "tok", None),
        P("tok", None),
        P("tok", None),
        P("tok", None),
        P("tok", None),
        P("tok", None),
        P("tok"),
        P("tok"),
        P("tok", None),
        P("tok", None),
        P("tok"),
        P("tok"),
    )
    return jax.shard_map(shards, mesh=mesh, in_specs=in_specs, out_specs=out_specs, check_vma=False)
```

profile of v0, /device:TPU:0, one launch (start us, length us, event | category | flops | bytes accessed | tf_op | source)
XLA Modules:
  0.0 1629.3 jit_solution(12365123535115007114)
XLA Ops:
  13.8 43.9 %all-gather = bf16[32,24,9]{1,2,0:T(8,128)(2,1)S(1)} all-gather(bf16[1,24,9]{1,2,0:T(8,128)(2,1)} %bitcast.729), channel_id=1, replica_groups=mesh['tok'=32] {'tok'}, dimensions={0}, use_global_device_ids=true | all-gather | bytes 14256 | tf_op jit(solution)/shard_map/all_gather | solution.py:376
  66.2 41.2 %all_gather.24 = bf16[768,384]{1,0:T(8,128)(2,1)} all-gather(bf16[24,384]{1,0:T(8,128)(2,1)S(1)} %copy-done.230), channel_id=1, replica_groups=mesh['tok'=32] {'tok'}, dimensions={0}, use_global_device_ids=true | all-gather | bytes 608256 | tf_op jit(solution)/shard_map/all_gather | solution.py:377
  107.4 41.0 %all-gather.1 = bf16[32,12,54]{2,1,0:T(8,128)(2,1)} all-gather(bf16[1,12,54]{2,1,0:T(8,128)(2,1)S(1)} %bitcast.730), channel_id=1, replica_groups=mesh['tok'=32] {'tok'}, dimensions={0}, use_global_device_ids=true | all-gather | bytes 42768 | tf_op jit(solution)/shard_map/all_gather | solution.py:378
  157.8 37.8 %all-reduce.51 = (bf16[768]{0:T(1024)(128)(2,1)}, bf16[768]{0:T(1024)(128)(2,1)}, bf16[768]{0:T(1024)(128)(2,1)}, bf16[768]{0:T(1024)(128)(2,1)}) all-reduce(bf16[768]{0:T(1024)(128)(2,1)} %dynamic-update-slice.1, bf16[768]{0:T(1024)(128)(2,1)} %dynamic-update-slice, ...), channel_id=1, replica_groups=mesh['tok'=32] {'tok'}, use_global_device_ids=true, to_apply=%add.39 | all-reduce | flops 3072 | bytes 12288
  219.1 9.1 add_convert_fusion.3
  229.5 9.1 add_convert_fusion.1
  284.0 47.2 %while.54 = (s32[]{:T(128)}, bf16[2,576,6,64]{1,3,2,0:T(8,128)(2,1)}, f32[2,6,576]{2,1,0:T(8,128)S(1)}, s32[2,576]{1,0:T(2,128)S(1)}, s32[1,1,1152]{2,1,0:T(1,12...) while((s32[]{:T(128)}, ...), condition=%wide.region_3.4_spmd, body=%wide.region_0.0_spmd.sunk | while | flops 1051726464 | bytes 52400500 | solution.py:88
  340.6 13.7 add_convert_fusion.7
  392.9 47.5 %while.55 = (s32[]{:T(128)}, bf16[2,576,6,64]{1,3,2,0:T(8,128)(2,1)}, f32[2,6,576]{2,1,0:T(8,128)S(1)}, s32[2,576]{1,0:T(2,128)S(1)}, s32[1,1,1152]{2,1,0:T(1,12...) while((s32[]{:T(128)}, ...), condition=%wide.region_13.14_spmd, body=%wide.region_10.13_spmd.sunk | while | flops 1051726464 | bytes 52400500 | solution.py:88
  449.7 14.1 add_convert_fusion.6
  469.8 37.3 %fusion.92 = (bf16[1152,2,1536]{2,0,1:T(8,128)(2,1)}, f32[1152,2,1536]{2,0,1:T(8,128)}, f32[2,1152,1536]{2,1,0:T(8,128)}) fusion(bf16[1152,2,384]{0,2,1:T(8,128)(2,1)S(1)} %bitcast.661, bf16[2,384,1536]{2,1,0:T(8,128)(2,1)} %bitcast.731), kind=kOutput, calls=%fused_computation.127 | convolution fusion | flops 2947940352 | bytes 39518208 | tf_op jit(solution)/shard_map/ngi,gio->ngo/dot_general | solution.py:178
  523.0 16.1 fusion.87
  551.5 37.9 %fusion.90 = (bf16[1152,2,1536]{2,0,1:T(8,128)(2,1)}, f32[1152,2,1536]{2,0,1:T(8,128)}, f32[2,1152,1536]{2,1,0:T(8,128)}) fusion(bf16[1152,2,384]{0,2,1:T(8,128)(2,1)S(1)} %bitcast.705, bf16[2,384,1536]{2,1,0:T(8,128)(2,1)S(1)} %bitcast.734), kind=kOutput, calls=%fused_computation.120 | convolution fusion | flops 2947940352 | bytes 39518208 | tf_op jit(solution)/shard_map/ngi,gio->ngo/dot_general | solution.py:178
  589.5 8.5 fusion.278
  611.3 16.7 %fusion.80 = bf16[1152,2,1536]{2,0,1:T(8,128)(2,1)} fusion(f32[1152,2,1536]{2,0,1:T(8,128)} %get-tuple-element.658, bf16[1152,2,384]{0,2,1:T(8,128)(2,1)} %bitcast.709, bf16[2,1536,384]{2,1,0:T(8,128)(2,1)} %bitcast.737, f32[2,1152,1536]{2,1,0:T(8,128)} %get-tuple-element.776), kind=kOutput, calls=%fused_computation.103 | convolution fusion | flops 2767454208 | bytes 39518208 | tf_op jit(solution)/shard_map/ngo,gho->ngh/dot_general | solution.py:258
  740.9 151.9 %while.56 = (s32[]{:T(128)}, f32[1152,6,64]{0,2,1:T(8,128)S(1)}, f32[1152,6,64]{0,2,1:T(8,128)}, f32[2,576,6,64]{1,0,3,2:T(2,128)}, bf16[2,576,6,64]{1,3,2,0:T(8...) while((s32[]{:T(128)}, f32[1152,6,64]{0,2,1:T(8,128)S(1)}, ...), condition=%wide.region_26.27_spmd.clone, body=%wide.region_24.26_spmd.clone.sunk | while | flops 2586964480 | bytes 172369360 | solution.py:119
  741.3 8.9 fusion.400
  753.4 15.3 multiply_reduce_fusion.34
  768.7 10.8 multiply_convert_fusion.6
  784.7 18.8 %dynamic_update_slice.36 = f32[2,576,6,64]{1,0,3,2:T(2,128)} dynamic-update-slice(f32[2,576,6,64]{1,0,3,2:T(2,128)} %get-tuple-element.1156, f32[1,576,6,64]{1,0,3,2:T(1,128)} %copy.681, s32[]{:T(128)} %get-tuple-element.1153, s32[]{:T(128)} %constant.89.clone.1..sunk.2, s32[]{:T(128)} %constant.89.clone.1..sunk.2, s32[]{:T(128)} %constant.89.clone.1..sunk.2) | dynamic-update-slice | bytes 1769476 | tf_op jit(solution)/shard_map/while/body/jit(dynamic_update_index_in_dim)/dynamic_update_slice | solution.py:88
  808.6 8.3 fusion.402
  816.9 8.9 fusion.400
  828.9 15.3 multiply_reduce_fusion.34
  844.2 10.8 multiply_convert_fusion.6
  860.2 18.8 %dynamic_update_slice.36 = f32[2,576,6,64]{1,0,3,2:T(2,128)} dynamic-update-slice(f32[2,576,6,64]{1,0,3,2:T(2,128)} %get-tuple-element.1156, f32[1,576,6,64]{1,0,3,2:T(1,128)} %copy.681, s32[]{:T(128)} %get-tuple-element.1153, s32[]{:T(128)} %constant.89.clone.1..sunk.2, s32[]{:T(128)} %constant.89.clone.1..sunk.2, s32[]{:T(128)} %constant.89.clone.1..sunk.2) | dynamic-update-slice | bytes 1769476 | tf_op jit(solution)/shard_map/while/body/jit(dynamic_update_index_in_dim)/dynamic_update_slice | solution.py:88
  884.1 8.8 fusion.402
  915.9 151.1 %while.57 = (s32[]{:T(128)}, f32[1152,6,64]{0,2,1:T(8,128)S(1)}, f32[1152,6,64]{0,2,1:T(8,128)}, f32[2,576,6,64]{1,0,3,2:T(2,128)}, bf16[2,576,6,64]{1,3,2,0:T(8...) while((s32[]{:T(128)}, f32[1152,6,64]{0,2,1:T(8,128)S(1)}, ...), condition=%wide.region_43.44_spmd.clone, body=%wide.region_41.43_spmd.clone.sunk | while | flops 2586964480 | bytes 172369360 | solution.py:119
  915.9 8.7 fusion.413
  927.9 15.2 multiply_reduce_fusion.35
  943.1 10.8 multiply_convert_fusion.7
  959.1 18.8 %dynamic_update_slice.37 = f32[2,576,6,64]{1,0,3,2:T(2,128)} dynamic-update-slice(f32[2,576,6,64]{1,0,3,2:T(2,128)} %get-tuple-element.1117, f32[1,576,6,64]{1,0,3,2:T(1,128)} %copy.682, s32[]{:T(128)} %get-tuple-element.1114, s32[]{:T(128)} %constant.89.clone.1..sunk.3, s32[]{:T(128)} %constant.89.clone.1..sunk.3, s32[]{:T(128)} %constant.89.clone.1..sunk.3) | dynamic-update-slice | bytes 1769476 | tf_op jit(solution)/shard_map/while/body/jit(dynamic_update_index_in_dim)/dynamic_update_slice | solution.py:88
  983.0 8.2 fusion.415
  991.3 8.7 fusion.413
  1003.2 15.2 multiply_reduce_fusion.35
  1018.4 10.8 multiply_convert_fusion.7
  1034.4 18.8 %dynamic_update_slice.37 = f32[2,576,6,64]{1,0,3,2:T(2,128)} dynamic-update-slice(f32[2,576,6,64]{1,0,3,2:T(2,128)} %get-tuple-element.1117, f32[1,576,6,64]{1,0,3,2:T(1,128)} %copy.682, s32[]{:T(128)} %get-tuple-element.1114, s32[]{:T(128)} %constant.89.clone.1..sunk.3, s32[]{:T(128)} %constant.89.clone.1..sunk.3, s32[]{:T(128)} %constant.89.clone.1..sunk.3) | dynamic-update-slice | bytes 1769476 | tf_op jit(solution)/shard_map/while/body/jit(dynamic_update_index_in_dim)/dynamic_update_slice | solution.py:88
  1058.3 8.7 fusion.415
  1097.7 10.3 convolution_add_fusion.4
  1129.8 70.6 %fusion = f32[16,54]{1,0:T(8,128)} fusion(f32[384,54]{1,0:T(8,128)S(1)} %convolution_add_fusion.8), kind=kCustom, calls=%all-reduce-scatter | all-reduce-scatter fusion | flops 27649 | bytes 86400
  1211.5 13.2 multiply_multiply_fusion
  1224.7 9.8 multiply_reduce_fusion.4
  1268.0 13.0 multiply_multiply_fusion.8
  1281.0 9.8 multiply_reduce_fusion.13
  1306.5 19.6 %fusion.129 = f32[1,1152,768]{1,2,0:T(8,128)} fusion(f32[1152,768]{0,1:T(8,128)} %copy-done.78, bf16[768,1536]{1,0:T(8,128)(2,1)} %all-gather.7.cloned.1.call-done, f32[1152,768]{0,1:T(8,128)} %get-tuple-element.676, f32[1152,768]{0,1:T(8,128)} %get-tuple-element.675, f32[1152,768]{0,1:T(8,128)} %get-tuple-element.674, ...), kind=kOutput, calls=%fused_computation.194 | convolution fusion | flops 2742681600 | bytes 44834304 | tf_op jit(solution)/shard_map/dot_general | solution.py:334
  1326.2 17.5 %fusion.130 = f32[1,1152,768]{1,2,0:T(8,128)} fusion(f32[1152,768]{0,1:T(8,128)} %copy-done.76, bf16[768,1536]{1,0:T(8,128)(2,1)} %all-gather.7.cloned.1.call-done, f32[1152,768]{0,1:T(8,128)} %get-tuple-element.694, f32[1152,768]{0,1:T(8,128)} %get-tuple-element.693, f32[1152,768]{0,1:T(8,128)} %get-tuple-element.692, ...), kind=kOutput, calls=%fused_computation.195 | convolution fusion | flops 2742681600 | bytes 44834304 | tf_op jit(solution)/shard_map/dot_general | solution.py:334
  1350.3 40.6 %all-reduce.50 = (f32[768,9]{0,1:T(8,128)S(1)}, f32[768]{0:T(1024)S(1)}, f32[768]{0:T(1024)S(1)}, f32[768]{0:T(1024)S(1)}, f32[768]{0:T(1024)S(1)}) all-reduce(f32[768,9]{0,1:T(8,128)S(1)} %copy-done.148, f32[768]{0:T(1024)S(1)} %copy-done.232, f32[768]{0:T(1024)S(1)} %copy-done.233, ...), channel_id=14, replica_groups=mesh['tok'=32] {'tok'}, use_global_device_ids=true, to_apply=%region_65.66.clone | all-reduce | flops 9984 | bytes 79872
  1422.7 87.2 %reduce-scatter.15.cloned.1.call-done = f32[24,1536]{1,0:T(8,128)} async-done(((f32[768,1536]{1,0:T(8,128)}), f32[24,1536]{1,0:T(8,128)}) %reduce-scatter.15.cloned.1.call-update) | async-done | bytes 147472 | tf_op jit(solution)/shard_map/reduce_scatter | solution.py:425
  1509.9 112.6 %reduce-scatter.19.cloned.1.call-done = f32[24,1536]{1,0:T(8,128)} async-done(((f32[768,1536]{1,0:T(8,128)}), f32[24,1536]{1,0:T(8,128)}) %reduce-scatter.19.cloned.1.call-update) | async-done | bytes 147472
  (926 shorter events, 631.1 us)
Async XLA Ops:
  7.2 243.6 %all-gather.7.cloned.1.call-start = ((), (), s32[]{:S(2)}) async-start(), calls=%async_computation.5 | async-start | bytes 2433024 | tf_op jit(solution)/shard_map/all_gather | solution.py:375
  7.9 346.4 %all-gather.9.cloned.1.call-start = ((), (), s32[]{:S(2)}) async-start(), calls=%async_computation.6 | async-start | bytes 1216512 | tf_op jit(solution)/shard_map/all_gather | solution.py:379
  8.7 461.1 %all-gather.11.cloned.1.call-start = ((), (), s32[]{:S(2)}) async-start(), calls=%async_computation.7 | async-start | bytes 2433024 | tf_op jit(solution)/shard_map/all_gather | solution.py:382
  9.4 497.6 %all-gather.13.cloned.1.call-start = ((), (), s32[]{:S(2)}) async-start(), calls=%async_computation.8 | async-start | bytes 2433024 | tf_op jit(solution)/shard_map/all_gather | solution.py:383
  10.0 1412.7 %reduce-scatter.21.cloned.1.call-start = ((), (), s32[]{:S(2)}) async-start(), calls=%async_computation.13 | async-start | bytes 1216512
  64.4 42.9 %copy-start.235 = (bf16[12,54]{1,0:T(8,128)(2,1)S(1)}, bf16[12,54]{1,0:T(8,128)(2,1)}, u32[]{:S(2)}) copy-start(bf16[12,54]{1,0:T(8,128)(2,1)} %param.28) | copy-start | bytes 3892
  66.2 152.7 %copy-start.31 = (f32[1152,768]{0,1:T(8,128)}, f32[1152,768]{0,1:T(8,128)S(1)}, u32[]{:S(2)}) copy-start(f32[1152,768]{0,1:T(8,128)S(1)} %bitcast_convert_fusion.1) | copy-start | bytes 10616836
  229.4 28.4 %copy-start.38 = (f32[1152,384]{1,0:T(8,128)}, f32[1152,384]{1,0:T(8,128)S(1)}, u32[]{:S(2)}) copy-start(f32[1152,384]{1,0:T(8,128)S(1)} %fusion.275) | copy-start | bytes 5308420
  331.3 23.0 %copy-start.114 = (s32[1,1,1152]{2,1,0:T(1,128)}, s32[1,1,1152]{2,1,0:T(1,128)S(1)}, u32[]{:S(2)}) copy-start(s32[1,1,1152]{2,1,0:T(1,128)S(1)} %get-tuple-element.1205) | copy-start | bytes 13828
  331.3 23.0 %copy-start.116 = (f32[2,6,576]{2,1,0:T(8,128)}, f32[2,6,576]{2,1,0:T(8,128)S(1)}, u32[]{:S(2)}) copy-start(f32[2,6,576]{2,1,0:T(8,128)S(1)} %get-tuple-element.1148) | copy-start | bytes 82948
  440.4 23.4 %copy-start.4 = (bf16[1152,6,64]{0,2,1:T(8,128)(2,1)}, bf16[1152,6,64]{0,2,1:T(8,128)(2,1)S(1)}, u32[]{:S(2)}) copy-start(bf16[1152,6,64]{0,2,1:T(8,128)(2,1)S(1)} %get-tuple-element.1189) | copy-start | bytes 2654212
  440.4 23.5 %copy-start.21 = (bf16[1152,6,64]{0,2,1:T(8,128)(2,1)}, bf16[1152,6,64]{0,2,1:T(8,128)(2,1)S(1)}, u32[]{:S(2)}) copy-start(bf16[1152,6,64]{0,2,1:T(8,128)(2,1)S(1)} %get-tuple-element.1191) | copy-start | bytes 2654212
  440.4 23.5 %copy-start.24 = (bf16[2,576,6,64]{1,3,2,0:T(8,128)(2,1)}, bf16[2,576,6,64]{1,3,2,0:T(8,128)(2,1)S(1)}, u32[]{:S(2)}) copy-start(bf16[2,576,6,64]{1,3,2,0:T(8,128)(2,1)S(1)} %get-tuple-element.1193) | copy-start | bytes 2654212
  440.4 23.5 %copy-start.117 = (f32[2,6,576]{2,1,0:T(8,128)}, f32[2,6,576]{2,1,0:T(8,128)S(1)}, u32[]{:S(2)}) copy-start(f32[2,6,576]{2,1,0:T(8,128)S(1)} %get-tuple-element.1109) | copy-start | bytes 82948
  465.9 48.7 %copy-start.130 = (f32[1152]{0:T(1024)}, f32[1152]{0:T(1024)S(1)}, u32[]{:S(2)}) copy-start(f32[1152]{0:T(1024)S(1)} %broadcast_multiply_fusion.11) | copy-start | bytes 13828
  469.7 37.3 %copy-start.35 = (bf16[1152,768]{0,1:T(8,128)(2,1)}, bf16[1152,768]{0,1:T(8,128)(2,1)S(1)}, u32[]{:S(2)}) copy-start(bf16[1152,768]{0,1:T(8,128)(2,1)S(1)} %fusion.155) | copy-start | bytes 5308420
  551.5 37.9 %copy-start.239 = (bf16[3072,384]{1,0:T(8,128)(2,1)S(1)}, bf16[3072,384]{1,0:T(8,128)(2,1)}, u32[]{:S(2)}) copy-start(bf16[3072,384]{1,0:T(8,128)(2,1)} %all-gather.13.cloned.1.call-done) | copy-start | bytes 7077892
  1082.2 340.5 %reduce-scatter.13.cloned.1.call-start = ((), (), s32[]{:S(2)}) async-start(), calls=%async_computation.9 | async-start | bytes 2433024 | tf_op jit(solution)/shard_map/reduce_scatter | solution.py:422
  1089.6 333.0 %reduce-scatter.17.cloned.1.call-start = ((), (), s32[]{:S(2)}) async-start(), calls=%async_computation.11 | async-start | bytes 4866048 | tf_op jit(solution)/shard_map/reduce_scatter | solution.py:426
  1108.1 401.8 %reduce-scatter.15.cloned.1.call-start = ((), (), s32[]{:S(2)}) async-start(), calls=%async_computation.10 | async-start | bytes 4866048 | tf_op jit(solution)/shard_map/reduce_scatter | solution.py:425
  1122.2 500.3 %reduce-scatter.19.cloned.1.call-start = ((), (), s32[]{:S(2)}) async-start(), calls=%async_computation.12 | async-start | bytes 4866048
  1124.8 86.5 %copy-start.72 = (bf16[768,384]{1,0:T(8,128)(2,1)S(1)}, bf16[768,384]{1,0:T(8,128)(2,1)}, u32[]{:S(2)}) copy-start(bf16[768,384]{1,0:T(8,128)(2,1)} %all_gather.24) | copy-start | bytes 1769476
  1124.8 86.5 %copy-start.174 = (f32[1152]{0:T(1024)S(1)}, f32[1152]{0:T(1024)}, u32[]{:S(2)}) copy-start(f32[1152]{0:T(1024)} %get-tuple-element.544) | copy-start | bytes 13828
  1124.8 86.5 %copy-start.176 = (f32[1152]{0:T(1024)S(1)}, f32[1152]{0:T(1024)}, u32[]{:S(2)}) copy-start(f32[1152]{0:T(1024)} %get-tuple-element.545) | copy-start | bytes 13828
  1124.8 86.5 %copy-start.178 = (f32[1152]{0:T(1024)S(1)}, f32[1152]{0:T(1024)}, u32[]{:S(2)}) copy-start(f32[1152]{0:T(1024)} %get-tuple-element.546) | copy-start | bytes 13828
  1124.8 86.5 %copy-start.180 = (f32[1152]{0:T(1024)S(1)}, f32[1152]{0:T(1024)}, u32[]{:S(2)}) copy-start(f32[1152]{0:T(1024)} %get-tuple-element.547) | copy-start | bytes 13828
  1124.9 86.5 %copy-start.182 = (f32[1152]{0:T(1024)S(1)}, f32[1152]{0:T(1024)}, u32[]{:S(2)}) copy-start(f32[1152]{0:T(1024)} %get-tuple-element.548) | copy-start | bytes 13828
  1124.9 86.5 %copy-start.184 = (f32[1152]{0:T(1024)S(1)}, f32[1152]{0:T(1024)}, u32[]{:S(2)}) copy-start(f32[1152]{0:T(1024)} %get-tuple-element.550) | copy-start | bytes 13828
  1124.9 86.5 %copy-start.186 = (f32[1152]{0:T(1024)S(1)}, f32[1152]{0:T(1024)}, u32[]{:S(2)}) copy-start(f32[1152]{0:T(1024)} %get-tuple-element.551) | copy-start | bytes 13828
  1124.9 86.5 %copy-start.188 = (f32[1152]{0:T(1024)S(1)}, f32[1152]{0:T(1024)}, u32[]{:S(2)}) copy-start(f32[1152]{0:T(1024)} %get-tuple-element.552) | copy-start | bytes 13828
  1124.9 86.5 %copy-start.194 = (f32[768]{0:T(1024)S(1)}, f32[768]{0:T(1024)}, u32[]{:S(2)}) copy-start(f32[768]{0:T(1024)} %get-tuple-element.553) | copy-start | bytes 9220
  1124.9 86.5 %copy-start.196 = (f32[768]{0:T(1024)S(1)}, f32[768]{0:T(1024)}, u32[]{:S(2)}) copy-start(f32[768]{0:T(1024)} %get-tuple-element.554) | copy-start | bytes 9220
  1124.9 86.5 %copy-start.198 = (f32[768]{0:T(1024)S(1)}, f32[768]{0:T(1024)}, u32[]{:S(2)}) copy-start(f32[768]{0:T(1024)} %get-tuple-element.555) | copy-start | bytes 9220
  1124.9 86.5 %copy-start.200 = (f32[768]{0:T(1024)S(1)}, f32[768]{0:T(1024)}, u32[]{:S(2)}) copy-start(f32[768]{0:T(1024)} %get-tuple-element.556) | copy-start | bytes 9220
  1124.9 86.5 %copy-start.202 = (f32[768]{0:T(1024)S(1)}, f32[768]{0:T(1024)}, u32[]{:S(2)}) copy-start(f32[768]{0:T(1024)} %get-tuple-element.557) | copy-start | bytes 9220
  1124.9 86.5 %copy-start.204 = (f32[768]{0:T(1024)S(1)}, f32[768]{0:T(1024)}, u32[]{:S(2)}) copy-start(f32[768]{0:T(1024)} %get-tuple-element.559) | copy-start | bytes 9220
  1125.0 86.5 %copy-start.206 = (f32[768]{0:T(1024)S(1)}, f32[768]{0:T(1024)}, u32[]{:S(2)}) copy-start(f32[768]{0:T(1024)} %get-tuple-element.560) | copy-start | bytes 9220
  1125.0 86.5 %copy-start.208 = (f32[768]{0:T(1024)S(1)}, f32[768]{0:T(1024)}, u32[]{:S(2)}) copy-start(f32[768]{0:T(1024)} %get-tuple-element.561) | copy-start | bytes 9220
  1201.7 191.0 %collective-permute-start = (f32[16,54]{1,0:T(8,128)}, f32[16,54]{1,0:T(8,128)}, u32[]{:S(2)}, u32[]{:S(2)}) collective-permute-start(f32[16,54]{1,0:T(8,128)} %fusion), channel_id=1, source_target_pairs={{0,1},{1,2},{2,3},{3,4},{4,5},{5,6},{6,7},{7,8},{8,9},{9,10},{10,1... | collective-permute-start | bytes 10376
  1203.8 193.1 %collective-permute-start.1 = (f32[16,54]{1,0:T(8,128)}, f32[16,54]{1,0:T(8,128)}, u32[]{:S(2)}, u32[]{:S(2)}) collective-permute-start(f32[16,54]{1,0:T(8,128)} %fusion), channel_id=1, source_target_pairs={{0,2},{1,3},{2,4},{3,5},{4,6},{5,7},{6,8},{7,9},{8,10},{9,11},{10,... | collective-permute-start | bytes 10376
  1205.7 210.8 %collective-permute-start.2 = (f32[16,54]{1,0:T(8,128)}, f32[16,54]{1,0:T(8,128)}, u32[]{:S(2)}, u32[]{:S(2)}) collective-permute-start(f32[16,54]{1,0:T(8,128)} %fusion), channel_id=1, source_target_pairs={{0,3},{1,4},{2,5},{3,6},{4,7},{5,8},{6,9},{7,10},{8,11},{9,12},{10... | collective-permute-start | bytes 10376
  1207.6 208.9 %collective-permute-start.3 = (f32[16,54]{1,0:T(8,128)}, f32[16,54]{1,0:T(8,128)}, u32[]{:S(2)}, u32[]{:S(2)}) collective-permute-start(f32[16,54]{1,0:T(8,128)} %fusion), channel_id=1, source_target_pairs={{0,4},{1,5},{2,6},{3,7},{4,8},{5,9},{6,10},{7,11},{8,12},{9,13},{1... | collective-permute-start | bytes 10376
  1209.5 181.4 %collective-permute-start.7 = (f32[12,54]{1,0:T(8,128)}, f32[12,54]{1,0:T(8,128)}, u32[]{:S(2)}, u32[]{:S(2)}) collective-permute-start(f32[12,54]{1,0:T(8,128)} %slice.766), channel_id=1, source_target_pairs={{0,8},{1,9},{2,10},{3,11},{4,12},{5,13},{6,14},{7,15},{8,16},{9,17... | collective-permute-start | bytes 7784
  1281.0 23.4 %copy-start.63 = (bf16[1,1152,768]{1,2,0:T(8,128)(2,1)S(1)}, bf16[1,1152,768]{1,2,0:T(8,128)(2,1)}, u32[]{:S(2)}) copy-start(bf16[1,1152,768]{1,2,0:T(8,128)(2,1)} %get-tuple-element.667) | copy-start | bytes 5308420
  1281.0 23.4 %copy-start.64 = (bf16[1,1152,768]{1,2,0:T(8,128)(2,1)S(1)}, bf16[1,1152,768]{1,2,0:T(8,128)(2,1)}, u32[]{:S(2)}) copy-start(bf16[1,1152,768]{1,2,0:T(8,128)(2,1)} %get-tuple-element.668) | copy-start | bytes 5308420
  1390.9 25.6 %collective-permute-start.4 = (f32[16,54]{1,0:T(8,128)}, f32[16,54]{1,0:T(8,128)S(1)}, u32[]{:S(2)}, u32[]{:S(2)}) collective-permute-start(f32[16,54]{1,0:T(8,128)} %fusion), channel_id=1, source_target_pairs={{0,5},{1,6},{2,7},{3,8},{4,9},{5,10},{6,11},{7,12},{8,13},{9,14},{... | collective-permute-start | bytes 10376
  1392.7 23.8 %collective-permute-start.5 = (f32[16,54]{1,0:T(8,128)}, f32[16,54]{1,0:T(8,128)S(1)}, u32[]{:S(2)}, u32[]{:S(2)}) collective-permute-start(f32[16,54]{1,0:T(8,128)} %fusion), channel_id=1, source_target_pairs={{0,6},{1,7},{2,8},{3,9},{4,10},{5,11},{6,12},{7,13},{8,14},{9,15},... | collective-permute-start | bytes 10376
  1396.9 19.6 %collective-permute-start.6 = (f32[16,54]{1,0:T(8,128)}, f32[16,54]{1,0:T(8,128)}, u32[]{:S(2)}, u32[]{:S(2)}) collective-permute-start(f32[16,54]{1,0:T(8,128)} %fusion), channel_id=1, source_target_pairs={{0,7},{1,8},{2,9},{3,10},{4,11},{5,12},{6,13},{7,14},{8,15},{9,16}... | collective-permute-start | bytes 10376
  (216 other events, 1249.3 us)
Sparse Core Ops, SparseCore 0:
  10.9 59.7 all-gather.6
  73.6 53.1 all-gather.8
  129.6 55.9 all-gather.10
  188.4 55.7 all-gather.12
  1082.3 97.8 reduce-scatter.20
  1185.9 98.5 reduce-scatter.12
  1290.6 106.4 reduce-scatter.16
  1403.2 106.6 reduce-scatter.14
  1516.0 106.4 reduce-scatter.18
where the time goes:
time: 1640 us; the launch traced here: 1630 us
  matrix products  514 us (31%)
  local copies, waits for them, and re-layouts  358 us (22%)
  blocking collectives  275 us (17%)
  other arithmetic  240 us (15%)
  waiting for transfers between devices  203 us (12%)
  starting transfers between devices  20.8 us (1%)
  between operations  18 us (1%)
    unnamed x3, blocking collectives  149 us
    unnamed x19, waiting for transfers between devices  115 us
    dot_general x8, matrix products, masked_scores(): jnp.einsum('qhd,khd->hqk', q_block, k_heads, preferred_element_type=jnp.f...  90.3 us
    reduce_scatter x1, waiting for transfers between devices, shards(): lax.psum_scatter(g_in, 'tok', scatter_dimension=0, tiled=True)  87.2 us
    dynamic_update_slice x8, local copies, waits for them, and re-layouts, attend(): context, log_sums = lax.map(one_block, (q_blocks, s_blocks))  83.1 us
    unnamed x524, local copies, waits for them, and re-layouts  75.2 us
    dot_general x2, matrix products, forward_pass(): jnp.einsum('ngi,gio->ngo', hidden_low.reshape(n_rows, 2, d_half), w_in.re...  75.2 us
    all_gather x1, blocking collectives, shards(): lax.all_gather(w_depth, 'tok', axis=0, tiled=True)  43.9 us
  transfers between devices with their start and end apart: 17, of which 2 were waited for; matrix products, arithmetic and copies ran while one was open for 37% of the time, Pallas kernels for 0%

commit v1 on v0

v1 whole, which is shorter than its diff:
```python
from functools import partial

import jax
import jax.numpy as jnp
from jax import lax
from jax.experimental import pallas as pl
from jax.experimental.pallas import tpu as pltpu
from jax.sharding import PartitionSpec as P

HEADS = 6
KERNEL = 9
REACH = 4
SEG_MOST = 1024
NORM_EPS = 1e-12
F32 = jnp.float32
BF16 = jnp.bfloat16
NT = (((1,), (1,)), ((), ()))
NN = (((1,), (0,)), ((), ()))
TN = (((0,), (0,)), ((), ()))
VMEM_CAP = 62 * 1024 * 1024


def mm(a, b, dims=NN):
    return lax.dot_general(a, b, dims, preferred_element_type=F32)


def lanes(shape):
    return lax.broadcasted_iota(jnp.int32, shape, 1)


def split2(v):
    hi = v.astype(BF16)
    return hi, (v - hi.astype(F32)).astype(BF16)


def split3(v):
    hi = v.astype(BF16)
    rest = v - hi.astype(F32)
    mid = rest.astype(BF16)
    return hi, mid, (rest - mid.astype(F32)).astype(BF16)


def expand_taps(tap_rows, e_ref):
    hi, lo = split2(tap_rows)
    both = jnp.concatenate([hi, lo], 0)
    return mm(both, e_ref[...], TN)


def fill_expander(e_ref):
    shape = e_ref.shape
    half = shape[1] // KERNEL
    row = lax.broadcasted_iota(jnp.int32, shape, 0) % 72
    col = lax.broadcasted_iota(jnp.int32, shape, 1)
    want = (col // half) * 8 + (col % half) // 64
    e_ref[...] = jnp.where(row == want, 1.0, 0.0).astype(BF16)


def mask_rows(segb_ref, r0, rows):
    own = segb_ref[pl.ds(8 + r0, rows), :]
    return [
        jnp.where(segb_ref[pl.ds(8 + r0 + o - REACH, rows), :] == own, 1.0, 0.0)
        for o in range(KERNEL)
    ]


def fill_segments(seg_ref, segb_ref, vt_ref):
    t = seg_ref.shape[-1]
    row = seg_ref[...]
    wide = jnp.broadcast_to(row, (128, t))
    segb_ref[0:8, :] = jnp.full((8, 128), -1.0, F32)
    segb_ref[t + 8 : t + 16, :] = jnp.full((8, 128), -1.0, F32)
    segb_ref[8 : t + 8, :] = wide.T
    tall = jnp.broadcast_to(row, (8, t))
    pos = lanes((8, t))
    for o in range(KERNEL):
        d = o - REACH
        moved = pltpu.roll(tall, (-d) % t, 1) if d else tall
        inside = (pos + d >= 0) & (pos + d < t)
        vt_ref[o] = jnp.where(inside & (moved == tall), 1.0, 0.0)


def masked_tiles(t, body):
    full = SEG_MOST // 128

    def inner(i, c):
        body(pl.multiple_of(i * 128, 128), False)
        return c

    lax.fori_loop(1, full - 1, inner, 0)

    def edge(i, c):
        idx = jnp.where(i == 0, 0, i + full - 2)
        body(pl.multiple_of(idx * 128, 128), True)
        return c

    lax.fori_loop(0, t // 128 - full + 2, edge, 0)


def kernel_a(
    s_ref, x_ref, cot_ref, seg_ref, wp_ref, wd_ref, wpt_ref, wk_ref,
    xr_ref, cotr_ref, q_ref, k_ref, v_ref, c_ref, depth_ref, span_ref, mixed_ref, taps_ref, conv_ref,
    raw, xs, segb, vt, cs, lt, e_ref, texp,
):
    t, d = x_ref.shape[1:]
    half = d // 2
    nch = d // 128
    b = pl.program_id(0)
    s = s_ref[b]

    @pl.when(b == 0)
    def _():
        fill_expander(e_ref)
        xs[:, 0:8, :] = jnp.zeros((nch, 8, 128), F32)
        xs[:, t + 8 : t + 16, :] = jnp.zeros((nch, 8, 128), F32)
        cs[:, 0:8, :] = jnp.zeros((nch // 2, 8, 128), F32)
        cs[:, t + 8 : t + 16, :] = jnp.zeros((nch // 2, 8, 128), F32)

    fill_segments(seg_ref, segb, vt)
    for src, dst in ((cot_ref, cotr_ref), (x_ref, xr_ref)):
        for j in range(nch):
            col = pl.ds(j * 128, 128)
            raw[0:t, :] = src[0, :, col].astype(F32)
            raw[t : t + 128, :] = src[0, 0:128, col].astype(F32)
            moved = raw[pl.ds(s, t), :]
            if dst is xr_ref:
                xs[j, 8 : t + 8, :] = moved
            dst[0, :, col] = moved.astype(BF16)

    def depth_tile(r0, masked):
        masks = mask_rows(segb, r0, 128) if masked else None
        for j in range(nch):
            acc = None
            for o in range(KERNEL):
                part = xs[j, pl.ds(8 + r0 + o - REACH, 128), :]
                w = wd_ref[o : o + 1, pl.ds(j * 128, 128)]
                part = part * (masks[o] * w) if masked else part * w
                acc = part if acc is None else acc + part
            depth_ref[0, pl.ds(r0, 128), pl.ds(j * 128, 128)] = acc.astype(BF16)

    masked_tiles(t, depth_tile)

    def proj_tile(i, carry):
        r0 = pl.multiple_of(i * 384, 128)
        rows = pl.ds(r0, 384)
        merged = mm(xr_ref[0, rows, :], wp_ref[...]).astype(BF16)
        q = merged[:, 0:half]
        q_ref[0, rows, :] = q
        k_ref[0, rows, :] = merged[:, half : 2 * half]
        v_ref[0, rows, :] = merged[:, 2 * half : 3 * half]
        c = merged[:, 3 * half :]
        c_ref[0, rows, :] = c
        for j in range(nch // 2):
            cs[j, pl.ds(8 + r0, 384), :] = c[:, j * 128 : (j + 1) * 128].astype(F32)
        span = mm(depth_ref[0, rows, :], wpt_ref[...])
        span_ref[0, rows, :] = span
        mixed = (span * q.astype(F32)).astype(BF16)
        mixed_ref[0, rows, :] = mixed
        lt[:, rows] = mm(wk_ref[...], mixed, NT)
        return carry

    lax.fori_loop(0, t // 384, proj_tile, 0)

    logits = [lt[o * 8 : o * 8 + 8, :] for o in range(KERNEL)]
    top = logits[0]
    for o in range(1, KERNEL):
        top = jnp.maximum(top, logits[o])
    exps = [jnp.exp(v - top) for v in logits]
    total = exps[0]
    for o in range(1, KERNEL):
        total = total + exps[o]
    inv = 1.0 / total
    for o in range(KERNEL):
        tap = exps[o] * inv
        taps_ref[0, o * 8 : o * 8 + 8, :] = tap
        lt[o * 8 : o * 8 + 8, :] = tap * vt[o]

    def conv_tile(i, carry):
        r0 = pl.multiple_of(i * 128, 128)
        rows = pl.ds(r0, 128)
        texp[...] = expand_taps(lt[:, rows], e_ref)
        for j in range(nch // 2):
            acc = None
            for o in range(KERNEL):
                part = cs[j, pl.ds(8 + r0 + o - REACH, 128), :] * texp[:, o * half + j * 128 : o * half + (j + 1) * 128]
                acc = part if acc is None else acc + part
            conv_ref[0, rows, pl.ds(j * 128, 128)] = acc.astype(BF16)
        return carry

    lax.fori_loop(0, t // 128, conv_tile, 0)


def whole(*shape):
    return pl.BlockSpec(shape, lambda *_: (0,) * len(shape), pipeline_mode=pl.Buffered(1))


def per_block(*shape):
    return pl.BlockSpec((1,) + shape, lambda b, *_: (b,) + (0,) * len(shape))


def params(n):
    return pltpu.CompilerParams(dimension_semantics=("arbitrary",) * n, vmem_limit_bytes=VMEM_CAP)


def stage_a(s, x, cot, segr, wp, wd, wpt, wk):
    mb, t, d = x.shape
    half = d // 2
    sds = jax.ShapeDtypeStruct
    out = [
        ((t, d), BF16), ((t, d), BF16), ((t, half), BF16), ((t, half), BF16), ((t, half), BF16), ((t, half), BF16),
        ((t, d), BF16), ((t, half), F32), ((t, half), BF16), ((72, t), F32), ((t, half), BF16),
    ]
    return pl.pallas_call(
        kernel_a,
        out_shape=[sds((mb,) + sh, dt) for sh, dt in out],
        grid_spec=pltpu.PrefetchScalarGridSpec(
            num_scalar_prefetch=1,
            grid=(mb,),
            in_specs=[
                per_block(t, d), per_block(t, d),
                pl.BlockSpec((pl.Squeezed(), 1, t), lambda b, *_: (b, 0, 0)),
                whole(*wp.shape), whole(*wd.shape), whole(*wpt.shape), whole(*wk.shape),
            ],
            out_specs=[per_block(*sh) for sh, _ in out],
            scratch_shapes=[
                pltpu.VMEM((t + 128, 128), F32),
                pltpu.VMEM((d // 128, t + 16, 128), F32),
                pltpu.VMEM((t + 16, 128), F32),
                pltpu.VMEM((KERNEL, 8, t), F32),
                pltpu.VMEM((half // 128, t + 16, 128), F32),
                pltpu.VMEM((72, t), F32),
                pltpu.VMEM((144, KERNEL * half), BF16),
                pltpu.VMEM((128, KERNEL * half), F32),
            ],
        ),
        compiler_params=params(1),
        name="mix_fwd",
    )(s, x, cot, segr, wp, wd, wpt, wk)


QT = 256


def seg_codes(segb, first):
    lane = lanes(segb.shape) - first
    hot = segb == lane.astype(F32)
    inside = (lane >= 0) & (lane < 24)
    return jnp.where(hot & inside, 1.0, 0.0), jnp.where(inside & ~hot, -1e30, 0.0)


def kernel_b(segt_ref, q_ref, k_ref, v_ref, ctx_ref, lse_ref):
    t = q_ref.shape[1]
    tail = t - SEG_MOST
    low_half = lanes((1, 128)) < 64

    def finish(rows, outs, tops):
        both = jnp.where(low_half, outs[0], outs[1])
        sums = jnp.where(low_half, outs[1], outs[0])
        ctx_ref[0, rows, :] = (both / pltpu.roll(sums, 64, 1)).astype(BF16)
        lse_ref[0, rows, :] = jnp.where(low_half, tops[1], tops[0]) + jnp.log(sums)

    def one(q, k, v):
        scores = mm(q, k, NT)
        top = jnp.max(scores, -1, keepdims=True)
        return mm(jnp.exp(scores - top).astype(BF16), v), top

    k = k_ref[0, 0:SEG_MOST, :]
    v = v_ref[0, 0:SEG_MOST, :]
    one_b = jnp.ones((), BF16)
    vs = (jnp.where(low_half, v, one_b), jnp.where(low_half, one_b, v))

    def tile(i, carry):
        rows = pl.ds(pl.multiple_of(i * QT, QT), QT)
        q = q_ref[0, rows, :] * 0.125
        zero = jnp.zeros((), BF16)
        outs = [one(jnp.where(low_half, q, zero), k, vs[0]), one(jnp.where(low_half, zero, q), k, vs[1])]
        finish(rows, [o[0] for o in outs], [o[1] for o in outs])
        return carry

    lax.fori_loop(0, SEG_MOST // QT, tile, 0)
    rows = pl.ds(SEG_MOST, tail)
    q = q_ref[0, rows, :] * 0.125
    kt = k_ref[0, rows, :]
    vt = v_ref[0, rows, :]
    segb = jnp.broadcast_to(segt_ref[...], (128, tail)).T
    outs = []
    for h in range(2):
        hot, pen = seg_codes(segb, 64 - 64 * h)
        mine = low_half if h == 0 else ~low_half
        outs.append(
            one(
                jnp.where(mine, q, pen.astype(BF16)),
                jnp.where(mine, kt, hot.astype(BF16)),
                jnp.where(mine, vt, one_b),
            )
        )
    finish(rows, [o[0] for o in outs], [o[1] for o in outs])


def pair(t):
    return pl.BlockSpec((1, t, 128), lambda b, j: (b, 0, j))


def seg_tail(tail):
    return pl.BlockSpec((pl.Squeezed(), 1, tail), lambda b, *_: (b, 0, 0))


def stage_b(segt, q, k, v):
    mb, t, half = q.shape
    sds = jax.ShapeDtypeStruct
    return pl.pallas_call(
        kernel_b,
        out_shape=[sds((mb, t, half), BF16), sds((mb, t, half), F32)],
        grid=(mb, half // 128),
        in_specs=[seg_tail(t - SEG_MOST), pair(t), pair(t), pair(t)],
        out_specs=[pair(t), pair(t)],
        compiler_params=params(2),
        name="att_fwd",
    )(segt, q, k, v)


ROWS = 384


def norm_fwd(values):
    centre = values - jnp.mean(values, -1, keepdims=True)
    inv_std = lax.rsqrt(jnp.mean(centre * centre, -1, keepdims=True) + NORM_EPS)
    return centre * inv_std, inv_std


def norm_back(grad, normed, inv_std):
    one = jnp.mean(grad, -1, keepdims=True)
    two = jnp.mean(grad * normed, -1, keepdims=True)
    return inv_std * (grad - one - normed * two)


def gelu_both(x):
    z = jnp.abs(x) * 0.7071067811865476
    r = 1.0 / (1.0 + 0.3275911 * z)
    e = jnp.exp(-0.5 * (x * x))
    poly = r * (0.254829592 + r * (-0.284496736 + r * (1.421413741 + r * (-1.453152027 + r * 1.061405429))))
    tail = 0.5 * (poly * e)
    cdf = jnp.where(x < 0, tail, 1.0 - tail)
    return x * cdf, cdf + x * (e * 0.3989422804014327)


def col_sum(v):
    return jnp.sum(v, 0, keepdims=True)


def kernel_c(
    ctx_ref, conv_ref, x_ref, cot_ref, wo_ref, wi_ref, wdn_ref, ln_ref,
    out_ref, dres_ref, dctx_ref, dconv_ref, go_ref, gi_ref, gd_ref, gs_ref,
    joined, act, slope, dinner,
):
    first = (pl.program_id(0) == 0) & (pl.program_id(1) == 0)
    d = x_ref.shape[-1]
    half = d // 2
    hid = wi_ref.shape[1]

    @pl.when(first)
    def _():
        go_ref[...] = jnp.zeros_like(go_ref)
        gi_ref[...] = jnp.zeros_like(gi_ref)
        gd_ref[...] = jnp.zeros_like(gd_ref)
        gs_ref[...] = jnp.zeros_like(gs_ref)

    joined[:, 0:half] = ctx_ref[0]
    joined[:, half:] = conv_ref[0]
    gain1, shift1, gain2, shift2 = (ln_ref[i : i + 1, :] for i in range(4))
    normed1, inv1 = norm_fwd(mm(joined[...], wo_ref[...]) + x_ref[0].astype(F32))
    hidden = normed1 * gain1 + shift1
    hidden_low = hidden.astype(BF16)
    outers = []
    for g in range(2):
        cols = pl.ds(g * hid, hid)
        inner = mm(hidden_low[:, g * half : (g + 1) * half], wi_ref[g * half : (g + 1) * half, :])
        value, deriv = gelu_both(inner)
        act[:, cols] = value.astype(BF16)
        slope[:, cols] = deriv
        outers.append(mm(act[:, cols], wdn_ref[g * hid : (g + 1) * hid, :]))
    normed2, inv2 = norm_fwd(jnp.concatenate(outers, 1) + hidden)
    out_ref[0] = (normed2 * gain2 + shift2).astype(BF16)
    cot = cot_ref[0].astype(F32)
    gs_ref[2:3, :] += col_sum(cot * normed2)
    gs_ref[3:4, :] += col_sum(cot)
    d_sum = norm_back(cot * gain2, normed2, inv2)
    d_outer = d_sum.astype(BF16)
    d_hid = []
    for g in range(2):
        cols = pl.ds(g * hid, hid)
        mine = d_outer[:, g * half : (g + 1) * half]
        d_act = mm(mine, wdn_ref[g * hid : (g + 1) * hid, :], NT)
        gd_ref[:, cols] += mm(mine, act[:, cols], TN)
        dinner[:, cols] = (d_act * slope[:, cols]).astype(BF16)
        d_hid.append(mm(dinner[:, cols], wi_ref[g * half : (g + 1) * half, :], NT))
        gi_ref[g * half : (g + 1) * half, :] += mm(hidden_low[:, g * half : (g + 1) * half], dinner[:, cols], TN)
    d_hidden = jnp.concatenate(d_hid, 1) + d_sum
    gs_ref[0:1, :] += col_sum(d_hidden * normed1)
    gs_ref[1:2, :] += col_sum(d_hidden)
    d_res = norm_back(d_hidden * gain1, normed1, inv1)
    dres_ref[0] = d_res
    d_attn = d_res.astype(BF16)
    d_joined = mm(d_attn, wo_ref[...], NT)
    dctx_ref[0] = d_joined[:, 0:half].astype(BF16)
    dconv_ref[0] = d_joined[:, half:]
    go_ref[...] += mm(joined[...], d_attn, TN)


def stage_c(ctx, conv, x, cot, wo, wi, wdn, ln):
    mb, t, d = x.shape
    half = d // 2
    hid = wi.shape[1]
    sds = jax.ShapeDtypeStruct

    def tile(cols):
        return pl.BlockSpec((1, ROWS, cols), lambda b, i: (b, i, 0))

    return pl.pallas_call(
        kernel_c,
        out_shape=[
            sds((mb, t, d), BF16), sds((mb, t, d), F32), sds((mb, t, half), BF16), sds((mb, t, half), F32),
            sds((d, d), F32), sds((d, hid), F32), sds((half, 2 * hid), F32), sds((8, d), F32),
        ],
        grid=(mb, t // ROWS),
        in_specs=[
            tile(half), tile(half), tile(d), tile(d),
            whole(*wo.shape), whole(*wi.shape), whole(*wdn.shape), whole(*ln.shape),
        ],
        out_specs=[
            tile(d), tile(d), tile(half), tile(half),
            whole(d, d), whole(d, hid), whole(half, 2 * hid), whole(8, d),
        ],
        scratch_shapes=[
            pltpu.VMEM((ROWS, d), BF16),
            pltpu.VMEM((ROWS, 2 * hid), BF16),
            pltpu.VMEM((ROWS, 2 * hid), F32),
            pltpu.VMEM((ROWS, 2 * hid), BF16),
        ],
        compiler_params=params(2),
        name="ffn",
    )(ctx, conv, x, cot, wo, wi, wdn, ln)


KT = 256


def kernel_d(segt_ref, q_ref, k_ref, v_ref, ctx_ref, lse_ref, do_ref, dq_ref, dk_ref, dv_ref, qa, da, dqt):
    t = q_ref.shape[1]
    tail = t - SEG_MOST
    lane = lanes((1, 128))
    low_half = lane < 64
    one_b = jnp.ones((), BF16)
    zero_b = jnp.zeros((), BF16)

    r = lax.broadcasted_iota(jnp.int32, (256, 128), 0) % 128
    c = lax.broadcasted_iota(jnp.int32, (256, 128), 1)
    swap = jnp.where((r < 64) != (c < 64), 1.0, 0.0).astype(BF16)
    prod = do_ref[0].astype(F32) * ctx_ref[0].astype(F32)
    hi, lo = split2(prod)
    dsum = mm(jnp.concatenate([hi, lo], 1), swap)
    q8 = q_ref[0] * 0.125
    do = do_ref[0]
    for stat, src, dst in ((lse_ref[0], q8, qa), (dsum, do, da)):
        pieces = split3(-stat)
        code = jnp.where(
            (lane & 63) == 0, pieces[0], jnp.where((lane & 63) == 1, pieces[1], jnp.where((lane & 63) == 2, pieces[2], zero_b))
        )
        dst[0] = jnp.where(low_half, src, code)
        dst[1] = jnp.where(low_half, code, src)

    def run(key_rows, q_rows, h, codes):
        mark = (lane & 63) < 3
        mine = low_half if h == 0 else ~low_half
        k = k_ref[0, key_rows, :]
        v = v_ref[0, key_rows, :]
        ka = jnp.where(mine, k, jnp.where(mark, one_b, zero_b))
        va = jnp.where(mine, v, jnp.where(mark, one_b, zero_b))
        qh = qa[h, q_rows, :]
        if codes is not None:
            hot, pen = codes
            qh = qh + pen
            ka = ka + hot
        p = jnp.exp(mm(ka, qh, NT))
        dp = mm(va, da[h, q_rows, :], NT)
        ds = (p * dp).astype(BF16)
        dv = mm(p.astype(BF16), do_ref[0, q_rows, :])
        dk = mm(ds, q_ref[0, q_rows, :] * 0.125)
        return ds, dk, dv, k

    main = pl.ds(0, SEG_MOST)

    def tile(i, carry):
        rows = pl.ds(pl.multiple_of(i * KT, KT), KT)
        halves = []
        for h in range(2):
            ds, dk, dv, k = run(rows, main, h, None)
            part = mm(k[:, 64 * h : 64 * h + 64], ds, TN)
            dqt[64 * h : 64 * h + 64, :] = jnp.where(i == 0, part, dqt[64 * h : 64 * h + 64, :] + part)
            halves.append((dk, dv))
        dk_ref[0, rows, :] = jnp.where(low_half, halves[0][0], halves[1][0]).astype(BF16)
        dv_ref[0, rows, :] = jnp.where(low_half, halves[0][1], halves[1][1]).astype(BF16)
        return carry

    dqt[...] = jnp.zeros_like(dqt)
    lax.fori_loop(0, SEG_MOST // KT, tile, 0)
    dq_ref[0, main, :] = dqt[...].T * 0.125

    rows = pl.ds(SEG_MOST, tail)
    segb = jnp.broadcast_to(segt_ref[...], (128, tail)).T
    halves = []
    for h in range(2):
        hot, pen = seg_codes(segb, 64 - 64 * h + 8)
        ds, dk, dv, k = run(rows, rows, h, (hot.astype(BF16), pen.astype(BF16)))
        halves.append((dk, dv, mm(ds, k, TN)))
    for ref, i in ((dk_ref, 0), (dv_ref, 1)):
        ref[0, rows, :] = jnp.where(low_half, halves[0][i], halves[1][i]).astype(BF16)
    dq_ref[0, rows, :] = jnp.where(low_half, halves[0][2], halves[1][2]) * 0.125


def stage_d(segt, q, k, v, ctx, lse, dctx):
    mb, t, half = q.shape
    sds = jax.ShapeDtypeStruct
    return pl.pallas_call(
        kernel_d,
        out_shape=[sds((mb, t, half), F32), sds((mb, t, half), BF16), sds((mb, t, half), BF16)],
        grid=(mb, half // 128),
        in_specs=[seg_tail(t - SEG_MOST)] + [pair(t)] * 6,
        out_specs=[pair(t)] * 3,
        scratch_shapes=[
            pltpu.VMEM((2, t, 128), BF16), pltpu.VMEM((2, t, 128), BF16), pltpu.VMEM((128, SEG_MOST), F32),
        ],
        compiler_params=params(2),
        name="att_bwd",
    )(segt, q, k, v, ctx, lse, dctx)


def kernel_e(
    s_ref, seg_ref, x_ref, out_ref_in, dres_ref, dconv_ref, dq_ref, dk_ref, dv_ref,
    q_ref, c_ref, depth_ref, span_ref, mixed_ref, taps_ref, wp_ref, wd_ref, wpt_ref, wk_ref,
    gx_ref, out_ref, gp_ref, gpt_ref, gk_ref, gdep_ref,
    pad, xs, segb, vt, dcs, dts, e_ref, er_ref, texp, dlt, rt, dm, dl, gacc,
):
    t, d = x_ref.shape[1:]
    half = d // 2
    nch = d // 128
    b = pl.program_id(0)
    s = s_ref[b]

    @pl.when(b == 0)
    def _():
        fill_expander(e_ref)
        row = lax.broadcasted_iota(jnp.int32, er_ref.shape, 0)
        col = lax.broadcasted_iota(jnp.int32, er_ref.shape, 1)
        head = ((row % 768) % half) // 64
        er_ref[...] = jnp.where(col == (row // 768) * 8 + head, 1.0, 0.0).astype(BF16)
        for ref in (xs, dts, dcs):
            n = ref.shape[0]
            ref[:, 0:8, :] = jnp.zeros((n, 8, 128), F32)
            ref[:, t + 8 : t + 16, :] = jnp.zeros((n, 8, 128), F32)
        gp_ref[...] = jnp.zeros_like(gp_ref)
        gpt_ref[...] = jnp.zeros_like(gpt_ref)
        gk_ref[...] = jnp.zeros_like(gk_ref)
        gacc[...] = jnp.zeros_like(gacc)

    fill_segments(seg_ref, segb, vt)
    cw = xs
    for j in range(nch // 2):
        cols = pl.ds(j * 128, 128)
        cw[j, 8 : t + 8, :] = c_ref[0, :, cols].astype(F32)
        dcs[j, 8 : t + 8, :] = dconv_ref[0, :, cols]

    def dtap_tile(i, carry):
        r0 = pl.multiple_of(i * 128, 128)
        rows = pl.ds(r0, 128)
        acc = None
        for o in range(KERNEL):
            his, los = [], []
            for j in range(nch // 2):
                prod = cw[j, pl.ds(8 + r0 + o - REACH, 128), :] * dcs[j, pl.ds(8 + r0, 128), :]
                hi, lo = split2(prod)
                his.append(hi)
                los.append(lo)
            part = mm(jnp.concatenate(his + los, 1), er_ref[o * 768 : (o + 1) * 768, :])
            acc = part if acc is None else acc + part
        dlt[:, rows] = acc.T[0:72, :]
        return carry

    lax.fori_loop(0, t // 128, dtap_tile, 0)

    taps = [taps_ref[0, o * 8 : o * 8 + 8, :] for o in range(KERNEL)]
    dtaps = [dlt[o * 8 : o * 8 + 8, :] * vt[o] for o in range(KERNEL)]
    mean = taps[0] * dtaps[0]
    for o in range(1, KERNEL):
        mean = mean + taps[o] * dtaps[o]
    for o in range(KERNEL):
        dl[o * 8 : o * 8 + 8, :] = taps[o] * (dtaps[o] - mean)
        tv = taps[o] * vt[o]
        move = (o - REACH) % t
        rt[o * 8 : o * 8 + 8, :] = pltpu.roll(tv, move, 1) if move else tv

    def point_tile(i, carry):
        r0 = pl.multiple_of(i * 384, 128)
        rows = pl.ds(r0, 384)
        dlog = dl[:, rows].astype(BF16)
        d_mixed = mm(dlog, wk_ref[...], TN)
        gk_ref[...] += mm(dlog, mixed_ref[0, rows, :])
        d_span = (d_mixed * q_ref[0, rows, :].astype(F32)).astype(BF16)
        dm[rows, 0:half] = (dq_ref[0, rows, :] + d_mixed * span_ref[0, rows, :]).astype(BF16)
        dm[rows, half : 2 * half] = dk_ref[0, rows, :]
        dm[rows, 2 * half : 3 * half] = dv_ref[0, rows, :]
        gpt_ref[...] += mm(depth_ref[0, rows, :], d_span, TN)
        d_depth = mm(d_span, wpt_ref[...], NT)
        for j in range(nch):
            dts[j, pl.ds(8 + r0, 384), :] = d_depth[:, j * 128 : (j + 1) * 128]
        return carry

    lax.fori_loop(0, t // 384, point_tile, 0)

    def dc_tile(i, carry):
        r0 = pl.multiple_of(i * 128, 128)
        rows = pl.ds(r0, 128)
        texp[...] = expand_taps(rt[:, rows], e_ref)
        for j in range(nch // 2):
            acc = None
            for o in range(KERNEL):
                part = dcs[j, pl.ds(8 + r0 - o + REACH, 128), :] * texp[:, o * half + j * 128 : o * half + (j + 1) * 128]
                acc = part if acc is None else acc + part
            dm[rows, pl.ds(3 * half + j * 128, 128)] = acc.astype(BF16)
        return carry

    lax.fori_loop(0, t // 128, dc_tile, 0)

    for j in range(nch):
        xs[j, 8 : t + 8, :] = x_ref[0, :, pl.ds(j * 128, 128)].astype(F32)

    def proj_tile(i, carry):
        r0 = pl.multiple_of(i * 384, 128)
        rows = pl.ds(r0, 384)
        gp_ref[...] += mm(x_ref[0, rows, :], dm[rows, :], TN)
        gx = mm(dm[rows, :], wp_ref[...], NT) + dres_ref[0, rows, :]
        for j in range(nch):
            pad[j, pl.ds(r0, 384), :] = gx[:, j * 128 : (j + 1) * 128]
        return carry

    lax.fori_loop(0, t // 384, proj_tile, 0)

    def depth_tile(r0, masked):
        masks = mask_rows(segb, r0, 128) if masked else None
        for j in range(nch):
            acc = pad[j, pl.ds(r0, 128), :]
            own = dts[j, pl.ds(8 + r0, 128), :]
            for o in range(KERNEL):
                w = wd_ref[KERNEL - 1 - o : KERNEL - o, pl.ds(j * 128, 128)]
                near = dts[j, pl.ds(8 + r0 + o - REACH, 128), :]
                xw = xs[j, pl.ds(8 + r0 + o - REACH, 128), :]
                if masked:
                    near = near * masks[o]
                    xw = xw * masks[o]
                acc = acc + near * w
                term = (own * xw).reshape(16, 8, 128)
                gacc[o, :, pl.ds(j * 128, 128)] += jnp.sum(term, 0)
            pad[j, pl.ds(r0, 128), :] = acc

    masked_tiles(t, depth_tile)

    for j in range(nch):
        cols = pl.ds(j * 128, 128)
        pad[j, pl.ds(t, 128), :] = pad[j, 0:128, :]
        back = t - s
        first = pl.ds(back, 128)
        gx_ref[0, :, cols] = xs[j, 8 : t + 8, :]
        xs[j, 0:128, :] = pad[j, first, :]
        gx_ref[0, 0:128, cols] = xs[j, 0:128, :]
        gx_ref[0, 128:, cols] = pad[j, pl.ds(128 - s, t - 128), :]
        pad[j, 0:t, :] = out_ref_in[0, :, cols].astype(F32)
        pad[j, pl.ds(t, 128), :] = pad[j, 0:128, :]
        out_ref[0, 0:128, cols] = pad[j, first, :].astype(BF16)
        out_ref[0, 128:, cols] = pad[j, pl.ds(128 - s, t - 128), :].astype(BF16)

    @pl.when(b == pl.num_programs(0) - 1)
    def _():
        for o in range(KERNEL):
            gdep_ref[o : o + 1, :] = jnp.sum(gacc[o], 0, keepdims=True)


def stage_e(s, segr, x, out_r, dres, dconv, dq, dk, dv, q, c, depth, span, mixed, taps, wp, wd, wpt, wk):
    mb, t, d = x.shape
    half = d // 2
    sds = jax.ShapeDtypeStruct

    def slow(*shape):
        return pl.BlockSpec((1,) + shape, lambda b, *_: (b,) + (0,) * len(shape), pipeline_mode=pl.Buffered(1))

    return pl.pallas_call(
        kernel_e,
        out_shape=[
            sds((mb, t, d), F32), sds((mb, t, d), BF16), sds(wp.shape, F32), sds(wpt.shape, F32), sds((72, half), F32),
            sds((16, d), F32),
        ],
        grid_spec=pltpu.PrefetchScalarGridSpec(
            num_scalar_prefetch=1,
            grid=(mb,),
            in_specs=[pl.BlockSpec((pl.Squeezed(), 1, t), lambda b, *_: (b, 0, 0))]
            + [slow(t, d), slow(t, d), slow(t, d), slow(t, half), slow(t, half), slow(t, half), slow(t, half)]
            + [slow(t, half), slow(t, half), slow(t, d), slow(t, half), slow(t, half), slow(72, t)]
            + [whole(*w.shape) for w in (wp, wd, wpt, wk)],
            out_specs=[slow(t, d), slow(t, d), whole(*wp.shape), whole(*wpt.shape), whole(72, half), whole(16, d)],
            scratch_shapes=[
                pltpu.VMEM((d // 128, t + 128, 128), F32),
                pltpu.VMEM((d // 128, t + 16, 128), F32),
                pltpu.VMEM((t + 16, 128), F32),
                pltpu.VMEM((KERNEL, 8, t), F32),
                pltpu.VMEM((half // 128, t + 16, 128), F32),
                pltpu.VMEM((d // 128, t + 16, 128), F32),
                pltpu.VMEM((144, KERNEL * half), BF16),
                pltpu.VMEM((KERNEL * 768, 128), BF16),
                pltpu.VMEM((128, KERNEL * half), F32),
                pltpu.VMEM((72, t), F32),
                pltpu.VMEM((72, t), F32),
                pltpu.VMEM((t, 2 * d), BF16),
                pltpu.VMEM((72, t), F32),
                pltpu.VMEM((KERNEL, 8, d), F32),
            ],
        ),
        compiler_params=params(1),
        name="mix_bwd",
    )(s, segr, x, out_r, dres, dconv, dq, dk, dv, q, c, depth, span, mixed, taps, wp, wd, wpt, wk)


def rolled_segments(segments):
    mb, t = segments.shape
    span = t - SEG_MOST + 1
    hit = segments[:, :span] == segments[:, SEG_MOST - 1 :]
    s = jnp.sum(jnp.where(hit, jnp.arange(span, dtype=jnp.int32)[None, :], 0), 1).astype(jnp.int32)
    twice = jnp.concatenate([segments, segments[:, : t - SEG_MOST]], 1).astype(F32)
    rows = [lax.dynamic_slice(twice[b], (s[b],), (t,)) for b in range(mb)]
    return s, jnp.stack(rows)[:, None, :]


def kernel_rows(w_kernel):
    half = w_kernel.shape[0]
    heads = w_kernel.reshape(half, HEADS, KERNEL).transpose(2, 1, 0)
    return jnp.pad(heads, ((0, 0), (0, 8 - HEADS), (0, 0))).reshape(72, half)


def local_step(tokens, segments, cotangent, full):
    wp, wd, wpt, wk, wo, g1, b1, wi, wdn, g2, b2 = full
    d = tokens.shape[-1]
    s, segr = rolled_segments(segments)
    segt = segr[:, :, SEG_MOST:]
    wd_rows = jnp.pad(wd.T.astype(F32), ((0, 16 - KERNEL), (0, 0)))
    wk_rows = kernel_rows(wk)
    ln = jnp.pad(jnp.stack([g1, b1, g2, b2]).astype(F32), ((0, 4), (0, 0)))
    xr, cotr, q, k, v, c, depth, span, mixed, taps, conv = stage_a(s, tokens, cotangent, segr, wp, wd_rows, wpt, wk_rows)
    ctx, lse = stage_b(segt, q, k, v)
    out_r, dres, dctx, dconv, g_out, g_in, g_down_t, g_small = stage_c(ctx, conv, xr, cotr, wo, wi, wdn, ln)
    dq, dk, dv = stage_d(segt, q, k, v, ctx, lse, dctx)
    gx, out, g_proj, g_point, g_kernel_t, g_depth_t = stage_e(
        s, segr, xr, out_r, dres, dconv, dq, dk, dv, q, c, depth, span, mixed, taps, wp, wd_rows, wpt, wk_rows
    )
    g_kernel = g_kernel_t.reshape(KERNEL, 8, -1)[:, :HEADS].transpose(2, 1, 0).reshape(-1, HEADS * KERNEL)
    grads = (
        g_proj, g_depth_t[:KERNEL].T, g_point, g_kernel, g_out, g_small[0], g_small[1], g_in, g_down_t.T,
        g_small[2], g_small[3],
    )
    return out, gx, grads


def shards(tokens, segments, cotangent, *weights):
    full = tuple(lax.all_gather(w, "tok", axis=0, tiled=True) for w in weights)
    out, gx, grads = local_step(tokens, segments[:, 0], cotangent, full)
    owned = tuple(lax.psum_scatter(g, "tok", scatter_dimension=0, tiled=True) for g in grads)
    return (out, gx) + owned


def solution(mesh):
    rows, vec, act = P("tok", None), P("tok"), P(None, "tok", None)
    in_specs = (act, act, act, rows, rows, rows, rows, rows, vec, vec, rows, rows, vec, vec)
    out_specs = (act, act, rows, rows, rows, rows, rows, vec, vec, rows, rows, vec, vec)
    return jax.shard_map(shards, mesh=mesh, in_specs=in_specs, out_specs=out_specs, check_vma=False)
```

time: 1640 us -> 1170 us (0.71)
  matrix products: 514 us -> 0 us
  waiting for transfers between devices: 203 us -> 619 us
  local copies, waits for them, and re-layouts: 358 us -> 20.1 us
  Pallas kernels: 0 us -> 302 us
  other arithmetic: 240 us -> 1.47 us
  blocking collectives: 275 us -> 203 us
  starting transfers between devices: 20.8 us -> 0.39 us
    dot_general x64 -> x0, matrix products: 514 us -> none  [the longest x8 90.3 us: masked_scores(): jnp.einsum('qhd,khd->hqk', q_block, k_heads, preferred_element_type=jnp.f...]
    pallas_call x0 -> x5, Pallas kernels: none -> 302 us  [the longest x1 97.1 us: stage_e(): pl.pallas_call(kernel_e, out_shape=[sds((mb, t, d), F32), sds((mb, t, d),...]
    reduce_scatter x3, waiting for transfers between devices: 87.2 us -> 330 us  [shards(): lax.psum_scatter(g, 'tok', scatter_dimension=0, tiled=True)]
    unnamed x19 -> x13, waiting for transfers between devices: 115 us -> 289 us
    dynamic_update_slice x8 -> x0, local copies, waits for them, and re-layouts: 83.1 us -> none  [attend(): context, log_sums = lax.map(one_block, (q_blocks, s_blocks))]
    reduce_sum x37 -> x1, other arithmetic: 78.6 us -> 0.19 us  [rolled_segments(): jnp.sum(jnp.where(hit, jnp.arange(span, dtype=jnp.int32)[None, :], 0), 1)]
    convert_element_type x19 -> x1, other arithmetic: 75.3 us -> 0.01 us  [rolled_segments(): jnp.concatenate([segments, segments[:, :t - SEG_MOST]], 1).astype(F32)]
    unnamed x3 -> x2, blocking collectives: 149 us -> 75 us
  transfers between devices with their start and end apart: 17 -> 10, of which waited for: 2 -> 6; matrix products, arithmetic and copies ran while one was open for 37% -> 2% of each run, Pallas kernels for 0% -> 6%
where the time goes in v1:
time: 1170 us; the launch traced here: 1160 us
  waiting for transfers between devices  619 us (53%)
  Pallas kernels  302 us (26%)
  blocking collectives  203 us (17%)
  local copies, waits for them, and re-layouts  20.1 us (2%)
  between operations  18.4 us (2%)
    reduce_scatter x3, waiting for transfers between devices, shards(): lax.psum_scatter(g, 'tok', scatter_dimension=0, tiled=True)  330 us
    unnamed x13, waiting for transfers between devices  289 us
    all_gather x3, blocking collectives, shards(): lax.all_gather(w, 'tok', axis=0, tiled=True)  128 us
    pallas_call x1, Pallas kernels, stage_e(): pl.pallas_call(kernel_e, out_shape=[sds((mb, t, d), F32), sds((mb, t, d),...  97.1 us
    pallas_call x1, Pallas kernels, stage_c(): pl.pallas_call(kernel_c, out_shape=[sds((mb, t, d), BF16), sds((mb, t, d)...  86.7 us
    unnamed x2, blocking collectives  75 us
    pallas_call x1, Pallas kernels, stage_d(): pl.pallas_call(kernel_d, out_shape=[sds((mb, t, half), F32), sds((mb, t,...  47.7 us
    pallas_call x1, Pallas kernels, stage_a(): pl.pallas_call(kernel_a, out_shape=[sds((mb,) + sh, dt) for sh, dt in out...  35.7 us
  transfers between devices with their start and end apart: 10, of which 6 were waited for; matrix products, arithmetic and copies ran while one was open for 2% of the time, Pallas kernels for 6%

profile of v1, /device:TPU:0, one launch (start us, length us, event | category | flops | bytes accessed | tf_op | source)
XLA Modules:
  0.0 1163.9 jit_solution(1040001204138528669)
XLA Ops:
  7.2 0.7 all-gather.7.cloned.1.call-update
  8.0 0.7 all-gather.9.cloned.1.call-update
  8.7 0.7 all-gather.11.cloned.1.call-update
  9.4 0.5 all-gather.13.cloned.1.call-update
  10.0 0.7 copy.55
  10.7 0.2 fusion.8.s_ref
  10.9 0.6 fusion.10
  15.6 44.1 %all-gather.1 = bf16[32,12,54]{2,1,0:T(8,128)(2,1)S(1)} all-gather(bf16[1,12,54]{2,1,0:T(8,128)(2,1)} %bitcast.38), channel_id=1, replica_groups=mesh['tok'=32] {'tok'}, dimensions={0}, use_global_device_ids=true | all-gather | bytes 42768 | tf_op jit(solution)/shard_map/all_gather | solution.py:770
  59.7 0.8 copy.38
  60.5 0.7 reshape.42
  61.3 37.2 %all-gather = bf16[32,24,9]{1,2,0:T(8,128)(2,1)S(1)} all-gather(bf16[1,24,9]{1,2,0:T(8,128)(2,1)} %bitcast.39), channel_id=1, replica_groups=mesh['tok'=32] {'tok'}, dimensions={0}, use_global_device_ids=true | all-gather | bytes 14256 | tf_op jit(solution)/shard_map/all_gather | solution.py:770
  98.6 0.1 reshape.55
  98.7 0.6 slice.61.segt_ref
  99.3 0.8 dynamic-update-slice
  100.1 0.8 dynamic-update-slice.1
  100.9 0.8 dynamic-update-slice.2
  101.8 0.8 dynamic-update-slice.3
  102.6 37.4 %all-reduce.15 = (bf16[768]{0:T(1024)(128)(2,1)S(1)}, bf16[768]{0:T(1024)(128)(2,1)S(1)}, bf16[768]{0:T(1024)(128)(2,1)S(1)}, bf16[768]{0:T(1024)(128)(2,1)S(1)}) all-reduce(bf16[768]{0:T(1024)(128)(2,1)S(1)} %dynamic-update-slice.3, bf16[768]{0:T(1024)(128)(2,1)S(1)} %dynamic-update-slice.2, ...), channel_id=1, replica_groups=mesh['tok'=32] {'tok'}, use_global_device_ids=true, to_apply=%add.6 | all-reduce | flops 3072 | bytes 12288
  140.0 0.6 fusion.7.ln_ref
  140.7 0.6 pad_convert_fusion.wd_ref
  141.3 0.6 pad_bitcast_fusion.wk_ref
  141.9 46.3 %all_gather.35.wpt_ref = bf16[768,384]{1,0:T(8,128)(2,1)} all-gather(bf16[24,384]{1,0:T(8,128)(2,1)} %param.19), channel_id=1, replica_groups=mesh['tok'=32] {'tok'}, dimensions={0}, use_global_device_ids=true | all-gather | bytes 608256 | tf_op jit(solution)/shard_map/all_gather | solution.py:770
  188.2 35.7 %mix_fwd.1 = (bf16[2,1152,768]{2,1,0:T(8,128)(2,1)}, bf16[2,1152,768]{2,1,0:T(8,128)(2,1)}, bf16[2,1152,384]{2,1,0:T(8,128)(2,1)}, bf16[2,1152,384]{2,1,0:T(8,12...) custom-call(s32[2]{0:T(128)} %copy-done.2, ...), custom_call_target="tpu_custom_call" | custom-call | tf_op jit(solution)/shard_map/mix_fwd/pallas_call | solution.py:212
  223.9 35.1 %att_fwd.1 = (bf16[2,1152,384]{2,1,0:T(8,128)(2,1)}, f32[2,1152,384]{2,1,0:T(8,128)}) custom-call(f32[2,1,128]{2,1,0:T(1,128)} %slice.61.segt_ref, bf16[2,1152,384]{2,1,0:T(8,128)(2,1)} %get-tuple-element.44.q_ref, bf16[2,1152,384]{2,1,0:T(8,128)(2,1)} %get-tuple-element.45.k_ref, bf16[2,1152,384]{2,1,0:T(8,128)(2,1)} %get-tuple-element.46.v_ref), custom_call_target="tpu_custom_call" | custom-call | tf_op jit(solution)/shard_map/att_fwd/pallas_call | solution.py:310
  259.1 86.7 %ffn.1 = (bf16[2,1152,768]{2,1,0:T(8,128)(2,1)}, f32[2,1152,768]{2,1,0:T(8,128)}, bf16[2,1152,384]{2,1,0:T(8,128)(2,1)}, f32[2,1152,384]{2,1,0:T(8,128)}, f32[76...) custom-call(bf16[2,1152,384]{2,1,0:T(8,128)(2,1)} %get-tuple-element.47.ctx_ref, ...), custom_call_target="tpu_custom_call" | custom-call | tf_op jit(solution)/shard_map/ffn/pallas_call | solution.py:418
  345.8 47.7 %att_bwd.1 = (f32[2,1152,384]{2,1,0:T(8,128)}, bf16[2,1152,384]{2,1,0:T(8,128)(2,1)}, bf16[2,1152,384]{2,1,0:T(8,128)(2,1)}) custom-call(f32[2,1,128]{2,1,0:T(1,128)} %slice.61.segt_ref, bf16[2,1152,384]{2,1,0:T(8,128)(2,1)} %get-tuple-element.44.q_ref, bf16[2,1152,384]{2,1,0:T(8,128)(2,1)} %get-tuple-element.45.k_ref, ...), custom_call_target="tpu_custom_call" | custom-call | tf_op jit(solution)/shard_map/att_bwd/pallas_call | solution.py:523
  393.5 97.1 %mix_bwd.1 = (f32[2,1152,768]{2,1,0:T(8,128)}, bf16[2,1152,768]{2,1,0:T(8,128)(2,1)}, f32[768,1536]{1,0:T(8,128)}, f32[768,384]{1,0:T(8,128)}, f32[72,384]{1,0:T(8,128)}, /*index=5*/f32[16,768]{1,0:T(8,128)}) custom-call(s32[2]{0:T(128)} %copy-done.2, f32[2,1,1152]{2,1,0:T(1,128)} %copy-done, bf16[2,1152,768]{2,1,0:T(8,128)(2,1)} %get-tuple-element.43.x_ref, ...), custom_call_target="tpu_custom_call" | custom-call | tf_op jit(solution)/shard_map/mix_bwd/pallas_call | solution.py:694
  490.6 0.9 copy.54
  491.5 0.7 reshape.45
  492.3 0.5 reduce-scatter.20.cloned.1.call-update
  492.8 0.7 reduce-scatter.14.cloned.1.call-update
  493.6 0.7 reduce-scatter.12.cloned.1.call-update
  494.3 6.1 copy.47
  500.5 0.5 reduce-scatter.16.cloned.1.call-update
  501.3 37.6 %all-reduce.14 = (f32[768,9]{0,1:T(8,128)S(1)}, f32[768]{0:T(1024)S(1)}, f32[768]{0:T(1024)S(1)}, f32[768]{0:T(1024)S(1)}, f32[768]{0:T(1024)S(1)}) all-reduce(f32[768,9]{0,1:T(8,128)S(1)} %slice_bitcast_fusion, f32[768]{0:T(1024)S(1)} %get-tuple-element.115, ...), channel_id=3, replica_groups=mesh['tok'=32] {'tok'}, use_global_device_ids=true, to_apply=%region_2.3.clone | all-reduce | flops 9984 | bytes 79872
  538.9 0.6 dynamic-slice.5
  539.4 0.6 dynamic-slice.6
  540.0 0.6 dynamic-slice.7
  540.6 0.6 dynamic-slice.8
  541.2 0.7 constant_dynamic-slice_fusion.1
  541.9 68.1 %all-reduce.18.cloned.1.call-done = f32[384,54]{0,1:T(8,128)} async-done(((f32[384,54]{0,1:T(8,128)}), f32[384,54]{0,1:T(8,128)}) %all-reduce.18.cloned.1.call-update) | async-done | bytes 82960
  610.0 0.9 constant_dynamic-slice_fusion
  610.9 0.7 copy.41
  611.6 103.1 %reduce-scatter.20.cloned.1.call-done = f32[24,384]{1,0:T(8,128)} async-done(((f32[768,384]{1,0:T(8,128)}), f32[24,384]{1,0:T(8,128)}) %reduce-scatter.20.cloned.1.call-update) | async-done | bytes 36880
  714.6 104.6 %reduce-scatter.14.cloned.1.call-done = f32[24,768]{1,0:T(8,128)} async-done(((f32[768,768]{1,0:T(8,128)}), f32[24,768]{1,0:T(8,128)}) %reduce-scatter.14.cloned.1.call-update) | async-done | bytes 73744 | tf_op jit(solution)/shard_map/reduce_scatter | solution.py:772
  819.2 112.6 %reduce-scatter.12.cloned.1.call-done = f32[24,1536]{1,0:T(8,128)} async-done(((f32[768,1536]{1,0:T(8,128)}), f32[24,1536]{1,0:T(8,128)}) %reduce-scatter.12.cloned.1.call-update) | async-done | bytes 147472 | tf_op jit(solution)/shard_map/reduce_scatter | solution.py:772
  931.9 112.6 %reduce-scatter.18.cloned.1.call-done = f32[96,384]{1,0:T(8,128)} async-done(((f32[3072,384]{1,0:T(8,128)}), f32[96,384]{1,0:T(8,128)}) %reduce-scatter.18.cloned.1.call-update) | async-done | bytes 147472
  1044.5 112.4 %reduce-scatter.16.cloned.1.call-done = f32[24,1536]{1,0:T(8,128)} async-done(((f32[768,1536]{1,0:T(8,128)}), f32[24,1536]{1,0:T(8,128)}) %reduce-scatter.16.cloned.1.call-update) | async-done | bytes 147472 | tf_op jit(solution)/shard_map/reduce_scatter | solution.py:772
  (42 shorter events, 0.9 us)
Async XLA Ops:
  7.2 181.0 %all-gather.7.cloned.1.call-start = ((), (), s32[]{:S(2)}) async-start(), calls=%async_computation.5 | async-start | bytes 2433024 | tf_op jit(solution)/shard_map/all_gather | solution.py:770
  7.9 251.1 %all-gather.9.cloned.1.call-start = ((), (), s32[]{:S(2)}) async-start(), calls=%async_computation.6 | async-start | bytes 1216512 | tf_op jit(solution)/shard_map/all_gather | solution.py:770
  8.7 250.4 %all-gather.11.cloned.1.call-start = ((), (), s32[]{:S(2)}) async-start(), calls=%async_computation.7 | async-start | bytes 2433024 | tf_op jit(solution)/shard_map/all_gather | solution.py:770
  9.4 249.7 %all-gather.13.cloned.1.call-start = ((), (), s32[]{:S(2)}) async-start(), calls=%async_computation.8 | async-start | bytes 2433024 | tf_op jit(solution)/shard_map/all_gather | solution.py:770
  10.0 600.0 %all-reduce.18.cloned.1.call-start = ((), (), s32[]{:S(2)}) async-start(), calls=%async_computation.13 | async-start | bytes 172032
  10.9 177.3 %copy-start.2 = (s32[2]{0:T(128)}, s32[2]{0:T(128)S(1)}, u32[]{:S(2)}) copy-start(s32[2]{0:T(128)S(1)} %fusion.8.s_ref) | copy-start | bytes 28
  15.6 172.7 %copy-start = (f32[2,1,1152]{2,1,0:T(1,128)}, f32[2,1,1152]{2,1,0:T(1,128)S(1)}, u32[]{:S(2)}) copy-start(f32[2,1,1152]{2,1,0:T(1,128)S(1)} %broadcast_in_dim.18.seg_ref) | copy-start | bytes 27652
  492.2 222.4 %reduce-scatter.20.cloned.1.call-start = ((), (), s32[]{:S(2)}) async-start(), calls=%async_computation.14 | async-start | bytes 1216512
  492.8 326.4 %reduce-scatter.14.cloned.1.call-start = ((), (), s32[]{:S(2)}) async-start(), calls=%async_computation.10 | async-start | bytes 2433024 | tf_op jit(solution)/shard_map/reduce_scatter | solution.py:772
  493.5 438.3 %reduce-scatter.12.cloned.1.call-start = ((), (), s32[]{:S(2)}) async-start(), calls=%async_computation.9 | async-start | bytes 4866048 | tf_op jit(solution)/shard_map/reduce_scatter | solution.py:772
  494.3 550.2 %reduce-scatter.18.cloned.1.call-start = ((), (), s32[]{:S(2)}) async-start(), calls=%async_computation.12 | async-start | bytes 4866048
  500.5 0.7 copy-start.3
  500.5 0.8 copy-start.1
  500.5 656.4 %reduce-scatter.16.cloned.1.call-start = ((), (), s32[]{:S(2)}) async-start(), calls=%async_computation.11 | async-start | bytes 4866048 | tf_op jit(solution)/shard_map/reduce_scatter | solution.py:772
Sparse Core Ops, SparseCore 0:
  10.9 59.9 all-gather.6
  73.7 52.8 all-gather.8
  129.6 56.9 all-gather.10
  189.4 56.1 all-gather.12
  492.3 117.6 all-reduce.17
  615.5 99.0 reduce-scatter.19
  720.5 98.6 reduce-scatter.13
  825.3 106.5 reduce-scatter.11
  937.9 106.4 reduce-scatter.17
  1050.4 106.4 reduce-scatter.15

commit v2 on v1

--- a/solution.py
+++ b/solution.py
@@ -18,6 +18,8 @@
 NN = (((1,), (0,)), ((), ()))
 TN = (((0,), (0,)), ((), ()))
 VMEM_CAP = 62 * 1024 * 1024
+MESH = pl.DeviceIdType.MESH
+PIECE = 24
 
 
 def mm(a, b, dims=NN):
@@ -38,6 +40,239 @@
     rest = v - hi.astype(F32)
     mid = rest.astype(BF16)
     return hi, mid, (rest - mid.astype(F32)).astype(BF16)
+
+
+def partner(me, bit):
+    return me + (1 - 2 * lax.rem(lax.div(me, bit), 2)) * bit
+
+
+def flipped(me, bits, k):
+    at = me
+    for j, bit in enumerate(bits):
+        at = at + (partner(me, bit) - me) * lax.rem(lax.div(k, 1 << j), 2)
+    return at
+
+
+def bit_orders(n):
+    one = [1 << b for b in range(n.bit_length() - 1)]
+    two = one[:1] + one[2:3] + one[1:2] + one[3:] if len(one) > 2 else one
+    return one, two
+
+
+def greet(n):
+    me = lax.axis_index("tok")
+    barrier = pltpu.get_barrier_semaphore()
+    bits = bit_orders(n)[0]
+    for bit in bits:
+        pl.semaphore_signal(barrier, inc=1, device_id=(partner(me, bit),), device_id_type=MESH)
+    pl.semaphore_wait(barrier, len(bits))
+
+
+def many(count, body):
+    if count <= 4:
+        for k in range(count):
+            body(k)
+    else:
+        lax.fori_loop(0, count, lambda k, c: (body(k), c)[1], 0)
+
+
+class Gather:
+    def __init__(self, n, src, dst, order, send, recv, own):
+        self.src, self.dst, self.order = src, dst, order[::-1]
+        self.send, self.recv, self.own = send, recv, own
+        self.me = lax.axis_index("tok")
+
+    def start(self):
+        pltpu.make_async_copy(self.src, self.dst.at[self.me], self.own).start()
+        self.stage(0)
+
+    def stage(self, s):
+        to = partner(self.me, self.order[s])
+
+        def one(k):
+            at = flipped(self.me, self.order[:s], k)
+            pltpu.make_async_remote_copy(
+                src_ref=self.dst.at[at] if s else self.src,
+                dst_ref=self.dst.at[at],
+                send_sem=self.send.at[s],
+                recv_sem=self.recv.at[s],
+                device_id=(to,),
+                device_id_type=MESH,
+            ).start()
+
+        many(1 << s, one)
+
+    def wait(self, sem, s):
+        whole = self.dst.at[pl.ds(0, 1 << s)]
+        pltpu.make_async_copy(whole, whole, sem.at[s]).wait()
+
+    def step(self, s):
+        if s == 1:
+            pltpu.make_async_copy(self.src, self.dst.at[self.me], self.own).wait()
+        self.wait(self.recv, s - 1)
+        self.stage(s)
+
+    def finish(self):
+        last = len(self.order) - 1
+        self.wait(self.recv, last)
+        for s in range(last + 1):
+            self.wait(self.send, s)
+
+
+class Scatter:
+    def __init__(self, n, src, first, acc, got, order, send, recv, own):
+        self.n, self.src, self.acc, self.got, self.order = n, src, acc, got, order
+        self.rows = pl.ds(first, acc.shape[1])
+        self.send, self.recv, self.own = send, recv, own
+        self.me = lax.axis_index("tok")
+
+    def term(self, k):
+        at = flipped(self.me, self.order[::-1], k)
+        return self.src.at[at, self.rows]
+
+    def start(self):
+        half = self.n // 2
+        to = partner(self.me, self.order[0])
+
+        def one(k):
+            pltpu.make_async_remote_copy(
+                src_ref=self.term(half + k),
+                dst_ref=self.got.at[half + k],
+                send_sem=self.send.at[0],
+                recv_sem=self.recv.at[0],
+                device_id=(to,),
+                device_id_type=MESH,
+            ).start()
+
+        def mine(k):
+            pltpu.make_async_copy(self.term(k), self.acc.at[k], self.own).start()
+
+        many(half, one)
+        many(half, mine)
+
+    def held(self, s):
+        return pl.ds(self.n >> (s + 1), self.n >> (s + 1))
+
+    def wait(self, sem, s):
+        ref = self.got.at[self.held(s)]
+        pltpu.make_async_copy(ref, ref, sem.at[s]).wait()
+
+    def add(self, s):
+        if s == 0:
+            pltpu.make_async_copy(self.acc, self.acc, self.own).wait()
+        self.wait(self.recv, s)
+        count = self.n >> (s + 1)
+
+        def one(k):
+            total = self.acc[k].astype(F32) + self.got[count + k].astype(F32)
+            self.acc[k] = total.astype(BF16)
+
+        many(count, one)
+
+    def step(self, s):
+        self.add(s - 1)
+        part = self.acc.at[self.held(s)]
+        pltpu.make_async_remote_copy(
+            src_ref=part,
+            dst_ref=self.got.at[self.held(s)],
+            send_sem=self.send.at[s],
+            recv_sem=self.recv.at[s],
+            device_id=(partner(self.me, self.order[s]),),
+            device_id_type=MESH,
+        ).start()
+
+    def finish(self, out):
+        last = len(self.order) - 1
+        self.wait(self.recv, last)
+        out[self.rows, :] = self.acc[0].astype(F32) + self.got[1].astype(F32)
+        for s in range(last + 1):
+            self.wait(self.send, s)
+
+
+ANY = pl.BlockSpec(memory_space=pl.ANY)
+
+
+def remote(cid):
+    return pltpu.CompilerParams(collective_id=cid, has_side_effects=True, vmem_limit_bytes=VMEM_CAP)
+
+
+def gather_all(n, shards):
+    count = len(shards)
+    stages = n.bit_length() - 1
+    orders = bit_orders(n)
+
+    def kernel(*refs):
+        srcs, dsts, (send, recv, own) = refs[:count], refs[count : 2 * count], refs[2 * count :]
+        greet(n)
+        plans = [
+            Gather(n, srcs[i], dsts[i], orders[i % 2], send.at[i], recv.at[i], own.at[i]) for i in range(count)
+        ]
+        for g in plans:
+            g.start()
+        for s in range(1, stages):
+            for g in plans:
+                g.step(s)
+        for g in plans:
+            g.finish()
+
+    return pl.pallas_call(
+        kernel,
+        out_shape=[jax.ShapeDtypeStruct((n,) + w.shape, w.dtype) for w in shards],
+        in_specs=[ANY] * count,
+        out_specs=[ANY] * count,
+        scratch_shapes=[
+            pltpu.SemaphoreType.DMA((count, stages)), pltpu.SemaphoreType.DMA((count, stages)),
+            pltpu.SemaphoreType.DMA((count,)),
+        ],
+        compiler_params=remote(0),
+        name="gather",
+    )(*shards)
+
+
+def split_rows(rows, parts):
+    tiles = rows // 16
+    cuts = [tiles * i // parts * 16 for i in range(parts + 1)]
+    return [(a, b - a) for a, b in zip(cuts, cuts[1:]) if b > a]
+
+
+def scatter_all(n, cid, packed, parts):
+    stages = n.bit_length() - 1
+    orders = bit_orders(n)
+    cuts = [(i, a, r) for i, w in enumerate(packed) for a, r in split_rows(w.shape[1], parts)]
+    count = len(packed)
+    total = len(cuts)
+
+    def kernel(*refs):
+        srcs, outs, rest = refs[:count], refs[count : 2 * count], refs[2 * count :]
+        accs, gots, (send, recv, own) = rest[:total], rest[total : 2 * total], rest[2 * total :]
+        greet(n)
+        plans = [
+            Scatter(n, srcs[i], a, accs[j], gots[j], orders[j % 2], send.at[j], recv.at[j], own.at[j])
+            for j, (i, a, r) in enumerate(cuts)
+        ]
+        for p in plans:
+            p.start()
+        for s in range(1, stages):
+            for p in plans:
+                p.step(s)
+        for p, (i, a, r) in zip(plans, cuts):
+            p.finish(outs[i])
+
+    bufs = [(r, packed[i].shape[2]) for i, a, r in cuts]
+    return pl.pallas_call(
+        kernel,
+        out_shape=[jax.ShapeDtypeStruct(w.shape[1:], F32) for w in packed],
+        in_specs=[ANY] * count,
+        out_specs=[pl.BlockSpec(memory_space=pltpu.VMEM)] * count,
+        scratch_shapes=[pltpu.VMEM((n // 2,) + b, BF16) for b in bufs]
+        + [pltpu.VMEM((n,) + b, BF16) for b in bufs]
+        + [
+            pltpu.SemaphoreType.DMA((total, stages)), pltpu.SemaphoreType.DMA((total, stages)),
+            pltpu.SemaphoreType.DMA((total,)),
+        ],
+        compiler_params=remote(cid),
+        name="scatter",
+    )(*packed)
 
 
 def expand_taps(tap_rows, e_ref):
@@ -96,9 +331,21 @@
     lax.fori_loop(0, t // 128 - full + 2, edge, 0)
 
 
+def unpack_small(sm_ref, wd_ref, wk_ref):
+    d = sm_ref.shape[0]
+    for j in range(d // 128):
+        rows = pl.ds(j * 128, 128)
+        wd_ref[:, rows] = sm_ref[rows, 0:128].astype(F32).T[0:24, :]
+    row = lax.broadcasted_iota(jnp.int32, (d, d // 2), 0)
+    col = lax.broadcasted_iota(jnp.int32, (d, d // 2), 1)
+    piece = row % PIECE
+    pick = jnp.where((piece < PIECE // 2) & (row // PIECE * (PIECE // 2) + piece == col), 1.0, 0.0).astype(BF16)
+    wk_ref[...] = mm(sm_ref[:, 128:256], pick, TN)[0:72, :].astype(BF16)
+
+
 def kernel_a(
-    s_ref, x_ref, cot_ref, seg_ref, wp_ref, wd_ref, wpt_ref, wk_ref,
-    xr_ref, cotr_ref, q_ref, k_ref, v_ref, c_ref, depth_ref, span_ref, mixed_ref, taps_ref, conv_ref,
+    s_ref, x_ref, cot_ref, seg_ref, wp_ref, sm_ref, wpt_ref,
+    xr_ref, cotr_ref, q_ref, k_ref, v_ref, c_ref, depth_ref, span_ref, mixed_ref, taps_ref, conv_ref, wd_ref, wk_ref,
     raw, xs, segb, vt, cs, lt, e_ref, texp,
 ):
     t, d = x_ref.shape[1:]
@@ -110,6 +357,7 @@
     @pl.when(b == 0)
     def _():
         fill_expander(e_ref)
+        unpack_small(sm_ref, wd_ref, wk_ref)
         xs[:, 0:8, :] = jnp.zeros((nch, 8, 128), F32)
         xs[:, t + 8 : t + 16, :] = jnp.zeros((nch, 8, 128), F32)
         cs[:, 0:8, :] = jnp.zeros((nch // 2, 8, 128), F32)
@@ -201,7 +449,7 @@
     return pltpu.CompilerParams(dimension_semantics=("arbitrary",) * n, vmem_limit_bytes=VMEM_CAP)
 
 
-def stage_a(s, x, cot, segr, wp, wd, wpt, wk):
+def stage_a(s, x, cot, segr, wp, sm, wpt):
     mb, t, d = x.shape
     half = d // 2
     sds = jax.ShapeDtypeStruct
@@ -211,16 +459,16 @@
     ]
     return pl.pallas_call(
         kernel_a,
-        out_shape=[sds((mb,) + sh, dt) for sh, dt in out],
+        out_shape=[sds((mb,) + sh, dt) for sh, dt in out] + [sds((24, d), F32), sds((72, half), BF16)],
         grid_spec=pltpu.PrefetchScalarGridSpec(
             num_scalar_prefetch=1,
             grid=(mb,),
             in_specs=[
                 per_block(t, d), per_block(t, d),
                 pl.BlockSpec((pl.Squeezed(), 1, t), lambda b, *_: (b, 0, 0)),
-                whole(*wp.shape), whole(*wd.shape), whole(*wpt.shape), whole(*wk.shape),
+                whole(*wp.shape), whole(*sm.shape), whole(*wpt.shape),
             ],
-            out_specs=[per_block(*sh) for sh, _ in out],
+            out_specs=[per_block(*sh) for sh, _ in out] + [whole(24, d), whole(72, half)],
             scratch_shapes=[
                 pltpu.VMEM((t + 128, 128), F32),
                 pltpu.VMEM((d // 128, t + 16, 128), F32),
@@ -234,7 +482,7 @@
         ),
         compiler_params=params(1),
         name="mix_fwd",
-    )(s, x, cot, segr, wp, wd, wpt, wk)
+    )(s, x, cot, segr, wp, sm, wpt)
 
 
 QT = 256
@@ -349,10 +597,11 @@
 
 def kernel_c(
     ctx_ref, conv_ref, x_ref, cot_ref, wo_ref, wi_ref, wdn_ref, ln_ref,
-    out_ref, dres_ref, dctx_ref, dconv_ref, go_ref, gi_ref, gd_ref, gs_ref,
-    joined, act, slope, dinner,
+    out_ref, dres_ref, dctx_ref, dconv_ref, gf_ref, gs_ref,
+    joined, act, slope, dinner, go_ref, gi_ref, gd_ref,
 ):
     first = (pl.program_id(0) == 0) & (pl.program_id(1) == 0)
+    last = (pl.program_id(0) == pl.num_programs(0) - 1) & (pl.program_id(1) == pl.num_programs(1) - 1)
     d = x_ref.shape[-1]
     half = d // 2
     hid = wi_ref.shape[1]
@@ -366,7 +615,7 @@
 
     joined[:, 0:half] = ctx_ref[0]
     joined[:, half:] = conv_ref[0]
-    gain1, shift1, gain2, shift2 = (ln_ref[i : i + 1, :] for i in range(4))
+    gain1, shift1, gain2, shift2 = (ln_ref[16 + i : 17 + i, :] for i in range(4))
     normed1, inv1 = norm_fwd(mm(joined[...], wo_ref[...]) + x_ref[0].astype(F32))
     hidden = normed1 * gain1 + shift1
     hidden_low = hidden.astype(BF16)
@@ -405,11 +654,39 @@
     dconv_ref[0] = d_joined[:, half:]
     go_ref[...] += mm(joined[...], d_attn, TN)
 
-
-def stage_c(ctx, conv, x, cot, wo, wi, wdn, ln):
+    @pl.when(last)
+    def _():
+        n, _, _ = gf_ref.shape
+        rows = d // n
+        tall = 2 * hid // n
+
+        def emit(p, c):
+            at = pl.ds(pl.multiple_of(p * rows, 8), rows)
+            gi = gi_ref[at, :]
+            go = go_ref[at, :]
+            parts = [gi[:, j * half : (j + 1) * half] for j in range(hid // half)] + [go[:, 0:half], go[:, half:]]
+            gf_ref[p, tall : tall + rows * len(parts), :] = jnp.concatenate(parts, 0).astype(BF16)
+            return c
+
+        lax.fori_loop(0, n, emit, 0)
+
+        step = 4
+        wide = step * tall
+
+        def emit_down(i, c):
+            block = gd_ref[:, pl.ds(pl.multiple_of(i * wide, 128), wide)].T.astype(BF16)
+            for j in range(step):
+                gf_ref[i * step + j, 0:tall, :] = block[j * tall : (j + 1) * tall, :]
+            return c
+
+        lax.fori_loop(0, n // step, emit_down, 0)
+
+
+def stage_c(n, ctx, conv, x, cot, wo, wi, wdn, ln):
     mb, t, d = x.shape
     half = d // 2
     hid = wi.shape[1]
+    packed = (d * d + d * hid + 2 * hid * half) // (n * half)
     sds = jax.ShapeDtypeStruct
 
     def tile(cols):
@@ -419,7 +696,7 @@
         kernel_c,
         out_shape=[
             sds((mb, t, d), BF16), sds((mb, t, d), F32), sds((mb, t, half), BF16), sds((mb, t, half), F32),
-            sds((d, d), F32), sds((d, hid), F32), sds((half, 2 * hid), F32), sds((8, d), F32),
+            sds((n, packed, half), BF16), sds((8, d), F32),
         ],
         grid=(mb, t // ROWS),
         in_specs=[
@@ -428,13 +705,16 @@
         ],
         out_specs=[
             tile(d), tile(d), tile(half), tile(half),
-            whole(d, d), whole(d, hid), whole(half, 2 * hid), whole(8, d),
+            whole(n, packed, half), whole(8, d),
         ],
         scratch_shapes=[
             pltpu.VMEM((ROWS, d), BF16),
             pltpu.VMEM((ROWS, 2 * hid), BF16),
             pltpu.VMEM((ROWS, 2 * hid), F32),
             pltpu.VMEM((ROWS, 2 * hid), BF16),
+            pltpu.VMEM((d, d), F32),
+            pltpu.VMEM((d, hid), F32),
+            pltpu.VMEM((half, 2 * hid), F32),
         ],
         compiler_params=params(2),
         name="ffn",
@@ -536,9 +816,9 @@
 
 def kernel_e(
     s_ref, seg_ref, x_ref, out_ref_in, dres_ref, dconv_ref, dq_ref, dk_ref, dv_ref,
-    q_ref, c_ref, depth_ref, span_ref, mixed_ref, taps_ref, wp_ref, wd_ref, wpt_ref, wk_ref,
-    gx_ref, out_ref, gp_ref, gpt_ref, gk_ref, gdep_ref,
-    pad, xs, segb, vt, dcs, dts, e_ref, er_ref, texp, dlt, rt, dm, dl, gacc,
+    q_ref, c_ref, depth_ref, span_ref, mixed_ref, taps_ref, wp_ref, wd_ref, wpt_ref, wk_ref, gs_ref,
+    gx_ref, out_ref, gm_ref,
+    pad, xs, segb, vt, dcs, dts, e_ref, er_ref, texp, dlt, rt, dm, dl, gacc, gp_ref, gpt_ref, gk_ref, small,
 ):
     t, d = x_ref.shape[1:]
     half = d // 2
@@ -679,13 +959,41 @@
 
     @pl.when(b == pl.num_programs(0) - 1)
     def _():
+        n = gm_ref.shape[0]
+        rows = d // n
+        small[...] = jnp.zeros_like(small)
         for o in range(KERNEL):
-            gdep_ref[o : o + 1, :] = jnp.sum(gacc[o], 0, keepdims=True)
-
-
-def stage_e(s, segr, x, out_r, dres, dconv, dq, dk, dv, q, c, depth, span, mixed, taps, wp, wd, wpt, wk):
+            small[o : o + 1, :] = jnp.sum(gacc[o], 0, keepdims=True)
+        small[16:24, :] = gs_ref[...]
+        row = lax.broadcasted_iota(jnp.int32, (128, 72), 0)
+        col = lax.broadcasted_iota(jnp.int32, (128, 72), 1)
+        order = jnp.where((row < HEADS * KERNEL) & (row % KERNEL * 8 + row // KERNEL == col), 1.0, 0.0).astype(BF16)
+        gk = mm(order, gk_ref[...].astype(BF16)).astype(BF16)
+        row = lax.broadcasted_iota(jnp.int32, (half, d), 0)
+        col = lax.broadcasted_iota(jnp.int32, (half, d), 1)
+        piece = col % PIECE
+        put = jnp.where((piece < PIECE // 2) & (col // PIECE * (PIECE // 2) + piece == row), 1.0, 0.0).astype(BF16)
+        gk = mm(gk, put)
+        for j in range(nch):
+            cols = pl.ds(j * 128, 128)
+            pad[0, cols, :] = small[:, cols].T
+            pad[1, cols, :] = gk[:, j * 128 : (j + 1) * 128].T
+
+        def emit(p, c):
+            at = pl.ds(pl.multiple_of(p * rows, 8), rows)
+            gp = gp_ref[at, :]
+            parts = [gp[:, j * half : (j + 1) * half] for j in range(gp.shape[1] // half)] + [gpt_ref[at, :]]
+            parts.append(jnp.concatenate([pad[0, at, :], pad[1, at, :], jnp.zeros((rows, half - 256), F32)], 1))
+            gm_ref[p] = jnp.concatenate(parts, 0).astype(BF16)
+            return c
+
+        lax.fori_loop(0, n, emit, 0)
+
+
+def stage_e(n, s, segr, x, out_r, dres, dconv, dq, dk, dv, q, c, depth, span, mixed, taps, wp, wd, wpt, wk, gs):
     mb, t, d = x.shape
     half = d // 2
+    packed = (d * 2 * d + d * half) // (n * half) + d // n
     sds = jax.ShapeDtypeStruct
 
     def slow(*shape):
@@ -694,8 +1002,7 @@
     return pl.pallas_call(
         kernel_e,
         out_shape=[
-            sds((mb, t, d), F32), sds((mb, t, d), BF16), sds(wp.shape, F32), sds(wpt.shape, F32), sds((72, half), F32),
-            sds((16, d), F32),
+            sds((mb, t, d), F32), sds((mb, t, d), BF16), sds((n, packed, half), BF16),
         ],
         grid_spec=pltpu.PrefetchScalarGridSpec(
             num_scalar_prefetch=1,
@@ -703,8 +1010,8 @@
             in_specs=[pl.BlockSpec((pl.Squeezed(), 1, t), lambda b, *_: (b, 0, 0))]
             + [slow(t, d), slow(t, d), slow(t, d), slow(t, half), slow(t, half), slow(t, half), slow(t, half)]
             + [slow(t, half), slow(t, half), slow(t, d), slow(t, half), slow(t, half), slow(72, t)]
-            + [whole(*w.shape) for w in (wp, wd, wpt, wk)],
-            out_specs=[slow(t, d), slow(t, d), whole(*wp.shape), whole(*wpt.shape), whole(72, half), whole(16, d)],
+            + [whole(*w.shape) for w in (wp, wd, wpt, wk, gs)],
+            out_specs=[slow(t, d), slow(t, d), whole(n, packed, half)],
             scratch_shapes=[
                 pltpu.VMEM((d // 128, t + 128, 128), F32),
                 pltpu.VMEM((d // 128, t + 16, 128), F32),
@@ -720,11 +1027,15 @@
                 pltpu.VMEM((t, 2 * d), BF16),
                 pltpu.VMEM((72, t), F32),
                 pltpu.VMEM((KERNEL, 8, d), F32),
+                pltpu.VMEM(wp.shape, F32),
+                pltpu.VMEM(wpt.shape, F32),
+                pltpu.VMEM((72, half), F32),
+                pltpu.VMEM((128, d), F32),
             ],
         ),
         compiler_params=params(1),
         name="mix_bwd",
-    )(s, segr, x, out_r, dres, dconv, dq, dk, dv, q, c, depth, span, mixed, taps, wp, wd, wpt, wk)
+    )(s, segr, x, out_r, dres, dconv, dq, dk, dv, q, c, depth, span, mixed, taps, wp, wd, wpt, wk, gs)
 
 
 def rolled_segments(segments):
@@ -737,44 +1048,115 @@
     return s, jnp.stack(rows)[:, None, :]
 
 
-def kernel_rows(w_kernel):
-    half = w_kernel.shape[0]
-    heads = w_kernel.reshape(half, HEADS, KERNEL).transpose(2, 1, 0)
-    return jnp.pad(heads, ((0, 0), (0, 8 - HEADS), (0, 0))).reshape(72, half)
-
-
-def local_step(tokens, segments, cotangent, full):
-    wp, wd, wpt, wk, wo, g1, b1, wi, wdn, g2, b2 = full
+def pack_small(w_depth, w_kernel, g1, b1, g2, b2):
+    rows = w_depth.shape[0]
+    units = rows // PIECE
+    heads = w_kernel.reshape(units, PIECE // 2, HEADS, KERNEL).transpose(0, 1, 3, 2)
+    heads = jnp.pad(heads, ((0, 0), (0, PIECE // 2), (0, 0), (0, 8 - HEADS))).reshape(rows, 8 * KERNEL)
+    norms = jnp.stack([g1, b1, g2, b2], 1)
+    gap = jnp.zeros((rows, 16 - KERNEL), BF16)
+    return jnp.concatenate(
+        [w_depth, gap, norms, jnp.zeros((rows, 128 - 20), BF16), heads, jnp.zeros((rows, 128 - 8 * KERNEL), BF16)], 1
+    )
+
+
+def finish_kernel(f_ref, m_ref, gp_ref, gdep_ref, gpt_ref, gk_ref, go_ref, gi_ref, gd_ref, gs_ref):
+    half = f_ref.shape[1]
+    rows = gp_ref.shape[0]
+    tall = gd_ref.shape[0]
+    gd_ref[...] = f_ref[0:tall, :]
+    for j in range(gi_ref.shape[1] // half):
+        gi_ref[:, j * half : (j + 1) * half] = f_ref[tall + j * rows : tall + (j + 1) * rows, :]
+    tall = tall + rows * (gi_ref.shape[1] // half)
+    for j in range(2):
+        go_ref[:, j * half : (j + 1) * half] = f_ref[tall + j * rows : tall + (j + 1) * rows, :]
+    wide = gp_ref.shape[1] // half
+    for j in range(wide):
+        gp_ref[:, j * half : (j + 1) * half] = m_ref[j * rows : (j + 1) * rows, :]
+    gpt_ref[...] = m_ref[wide * rows : (wide + 1) * rows, :]
+    small = m_ref[(wide + 1) * rows : (wide + 2) * rows, 0:256]
+    gdep_ref[...] = small[:, 0:KERNEL]
+    gk_ref[...] = small[0 : rows // 2, 128 : 128 + HEADS * KERNEL]
+    gs_ref[...] = small[:, 16:24]
+
+
+def finish(n, d, hid, f, m):
+    half = d // 2
+    sds = jax.ShapeDtypeStruct
+    rows = d // n
+    return pl.pallas_call(
+        finish_kernel,
+        out_shape=[
+            sds((rows, 2 * d), F32), sds((rows, KERNEL), F32), sds((rows, half), F32), sds((half // n, HEADS * KERNEL), F32),
+            sds((rows, d), F32), sds((rows, hid), F32), sds((2 * hid // n, half), F32), sds((rows, 8), F32),
+        ],
+        name="finish",
+    )(f, m)
+
+
+def side_by_side(block, parts):
+    units, _, cols = block.shape
+    return block.reshape(units, parts, PIECE, cols).transpose(0, 2, 1, 3).reshape(units * PIECE, parts * cols)
+
+
+def native_sums(gf, gm, d, hid):
+    gf, gm = gf.astype(F32), gm.astype(F32)
+    half = d // 2
+    tall = 2 * hid * PIECE // d
+    wide = hid // half * PIECE
+    many_p = 2 * d // half
+    g_down = gf[:, :tall].reshape(-1, half)
+    g_in = side_by_side(gf[:, tall : tall + wide], hid // half)
+    g_out = side_by_side(gf[:, tall + wide :], 2)
+    g_proj = side_by_side(gm[:, : many_p * PIECE], many_p)
+    g_point = gm[:, many_p * PIECE : (many_p + 1) * PIECE].reshape(-1, half)
+    small = gm[:, (many_p + 1) * PIECE :]
+    g_kernel = small[:, : PIECE // 2, 128 : 128 + HEADS * KERNEL].reshape(half, -1)
+    small = small[:, :, 0:24].reshape(d, -1)
+    grads = [g_proj, small[:, :KERNEL], g_point, g_kernel, g_out, g_in, g_down, small[:, 16:]]
+    return [lax.psum_scatter(g, "tok", scatter_dimension=0, tiled=True) for g in grads]
+
+
+def shards(n, tokens, segments, cotangent, w_proj, w_depth, w_point, w_kernel, w_out, g1, b1, w_in, w_down, g2, b2):
     d = tokens.shape[-1]
-    s, segr = rolled_segments(segments)
+    hid = w_in.shape[1]
+    units = d // PIECE
+    own = n == units
+    if own:
+        small = pack_small(w_depth, w_kernel, g1, b1, g2, b2)
+        full = gather_all(n, [w_proj, w_in, small, w_down, w_point, w_out])
+        wp, wi, sm, wdn, wpt, wo = [w.reshape(-1, w.shape[2]) for w in full]
+    else:
+        given = [w_proj, w_in, w_down, w_point, w_out, w_depth, w_kernel, g1, b1, g2, b2]
+        wp, wi, wdn, wpt, wo, *rest = [lax.all_gather(w, "tok", axis=0, tiled=True) for w in given]
+        sm = pack_small(*rest)
+    s, segr = rolled_segments(segments[:, 0])
     segt = segr[:, :, SEG_MOST:]
-    wd_rows = jnp.pad(wd.T.astype(F32), ((0, 16 - KERNEL), (0, 0)))
-    wk_rows = kernel_rows(wk)
-    ln = jnp.pad(jnp.stack([g1, b1, g2, b2]).astype(F32), ((0, 4), (0, 0)))
-    xr, cotr, q, k, v, c, depth, span, mixed, taps, conv = stage_a(s, tokens, cotangent, segr, wp, wd_rows, wpt, wk_rows)
+    xr, cotr, q, k, v, c, depth, span, mixed, taps, conv, wd_rows, wk_rows = stage_a(
+        s, tokens, cotangent, segr, wp, sm, wpt
+    )
     ctx, lse = stage_b(segt, q, k, v)
-    out_r, dres, dctx, dconv, g_out, g_in, g_down_t, g_small = stage_c(ctx, conv, xr, cotr, wo, wi, wdn, ln)
+    out_r, dres, dctx, dconv, gf, g_small = stage_c(units, ctx, conv, xr, cotr, wo, wi, wdn, wd_rows)
     dq, dk, dv = stage_d(segt, q, k, v, ctx, lse, dctx)
-    gx, out, g_proj, g_point, g_kernel_t, g_depth_t = stage_e(
-        s, segr, xr, out_r, dres, dconv, dq, dk, dv, q, c, depth, span, mixed, taps, wp, wd_rows, wpt, wk_rows
+    gx, out, gm = stage_e(
+        units, s, segr, xr, out_r, dres, dconv, dq, dk, dv, q, c, depth, span, mixed, taps, wp, wd_rows, wpt, wk_rows,
+        g_small,
     )
-    g_kernel = g_kernel_t.reshape(KERNEL, 8, -1)[:, :HEADS].transpose(2, 1, 0).reshape(-1, HEADS * KERNEL)
-    grads = (
-        g_proj, g_depth_t[:KERNEL].T, g_point, g_kernel, g_out, g_small[0], g_small[1], g_in, g_down_t.T,
-        g_small[2], g_small[3],
+    if own:
+        f, m = scatter_all(n, 1, [gf, gm], 2)
+        sums = finish(n, d, hid, f, m)
+    else:
+        sums = native_sums(gf, gm, d, hid)
+    g_proj, g_depth, g_point, g_kernel, g_out, g_in, g_down, g_vec = sums
+    return (
+        out, gx, g_proj, g_depth, g_point, g_kernel, g_out, g_vec[:, 0], g_vec[:, 1], g_in, g_down,
+        g_vec[:, 2], g_vec[:, 3],
     )
-    return out, gx, grads
-
-
-def shards(tokens, segments, cotangent, *weights):
-    full = tuple(lax.all_gather(w, "tok", axis=0, tiled=True) for w in weights)
-    out, gx, grads = local_step(tokens, segments[:, 0], cotangent, full)
-    owned = tuple(lax.psum_scatter(g, "tok", scatter_dimension=0, tiled=True) for g in grads)
-    return (out, gx) + owned
 
 
 def solution(mesh):
     rows, vec, act = P("tok", None), P("tok"), P(None, "tok", None)
     in_specs = (act, act, act, rows, rows, rows, rows, rows, vec, vec, rows, rows, vec, vec)
     out_specs = (act, act, rows, rows, rows, rows, rows, vec, vec, rows, rows, vec, vec)
-    return jax.shard_map(shards, mesh=mesh, in_specs=in_specs, out_specs=out_specs, check_vma=False)
+    run = partial(shards, mesh.shape["tok"])
+    return jax.shard_map(run, mesh=mesh, in_specs=in_specs, out_specs=out_specs, check_vma=False)

time: 1170 us -> 460 us (0.39)
  waiting for transfers between devices: 619 us -> 0 us
  blocking collectives: 203 us -> 0 us
  Pallas kernels: 302 us -> 438 us
  between operations: 18.4 us -> 4.85 us
    reduce_scatter x3 -> x0, waiting for transfers between devices: 330 us -> none  [shards(): lax.psum_scatter(g, 'tok', scatter_dimension=0, tiled=True)]
    unnamed x13 -> x0, waiting for transfers between devices: 289 us -> none
    pallas_call x0 -> x3, Pallas kernels: none -> 134 us  [the longest x1 67.7 us: scatter_all(): pl.pallas_call(kernel, out_shape=[jax.ShapeDtypeStruct(w.shape[1:], F32)...]
    all_gather x3 -> x0, blocking collectives: 128 us -> none  [shards(): lax.all_gather(w, 'tok', axis=0, tiled=True)]
    unnamed x2 -> x0, blocking collectives: 75 us -> none
    unnamed x28 -> x8, local copies, waits for them, and re-layouts: 16 us -> 3.02 us
  transfers between devices with their start and end apart: 10 -> 0, of which waited for: 6 -> 0; matrix products, arithmetic and copies ran while one was open for 2% -> 0% of each run, Pallas kernels for 6% -> 0%
where the time goes in v2:
time: 460 us; the launch traced here: 454 us
  Pallas kernels  438 us (95%)
  local copies, waits for them, and re-layouts  10.4 us (2%)
  between operations  4.85 us (1%)
    pallas_call x1, Pallas kernels, stage_e(): pl.pallas_call(kernel_e, out_shape=[sds((mb, t, d), F32), sds((mb, t, d),...  97.1 us
    pallas_call x1, Pallas kernels, stage_c(): pl.pallas_call(kernel_c, out_shape=[sds((mb, t, d), BF16), sds((mb, t, d)...  87.8 us
    pallas_call x1, Pallas kernels, scatter_all(): pl.pallas_call(kernel, out_shape=[jax.ShapeDtypeStruct(w.shape[1:], F32)...  67.7 us
    pallas_call x1, Pallas kernels, gather_all(): pl.pallas_call(kernel, out_shape=[jax.ShapeDtypeStruct((n,) + w.shape, w....  64.6 us
    pallas_call x1, Pallas kernels, stage_d(): pl.pallas_call(kernel_d, out_shape=[sds((mb, t, half), F32), sds((mb, t,...  47.7 us
    pallas_call x1, Pallas kernels, stage_a(): pl.pallas_call(kernel_a, out_shape=[sds((mb,) + sh, dt) for sh, dt in out...  36.5 us
    pallas_call x1, Pallas kernels, stage_b(): pl.pallas_call(kernel_b, out_shape=[sds((mb, t, half), BF16), sds((mb, t,...  35.1 us

profile of v2, /device:TPU:0, one launch (start us, length us, event | category | flops | bytes accessed | tf_op | source)
XLA Modules:
  0.0 453.8 jit_solution(3479305884116660438)
XLA Ops:
  0.6 0.8 copy.35
  1.4 0.7 copy.36
  2.2 0.7 copy.37
  2.9 0.7 copy.38
  3.7 0.7 copy.39
  4.4 0.7 copy.45
  5.1 0.2 fusion.s_ref
  5.3 0.0 copy-start.1
  5.4 0.6 fusion.2
  9.8 0.1 constant_dynamic-slice_fusion
  9.9 0.0 copy-start
  10.0 0.6 slice.53.segt_ref
  10.5 0.8 reshape.54
  11.3 0.2 copy.43
  11.5 0.1 copy.40
  11.6 0.7 concatenate.7.refs_2_
  12.3 64.6 %gather.1 = (bf16[32,24,1536]{2,1,0:T(8,128)(2,1)}, bf16[32,24,1536]{2,1,0:T(8,128)(2,1)}, bf16[32,24,256]{2,1,0:T(8,128)(2,1)}, bf16[32,96,384]{2,1,0:T(8,128)(...) custom-call(bf16[24,1536]{1,0:T(8,128)(2,1)} %refs_0_.1, bf16[24,1536]{1,0:T(8,128)(2,1)} %refs_1_.1, ...), custom_call_target="tpu_custom_call" | custom-call | tf_op jit(solution)/shard_map/gather/pallas_call | solution.py:218
  76.9 0.0 copy-done.1
  76.9 0.0 copy-done
  76.9 36.5 %mix_fwd.1 = (bf16[2,1152,768]{2,1,0:T(8,128)(2,1)}, bf16[2,1152,768]{2,1,0:T(8,128)(2,1)}, bf16[2,1152,384]{2,1,0:T(8,128)(2,1)}, bf16[2,1152,384]{2,1,0:T(8,12...) custom-call(s32[2]{0:T(128)} %copy-done.1, ...), custom_call_target="tpu_custom_call" | custom-call | tf_op jit(solution)/shard_map/mix_fwd/pallas_call | solution.py:460
  113.4 35.1 %att_fwd.1 = (bf16[2,1152,384]{2,1,0:T(8,128)(2,1)}, f32[2,1152,384]{2,1,0:T(8,128)}) custom-call(f32[2,1,128]{2,1,0:T(1,128)} %slice.53.segt_ref, bf16[2,1152,384]{2,1,0:T(8,128)(2,1)} %get-tuple-element.60.q_ref, bf16[2,1152,384]{2,1,0:T(8,128)(2,1)} %get-tuple-element.61.k_ref, bf16[2,1152,384]{2,1,0:T(8,128)(2,1)} %get-tuple-element.62.v_ref), custom_call_target="tpu_custom_call" | custom-call | tf_op jit(solution)/shard_map/att_fwd/pallas_call | solution.py:558
  148.5 87.8 %ffn.1 = (bf16[2,1152,768]{2,1,0:T(8,128)(2,1)}, f32[2,1152,768]{2,1,0:T(8,128)}, bf16[2,1152,384]{2,1,0:T(8,128)(2,1)}, f32[2,1152,384]{2,1,0:T(8,128)}, bf16[3...) custom-call(bf16[2,1152,384]{2,1,0:T(8,128)(2,1)} %get-tuple-element.63.ctx_ref, ...), custom_call_target="tpu_custom_call" | custom-call | tf_op jit(solution)/shard_map/ffn/pallas_call | solution.py:695
  236.3 47.7 %att_bwd.1 = (f32[2,1152,384]{2,1,0:T(8,128)}, bf16[2,1152,384]{2,1,0:T(8,128)(2,1)}, bf16[2,1152,384]{2,1,0:T(8,128)(2,1)}) custom-call(f32[2,1,128]{2,1,0:T(1,128)} %slice.53.segt_ref, bf16[2,1152,384]{2,1,0:T(8,128)(2,1)} %get-tuple-element.60.q_ref, bf16[2,1152,384]{2,1,0:T(8,128)(2,1)} %get-tuple-element.61.k_ref, ...), custom_call_target="tpu_custom_call" | custom-call | tf_op jit(solution)/shard_map/att_bwd/pallas_call | solution.py:803
  284.0 97.1 %mix_bwd.1 = (f32[2,1152,768]{2,1,0:T(8,128)}, bf16[2,1152,768]{2,1,0:T(8,128)(2,1)}, bf16[32,144,384]{2,1,0:T(8,128)(2,1)}) custom-call(s32[2]{0:T(128)} %copy-done.1, f32[2,1,1152]{2,1,0:T(1,128)} %copy-done, bf16[2,1152,768]{2,1,0:T(8,128)(2,1)} %get-tuple-element.59.x_ref, bf16[2,1152,768]{2,1,0:T(8,128)(2,1)} %get-tuple-element.70.out_ref_in, ...), custom_call_target="tpu_custom_call" | custom-call | tf_op jit(solution)/shard_map/mix_bwd/pallas_call | solution.py:1002
  381.1 67.7 %scatter.1 = (f32[240,384]{1,0:T(8,128)}, f32[144,384]{1,0:T(8,128)}) custom-call(bf16[32,240,384]{2,1,0:T(8,128)(2,1)} %get-tuple-element.87.refs_0_, bf16[32,144,384]{2,1,0:T(8,128)(2,1)} %get-tuple-element.88.refs_1_), custom_call_target="tpu_custom_call" | custom-call | tf_op jit(solution)/shard_map/scatter/pallas_call | solution.py:262
  448.7 1.9 finish.1
  450.6 1.6 slice_reduce_fusion
  452.2 1.4 copy.41
  (9 shorter events, 0.1 us)
Async XLA Ops:
  5.3 71.6 %copy-start.1 = (s32[2]{0:T(128)}, s32[2]{0:T(128)S(1)}, u32[]{:S(2)}) copy-start(s32[2]{0:T(128)S(1)} %fusion.s_ref) | copy-start | bytes 28
  9.9 67.0 %copy-start = (f32[2,1,1152]{2,1,0:T(1,128)}, f32[2,1,1152]{2,1,0:T(1,128)S(1)}, u32[]{:S(2)}) copy-start(f32[2,1,1152]{2,1,0:T(1,128)S(1)} %broadcast_in_dim.27.seg_ref) | copy-start | bytes 27652

commit v3 on v2

--- a/solution.py
+++ b/solution.py
@@ -77,13 +77,16 @@
 
 
 class Gather:
-    def __init__(self, n, src, dst, order, send, recv, own):
-        self.src, self.dst, self.order = src, dst, order[::-1]
+    def __init__(self, src, dst, cols, order, send, recv, own):
+        self.src, self.all, self.cols, self.order = src.at[:, cols], dst, cols, order[::-1]
         self.send, self.recv, self.own = send, recv, own
         self.me = lax.axis_index("tok")
 
+    def dst(self, at):
+        return self.all.at[at, :, self.cols]
+
     def start(self):
-        pltpu.make_async_copy(self.src, self.dst.at[self.me], self.own).start()
+        pltpu.make_async_copy(self.src, self.dst(self.me), self.own).start()
         self.stage(0)
 
     def stage(self, s):
@@ -92,8 +95,8 @@
         def one(k):
             at = flipped(self.me, self.order[:s], k)
             pltpu.make_async_remote_copy(
-                src_ref=self.dst.at[at] if s else self.src,
-                dst_ref=self.dst.at[at],
+                src_ref=self.dst(at) if s else self.src,
+                dst_ref=self.dst(at),
                 send_sem=self.send.at[s],
                 recv_sem=self.recv.at[s],
                 device_id=(to,),
@@ -103,12 +106,12 @@
         many(1 << s, one)
 
     def wait(self, sem, s):
-        whole = self.dst.at[pl.ds(0, 1 << s)]
+        whole = self.dst(pl.ds(0, 1 << s))
         pltpu.make_async_copy(whole, whole, sem.at[s]).wait()
 
     def step(self, s):
         if s == 1:
-            pltpu.make_async_copy(self.src, self.dst.at[self.me], self.own).wait()
+            pltpu.make_async_copy(self.src, self.dst(self.me), self.own).wait()
         self.wait(self.recv, s - 1)
         self.stage(s)
 
@@ -196,34 +199,52 @@
     return pltpu.CompilerParams(collective_id=cid, has_side_effects=True, vmem_limit_bytes=VMEM_CAP)
 
 
+class Gathers:
+    def __init__(self, n, srcs, dsts, send, recv, own):
+        self.parts = []
+        self.last = n.bit_length() - 1
+        for src, dst in zip(srcs, dsts):
+            wide = src.shape[1]
+            cut = wide // 256 * 128
+            for cols, order in zip((pl.ds(0, cut), pl.ds(cut, wide - cut)), bit_orders(n)):
+                i = len(self.parts)
+                self.parts.append(Gather(src, dst, cols, order, send.at[i], recv.at[i], own.at[i]))
+
+    def step(self, s):
+        for g in self.parts:
+            if s == 0:
+                g.start()
+            elif s < self.last:
+                g.step(s)
+            else:
+                g.finish()
+
+    @staticmethod
+    def sems(n, count):
+        stages = n.bit_length() - 1
+        dma = pltpu.SemaphoreType.DMA
+        return [dma((2 * count, stages)), dma((2 * count, stages)), dma((2 * count,))]
+
+
+def gathered(n, shards):
+    return [jax.ShapeDtypeStruct((n,) + w.shape, w.dtype) for w in shards]
+
+
 def gather_all(n, shards):
     count = len(shards)
-    stages = n.bit_length() - 1
-    orders = bit_orders(n)
 
     def kernel(*refs):
-        srcs, dsts, (send, recv, own) = refs[:count], refs[count : 2 * count], refs[2 * count :]
         greet(n)
-        plans = [
-            Gather(n, srcs[i], dsts[i], orders[i % 2], send.at[i], recv.at[i], own.at[i]) for i in range(count)
-        ]
-        for g in plans:
-            g.start()
-        for s in range(1, stages):
-            for g in plans:
-                g.step(s)
-        for g in plans:
-            g.finish()
+        plan = Gathers(n, refs[:count], refs[count : 2 * count], *refs[2 * count :])
+        for s in range(plan.last + 1):
+            plan.step(s)
 
     return pl.pallas_call(
         kernel,
-        out_shape=[jax.ShapeDtypeStruct((n,) + w.shape, w.dtype) for w in shards],
+        out_shape=gathered(n, shards),
         in_specs=[ANY] * count,
         out_specs=[ANY] * count,
-        scratch_shapes=[
-            pltpu.SemaphoreType.DMA((count, stages)), pltpu.SemaphoreType.DMA((count, stages)),
-            pltpu.SemaphoreType.DMA((count,)),
-        ],
+        scratch_shapes=Gathers.sems(n, count),
         compiler_params=remote(0),
         name="gather",
     )(*shards)
@@ -235,41 +256,59 @@
     return [(a, b - a) for a, b in zip(cuts, cuts[1:]) if b > a]
 
 
-def scatter_all(n, cid, packed, parts):
-    stages = n.bit_length() - 1
-    orders = bit_orders(n)
-    cuts = [(i, a, r) for i, w in enumerate(packed) for a, r in split_rows(w.shape[1], parts)]
-    count = len(packed)
-    total = len(cuts)
-
-    def kernel(*refs):
-        srcs, outs, rest = refs[:count], refs[count : 2 * count], refs[2 * count :]
-        accs, gots, (send, recv, own) = rest[:total], rest[total : 2 * total], rest[2 * total :]
-        greet(n)
-        plans = [
+class Scatters:
+    def __init__(self, n, cuts, srcs, outs, refs):
+        total = len(cuts)
+        accs, gots, (send, recv, own) = refs[:total], refs[total : 2 * total], refs[2 * total :]
+        orders = bit_orders(n)
+        self.last = n.bit_length() - 1
+        self.outs = [outs[i] for i, a, r in cuts]
+        self.parts = [
             Scatter(n, srcs[i], a, accs[j], gots[j], orders[j % 2], send.at[j], recv.at[j], own.at[j])
             for j, (i, a, r) in enumerate(cuts)
         ]
-        for p in plans:
-            p.start()
-        for s in range(1, stages):
-            for p in plans:
+
+    def step(self, s):
+        for p, out in zip(self.parts, self.outs):
+            if s == 0:
+                p.start()
+            elif s < self.last:
                 p.step(s)
-        for p, (i, a, r) in zip(plans, cuts):
-            p.finish(outs[i])
-
-    bufs = [(r, packed[i].shape[2]) for i, a, r in cuts]
+            else:
+                p.finish(out)
+
+    @staticmethod
+    def cuts(packed, parts):
+        return [(i, a, r) for i, w in enumerate(packed) for a, r in split_rows(w.shape[1], parts)]
+
+    @staticmethod
+    def scratch(n, cuts, packed):
+        total, stages = len(cuts), n.bit_length() - 1
+        dma = pltpu.SemaphoreType.DMA
+        bufs = [(r, packed[i].shape[2]) for i, a, r in cuts]
+        return (
+            [pltpu.VMEM((n // 2,) + b, BF16) for b in bufs]
+            + [pltpu.VMEM((n,) + b, BF16) for b in bufs]
+            + [dma((total, stages)), dma((total, stages)), dma((total,))]
+        )
+
+
+def scatter_all(n, cid, packed, parts):
+    cuts = Scatters.cuts(packed, parts)
+    count = len(packed)
+
+    def kernel(*refs):
+        greet(n)
+        plan = Scatters(n, cuts, refs[:count], refs[count : 2 * count], refs[2 * count :])
+        for s in range(plan.last + 1):
+            plan.step(s)
+
     return pl.pallas_call(
         kernel,
         out_shape=[jax.ShapeDtypeStruct(w.shape[1:], F32) for w in packed],
         in_specs=[ANY] * count,
         out_specs=[pl.BlockSpec(memory_space=pltpu.VMEM)] * count,
-        scratch_shapes=[pltpu.VMEM((n // 2,) + b, BF16) for b in bufs]
-        + [pltpu.VMEM((n,) + b, BF16) for b in bufs]
-        + [
-            pltpu.SemaphoreType.DMA((total, stages)), pltpu.SemaphoreType.DMA((total, stages)),
-            pltpu.SemaphoreType.DMA((total,)),
-        ],
+        scratch_shapes=Scatters.scratch(n, cuts, packed),
         compiler_params=remote(cid),
         name="scatter",
     )(*packed)
@@ -343,16 +382,20 @@
     wk_ref[...] = mm(sm_ref[:, 128:256], pick, TN)[0:72, :].astype(BF16)
 
 
-def kernel_a(
-    s_ref, x_ref, cot_ref, seg_ref, wp_ref, sm_ref, wpt_ref,
-    xr_ref, cotr_ref, q_ref, k_ref, v_ref, c_ref, depth_ref, span_ref, mixed_ref, taps_ref, conv_ref, wd_ref, wk_ref,
-    raw, xs, segb, vt, cs, lt, e_ref, texp,
-):
+def kernel_a(n, count, *refs):
+    s_ref, x_ref, cot_ref, seg_ref, wp_ref, sm_ref, wpt_ref = refs[:7]
+    srcs, refs = refs[7 : 7 + count], refs[7 + count :]
+    xr_ref, cotr_ref, q_ref, k_ref, v_ref, c_ref, depth_ref, span_ref, mixed_ref, taps_ref, conv_ref = refs[:11]
+    wd_ref, wk_ref = refs[11:13]
+    dsts, refs = refs[13 : 13 + count], refs[13 + count :]
+    raw, xs, segb, vt, cs, lt, e_ref, texp, *sems = refs
+    plan = Gathers(n, srcs, dsts, *sems) if count else None
     t, d = x_ref.shape[1:]
     half = d // 2
     nch = d // 128
     b = pl.program_id(0)
     s = s_ref[b]
+    point(b == 0, lambda: greet(n), plan, 0)
 
     @pl.when(b == 0)
     def _():
@@ -385,7 +428,9 @@
                 acc = part if acc is None else acc + part
             depth_ref[0, pl.ds(r0, 128), pl.ds(j * 128, 128)] = acc.astype(BF16)
 
+    point(b == 0, None, plan, 1)
     masked_tiles(t, depth_tile)
+    point(b == 0, None, plan, 2)
 
     def proj_tile(i, carry):
         r0 = pl.multiple_of(i * 384, 128)
@@ -408,6 +453,7 @@
 
     lax.fori_loop(0, t // 384, proj_tile, 0)
 
+    point(b == 0, None, plan, 3)
     logits = [lt[o * 8 : o * 8 + 8, :] for o in range(KERNEL)]
     top = logits[0]
     for o in range(1, KERNEL):
@@ -434,7 +480,11 @@
             conv_ref[0, rows, pl.ds(j * 128, 128)] = acc.astype(BF16)
         return carry
 
+    point(b == 1, None, plan, 4)
     lax.fori_loop(0, t // 128, conv_tile, 0)
+    if plan is not None:
+        for i in range(5, plan.last + 1):
+            point(b == pl.num_programs(0) - 1, None, plan, i)
 
 
 def whole(*shape):
@@ -445,11 +495,23 @@
     return pl.BlockSpec((1,) + shape, lambda b, *_: (b,) + (0,) * len(shape))
 
 
-def params(n):
-    return pltpu.CompilerParams(dimension_semantics=("arbitrary",) * n, vmem_limit_bytes=VMEM_CAP)
-
-
-def stage_a(s, x, cot, segr, wp, sm, wpt):
+def params(n, cid=None):
+    more = {} if cid is None else {"collective_id": cid, "has_side_effects": True}
+    return pltpu.CompilerParams(dimension_semantics=("arbitrary",) * n, vmem_limit_bytes=VMEM_CAP, **more)
+
+
+def point(when, first, plan, s):
+    if plan is None:
+        return
+
+    @pl.when(when)
+    def _():
+        if s == 0:
+            first()
+        plan.step(s)
+
+
+def stage_a(n, s, x, cot, segr, wp, sm, wpt, more):
     mb, t, d = x.shape
     half = d // 2
     sds = jax.ShapeDtypeStruct
@@ -458,8 +520,8 @@
         ((t, d), BF16), ((t, half), F32), ((t, half), BF16), ((72, t), F32), ((t, half), BF16),
     ]
     return pl.pallas_call(
-        kernel_a,
-        out_shape=[sds((mb,) + sh, dt) for sh, dt in out] + [sds((24, d), F32), sds((72, half), BF16)],
+        partial(kernel_a, n, len(more)),
+        out_shape=[sds((mb,) + sh, dt) for sh, dt in out] + [sds((24, d), F32), sds((72, half), BF16)] + gathered(n, more),
         grid_spec=pltpu.PrefetchScalarGridSpec(
             num_scalar_prefetch=1,
             grid=(mb,),
@@ -467,8 +529,9 @@
                 per_block(t, d), per_block(t, d),
                 pl.BlockSpec((pl.Squeezed(), 1, t), lambda b, *_: (b, 0, 0)),
                 whole(*wp.shape), whole(*sm.shape), whole(*wpt.shape),
-            ],
-            out_specs=[per_block(*sh) for sh, _ in out] + [whole(24, d), whole(72, half)],
+            ]
+            + [ANY] * len(more),
+            out_specs=[per_block(*sh) for sh, _ in out] + [whole(24, d), whole(72, half)] + [ANY] * len(more),
             scratch_shapes=[
                 pltpu.VMEM((t + 128, 128), F32),
                 pltpu.VMEM((d // 128, t + 16, 128), F32),
@@ -478,11 +541,12 @@
                 pltpu.VMEM((72, t), F32),
                 pltpu.VMEM((144, KERNEL * half), BF16),
                 pltpu.VMEM((128, KERNEL * half), F32),
-            ],
+            ]
+            + (Gathers.sems(n, len(more)) if more else []),
         ),
-        compiler_params=params(1),
+        compiler_params=params(1, 2 if more else None),
         name="mix_fwd",
-    )(s, x, cot, segr, wp, sm, wpt)
+    )(s, x, cot, segr, wp, sm, wpt, *more)
 
 
 QT = 256
@@ -495,7 +559,30 @@
     return jnp.where(hot & inside, 1.0, 0.0), jnp.where(inside & ~hot, -1e30, 0.0)
 
 
-def kernel_b(segt_ref, q_ref, k_ref, v_ref, ctx_ref, lse_ref):
+def steps_done():
+    across = pl.num_programs(1)
+    return pl.program_id(0) * across + pl.program_id(1), pl.num_programs(0) * across - 1
+
+
+def stage_points(n, plan, now, early):
+    if plan is None:
+        return
+    step, last = steps_done()
+    if early:
+        for s, at in enumerate(now):
+            point(step == at, lambda: greet(n), plan, s)
+    else:
+        for s in range(len(now), plan.last + 1):
+            point(step == last, None, plan, s)
+
+
+def kernel_b(n, count, *refs):
+    segt_ref, q_ref, k_ref, v_ref = refs[:4]
+    srcs, (ctx_ref, lse_ref) = refs[4 : 4 + count], refs[4 + count : 6 + count]
+    dsts, sems = refs[6 + count : 6 + 2 * count], refs[6 + 2 * count :]
+    plan = Gathers(n, srcs, dsts, *sems) if count else None
+    times = (0, 1, 2, 3, 5)
+    stage_points(n, plan, times, True)
     t = q_ref.shape[1]
     tail = t - SEG_MOST
     low_half = lanes((1, 128)) < 64
@@ -542,6 +629,7 @@
             )
         )
     finish(rows, [o[0] for o in outs], [o[1] for o in outs])
+    stage_points(n, plan, times, False)
 
 
 def pair(t):
@@ -552,18 +640,19 @@
     return pl.BlockSpec((pl.Squeezed(), 1, tail), lambda b, *_: (b, 0, 0))
 
 
-def stage_b(segt, q, k, v):
+def stage_b(n, segt, q, k, v, more):
     mb, t, half = q.shape
     sds = jax.ShapeDtypeStruct
     return pl.pallas_call(
-        kernel_b,
-        out_shape=[sds((mb, t, half), BF16), sds((mb, t, half), F32)],
+        partial(kernel_b, n, len(more)),
+        out_shape=[sds((mb, t, half), BF16), sds((mb, t, half), F32)] + gathered(n, more),
         grid=(mb, half // 128),
-        in_specs=[seg_tail(t - SEG_MOST), pair(t), pair(t), pair(t)],
-        out_specs=[pair(t), pair(t)],
-        compiler_params=params(2),
+        in_specs=[seg_tail(t - SEG_MOST), pair(t), pair(t), pair(t)] + [ANY] * len(more),
+        out_specs=[pair(t), pair(t)] + [ANY] * len(more),
+        scratch_shapes=Gathers.sems(n, len(more)) if more else [],
+        compiler_params=params(2, 3 if more else None),
         name="att_fwd",
-    )(segt, q, k, v)
+    )(segt, q, k, v, *more)
 
 
 ROWS = 384
@@ -724,7 +813,16 @@
 KT = 256
 
 
-def kernel_d(segt_ref, q_ref, k_ref, v_ref, ctx_ref, lse_ref, do_ref, dq_ref, dk_ref, dv_ref, qa, da, dqt):
+def kernel_d(n, cuts, *refs):
+    count = 1 if cuts else 0
+    segt_ref, q_ref, k_ref, v_ref, ctx_ref, lse_ref, do_ref = refs[:7]
+    srcs, refs = refs[7 : 7 + count], refs[7 + count :]
+    dq_ref, dk_ref, dv_ref = refs[:3]
+    outs, refs = refs[3 : 3 + count], refs[3 + count :]
+    qa, da, dqt, *rest = refs
+    plan = Scatters(n, cuts, srcs, outs, rest) if count else None
+    times = (0, 1, 3, 4, 5)
+    stage_points(n, plan, times, True)
     t = q_ref.shape[1]
     tail = t - SEG_MOST
     lane = lanes((1, 128))
@@ -795,23 +893,27 @@
     for ref, i in ((dk_ref, 0), (dv_ref, 1)):
         ref[0, rows, :] = jnp.where(low_half, halves[0][i], halves[1][i]).astype(BF16)
     dq_ref[0, rows, :] = jnp.where(low_half, halves[0][2], halves[1][2]) * 0.125
-
-
-def stage_d(segt, q, k, v, ctx, lse, dctx):
+    stage_points(n, plan, times, False)
+
+
+def stage_d(n, segt, q, k, v, ctx, lse, dctx, more):
     mb, t, half = q.shape
+    cuts = Scatters.cuts(more, 2)
     sds = jax.ShapeDtypeStruct
     return pl.pallas_call(
-        kernel_d,
-        out_shape=[sds((mb, t, half), F32), sds((mb, t, half), BF16), sds((mb, t, half), BF16)],
+        partial(kernel_d, n, cuts),
+        out_shape=[sds((mb, t, half), F32), sds((mb, t, half), BF16), sds((mb, t, half), BF16)]
+        + [sds(w.shape[1:], F32) for w in more],
         grid=(mb, half // 128),
-        in_specs=[seg_tail(t - SEG_MOST)] + [pair(t)] * 6,
-        out_specs=[pair(t)] * 3,
+        in_specs=[seg_tail(t - SEG_MOST)] + [pair(t)] * 6 + [ANY] * len(more),
+        out_specs=[pair(t)] * 3 + [whole(*w.shape[1:]) for w in more],
         scratch_shapes=[
             pltpu.VMEM((2, t, 128), BF16), pltpu.VMEM((2, t, 128), BF16), pltpu.VMEM((128, SEG_MOST), F32),
-        ],
-        compiler_params=params(2),
+        ]
+        + (Scatters.scratch(n, cuts, more) if more else []),
+        compiler_params=params(2, 4 if more else None),
         name="att_bwd",
-    )(segt, q, k, v, ctx, lse, dctx)
+    )(segt, q, k, v, ctx, lse, dctx, *more)
 
 
 def kernel_e(
@@ -1117,6 +1219,10 @@
     return [lax.psum_scatter(g, "tok", scatter_dimension=0, tiled=True) for g in grads]
 
 
+def rows_of(w):
+    return w.reshape(-1, w.shape[2])
+
+
 def shards(n, tokens, segments, cotangent, w_proj, w_depth, w_point, w_kernel, w_out, g1, b1, w_in, w_down, g2, b2):
     d = tokens.shape[-1]
     hid = w_in.shape[1]
@@ -1124,27 +1230,29 @@
     own = n == units
     if own:
         small = pack_small(w_depth, w_kernel, g1, b1, g2, b2)
-        full = gather_all(n, [w_proj, w_in, small, w_down, w_point, w_out])
-        wp, wi, sm, wdn, wpt, wo = [w.reshape(-1, w.shape[2]) for w in full]
+        wp, sm, wpt = (rows_of(w) for w in gather_all(n, [w_proj, small, w_point]))
+        more_a, more_b = [w_in, w_out], [w_down]
     else:
         given = [w_proj, w_in, w_down, w_point, w_out, w_depth, w_kernel, g1, b1, g2, b2]
         wp, wi, wdn, wpt, wo, *rest = [lax.all_gather(w, "tok", axis=0, tiled=True) for w in given]
         sm = pack_small(*rest)
+        more_a = more_b = []
     s, segr = rolled_segments(segments[:, 0])
     segt = segr[:, :, SEG_MOST:]
-    xr, cotr, q, k, v, c, depth, span, mixed, taps, conv, wd_rows, wk_rows = stage_a(
-        s, tokens, cotangent, segr, wp, sm, wpt
+    xr, cotr, q, k, v, c, depth, span, mixed, taps, conv, wd_rows, wk_rows, *got_a = stage_a(
+        n, s, tokens, cotangent, segr, wp, sm, wpt, more_a
     )
-    ctx, lse = stage_b(segt, q, k, v)
+    ctx, lse, *got_b = stage_b(n, segt, q, k, v, more_b)
+    if own:
+        wi, wo, wdn = (rows_of(w) for w in got_a + got_b)
     out_r, dres, dctx, dconv, gf, g_small = stage_c(units, ctx, conv, xr, cotr, wo, wi, wdn, wd_rows)
-    dq, dk, dv = stage_d(segt, q, k, v, ctx, lse, dctx)
+    dq, dk, dv, *sums = stage_d(n, segt, q, k, v, ctx, lse, dctx, [gf] if own else [])
     gx, out, gm = stage_e(
         units, s, segr, xr, out_r, dres, dconv, dq, dk, dv, q, c, depth, span, mixed, taps, wp, wd_rows, wpt, wk_rows,
         g_small,
     )
     if own:
-        f, m = scatter_all(n, 1, [gf, gm], 2)
-        sums = finish(n, d, hid, f, m)
+        sums = finish(n, d, hid, sums[0], scatter_all(n, 1, [gm], 4)[0])
     else:
         sums = native_sums(gf, gm, d, hid)
     g_proj, g_depth, g_point, g_kernel, g_out, g_in, g_down, g_vec = sums

time: 460 us -> 417 us (0.907)
  Pallas kernels: 438 us -> 394 us
    pallas_call x1, Pallas kernels: 67.7 us -> 30.8 us  [scatter_all(): pl.pallas_call(kernel, out_shape=[jax.ShapeDtypeStruct(w.shape[1:], F32)...]
    pallas_call x4, Pallas kernels: 184 us -> 177 us  [the longest x1 57.3 us: stage_d(): pl.pallas_call(partial(kernel_d, n, cuts), out_shape=[sds((mb, t, half),...]
where the time goes in v3:
time: 417 us; the launch traced here: 410 us
  Pallas kernels  394 us (94%)
  local copies, waits for them, and re-layouts  10.4 us (2%)
  between operations  4.87 us (1%)
    pallas_call x1, Pallas kernels, stage_e(): pl.pallas_call(kernel_e, out_shape=[sds((mb, t, d), F32), sds((mb, t, d),...  97.1 us
    pallas_call x1, Pallas kernels, stage_c(): pl.pallas_call(kernel_c, out_shape=[sds((mb, t, d), BF16), sds((mb, t, d)...  87.9 us
    pallas_call x1, Pallas kernels, stage_d(): pl.pallas_call(partial(kernel_d, n, cuts), out_shape=[sds((mb, t, half),...  57.3 us
    pallas_call x1, Pallas kernels, stage_a(): pl.pallas_call(partial(kernel_a, n, len(more)), out_shape=[sds((mb,) + sh...  48.2 us
    pallas_call x1, Pallas kernels, stage_b(): pl.pallas_call(partial(kernel_b, n, len(more)), out_shape=[sds((mb, t, ha...  39.1 us
    pallas_call x1, Pallas kernels, gather_all(): pl.pallas_call(kernel, out_shape=gathered(n, shards), in_specs=[ANY] * co...  32.1 us
    pallas_call x1, Pallas kernels, scatter_all(): pl.pallas_call(kernel, out_shape=[jax.ShapeDtypeStruct(w.shape[1:], F32)...  30.8 us

profile of v3, /device:TPU:0, one launch (start us, length us, event | category | flops | bytes accessed | tf_op | source)
XLA Modules:
  0.0 409.9 jit_solution(1366024589132651732)
XLA Ops:
  0.6 0.8 copy.35
  1.4 0.7 copy.36
  2.2 0.7 copy.37
  2.9 0.7 copy.38
  3.7 0.7 copy.39
  4.4 0.7 copy.45
  5.1 0.2 fusion.refs_0_.s_ref
  5.3 0.0 copy-start.1
  5.4 0.6 fusion.2
  9.8 0.1 constant_dynamic-slice_fusion
  9.9 0.0 copy-start
  10.0 0.6 slice.53.refs_0_
  10.5 0.8 reshape.54
  11.3 0.2 copy.43
  11.5 0.1 copy.40
  11.6 0.7 concatenate.7.refs_1_
  12.3 32.1 %gather.1 = (bf16[32,24,1536]{2,1,0:T(8,128)(2,1)}, bf16[32,24,256]{2,1,0:T(8,128)(2,1)}, bf16[32,24,384]{2,1,0:T(8,128)(2,1)}) custom-call(bf16[24,1536]{1,0:T(8,128)(2,1)} %refs_0_.1, bf16[24,256]{1,0:T(8,128)(2,1)} %concatenate.7.refs_1_, bf16[24,384]{1,0:T(8,128)(2,1)} %refs_2_.2), custom_call_target="tpu_custom_call" | custom-call | tf_op jit(solution)/shard_map/gather/pallas_call | solution.py:242
  44.4 0.0 copy-done.1
  44.4 0.0 copy-done
  44.4 48.2 %mix_fwd.1 = (bf16[2,1152,768]{2,1,0:T(8,128)(2,1)}, bf16[2,1152,768]{2,1,0:T(8,128)(2,1)}, bf16[2,1152,384]{2,1,0:T(8,128)(2,1)}, bf16[2,1152,384]{2,1,0:T(8,12...) custom-call(s32[2]{0:T(128)} %copy-done.1, ...), custom_call_target="tpu_custom_call" | custom-call | tf_op jit(solution)/shard_map/mix_fwd/pallas_call | solution.py:522
  92.6 39.1 %att_fwd.1 = (bf16[2,1152,384]{2,1,0:T(8,128)(2,1)}, f32[2,1152,384]{2,1,0:T(8,128)}, bf16[32,96,384]{2,1,0:T(8,128)(2,1)}) custom-call(f32[2,1,128]{2,1,0:T(1,128)} %slice.53.refs_0_, bf16[2,1152,384]{2,1,0:T(8,128)(2,1)} %get-tuple-element.59.refs_1_.q_ref, bf16[2,1152,384]{2,1,0:T(8,128)(2,1)} %get-tuple-element.60.refs_2_, ...), custom_call_target="tpu_custom_call" | custom-call | tf_op jit(solution)/shard_map/att_fwd/pallas_call | solution.py:646
  131.8 87.9 %ffn.1 = (bf16[2,1152,768]{2,1,0:T(8,128)(2,1)}, f32[2,1152,768]{2,1,0:T(8,128)}, bf16[2,1152,384]{2,1,0:T(8,128)(2,1)}, f32[2,1152,384]{2,1,0:T(8,128)}, bf16[3...) custom-call(bf16[2,1152,384]{2,1,0:T(8,128)(2,1)} %get-tuple-element.62.ctx_ref.refs_4_, ...), custom_call_target="tpu_custom_call" | custom-call | tf_op jit(solution)/shard_map/ffn/pallas_call | solution.py:784
  219.7 57.3 %att_bwd.1 = (f32[2,1152,384]{2,1,0:T(8,128)}, bf16[2,1152,384]{2,1,0:T(8,128)(2,1)}, bf16[2,1152,384]{2,1,0:T(8,128)(2,1)}, f32[240,384]{1,0:T(8,128)}) custom-call(f32[2,1,128]{2,1,0:T(1,128)} %slice.53.refs_0_, bf16[2,1152,384]{2,1,0:T(8,128)(2,1)} %get-tuple-element.59.refs_1_.q_ref, bf16[2,1152,384]{2,1,0:T(8,128)(2,1)} %get-tuple-element.60.refs_2_, ...), custom_call_target="tpu_custom_call" | custom-call | tf_op jit(solution)/shard_map/att_bwd/pallas_call | solution.py:903
  277.0 97.1 %mix_bwd.1 = (f32[2,1152,768]{2,1,0:T(8,128)}, bf16[2,1152,768]{2,1,0:T(8,128)(2,1)}, bf16[32,144,384]{2,1,0:T(8,128)(2,1)}) custom-call(s32[2]{0:T(128)} %copy-done.1, f32[2,1,1152]{2,1,0:T(1,128)} %copy-done, bf16[2,1152,768]{2,1,0:T(8,128)(2,1)} %get-tuple-element.58.x_ref, bf16[2,1152,768]{2,1,0:T(8,128)(2,1)} %get-tuple-element.69.out_ref_in, ...), custom_call_target="tpu_custom_call" | custom-call | tf_op jit(solution)/shard_map/mix_bwd/pallas_call | solution.py:1104
  374.1 30.8 %scatter.1.m_ref = f32[144,384]{1,0:T(8,128)} custom-call(bf16[32,144,384]{2,1,0:T(8,128)(2,1)} %get-tuple-element.88.refs_0_), custom_call_target="tpu_custom_call" | custom-call | tf_op jit(solution)/shard_map/scatter/pallas_call | solution.py:306
  404.9 1.9 finish.1
  406.7 1.6 slice_reduce_fusion
  408.3 1.4 copy.41
  (9 shorter events, 0.1 us)
Async XLA Ops:
  5.3 39.1 %copy-start.1 = (s32[2]{0:T(128)}, s32[2]{0:T(128)S(1)}, u32[]{:S(2)}) copy-start(s32[2]{0:T(128)S(1)} %fusion.refs_0_.s_ref) | copy-start | bytes 28
  9.9 34.5 %copy-start = (f32[2,1,1152]{2,1,0:T(1,128)}, f32[2,1,1152]{2,1,0:T(1,128)S(1)}, u32[]{:S(2)}) copy-start(f32[2,1,1152]{2,1,0:T(1,128)S(1)} %broadcast_in_dim.27.refs_3_.seg_ref) | copy-start | bytes 27652

commit v4 on v2

--- a/solution.py
+++ b/solution.py
@@ -1,3 +1,4 @@
+import math
 from functools import partial
 
 import jax
@@ -46,11 +47,8 @@
     return me + (1 - 2 * lax.rem(lax.div(me, bit), 2)) * bit
 
 
-def flipped(me, bits, k):
-    at = me
-    for j, bit in enumerate(bits):
-        at = at + (partner(me, bit) - me) * lax.rem(lax.div(k, 1 << j), 2)
-    return at
+def bit_of(me, bit):
+    return lax.rem(lax.div(me, bit), 2)
 
 
 def bit_orders(n):
@@ -68,125 +66,127 @@
     pl.semaphore_wait(barrier, len(bits))
 
 
-def many(count, body):
-    if count <= 4:
-        for k in range(count):
-            body(k)
-    else:
-        lax.fori_loop(0, count, lambda k, c: (body(k), c)[1], 0)
-
-
 class Gather:
-    def __init__(self, n, src, dst, order, send, recv, own):
-        self.src, self.dst, self.order = src, dst, order[::-1]
+    def __init__(self, src, dst, take, part, order, send, recv, own):
+        self.src, self.all, self.part, self.order = src.at[take], dst, part, order[::-1]
         self.send, self.recv, self.own = send, recv, own
         self.me = lax.axis_index("tok")
 
-    def start(self):
-        pltpu.make_async_copy(self.src, self.dst.at[self.me], self.own).start()
-        self.stage(0)
-
-    def stage(self, s):
-        to = partner(self.me, self.order[s])
-
-        def one(k):
-            at = flipped(self.me, self.order[:s], k)
+    def sizes(self):
+        one = math.prod(self.src.shape) * jnp.dtype(self.all.dtype).itemsize
+        return [one << i for i in range(len(self.order))]
+
+    def held(self, s):
+        free = self.order[:s]
+        bits = [1 << b for b in reversed(range(len(self.order)))]
+        return self.all.at[tuple(ALL if bit in free else bit_of(self.me, bit) for bit in bits) + self.part]
+
+    def wait(self, sem, s):
+        ref = self.held(s)
+        pltpu.make_async_copy(ref, ref, sem.at[s]).wait()
+
+    def step(self, s):
+        if s == 0:
+            pltpu.make_async_copy(self.src, self.held(0), self.own).start()
+        elif s == 1:
+            pltpu.make_async_copy(self.src, self.held(0), self.own).wait()
+        if s > 0:
+            self.wait(self.recv, s - 1)
+        if s < len(self.order):
             pltpu.make_async_remote_copy(
-                src_ref=self.dst.at[at] if s else self.src,
-                dst_ref=self.dst.at[at],
+                src_ref=self.held(s) if s else self.src,
+                dst_ref=self.held(s),
                 send_sem=self.send.at[s],
                 recv_sem=self.recv.at[s],
-                device_id=(to,),
+                device_id=(partner(self.me, self.order[s]),),
                 device_id_type=MESH,
             ).start()
-
-        many(1 << s, one)
-
-    def wait(self, sem, s):
-        whole = self.dst.at[pl.ds(0, 1 << s)]
-        pltpu.make_async_copy(whole, whole, sem.at[s]).wait()
-
-    def step(self, s):
-        if s == 1:
-            pltpu.make_async_copy(self.src, self.dst.at[self.me], self.own).wait()
-        self.wait(self.recv, s - 1)
-        self.stage(s)
-
-    def finish(self):
-        last = len(self.order) - 1
-        self.wait(self.recv, last)
-        for s in range(last + 1):
-            self.wait(self.send, s)
+        else:
+            for i in range(s):
+                self.wait(self.send, i)
+
+
+def halves(order, s):
+    left = sorted(set(order) - set(order[:s]), reverse=True)
+    at = left.index(order[s])
+    return 1 << at, 1 << (len(left) - 1 - at)
 
 
 class Scatter:
-    def __init__(self, n, src, first, acc, got, order, send, recv, own):
-        self.n, self.src, self.acc, self.got, self.order = n, src, acc, got, order
-        self.rows = pl.ds(first, acc.shape[1])
+    def __init__(self, n, src, first, out, mine, got, order, send, recv, own):
+        self.n, self.src, self.mine, self.got, self.order, self.out = n, src, mine, got, order, out
+        self.rows = pl.ds(first, mine.shape[1])
         self.send, self.recv, self.own = send, recv, own
         self.me = lax.axis_index("tok")
 
-    def term(self, k):
-        at = flipped(self.me, self.order[::-1], k)
-        return self.src.at[at, self.rows]
-
-    def start(self):
-        half = self.n // 2
-        to = partner(self.me, self.order[0])
-
-        def one(k):
-            pltpu.make_async_remote_copy(
-                src_ref=self.term(half + k),
-                dst_ref=self.got.at[half + k],
-                send_sem=self.send.at[0],
-                recv_sem=self.recv.at[0],
-                device_id=(to,),
-                device_id_type=MESH,
-            ).start()
-
-        def mine(k):
-            pltpu.make_async_copy(self.term(k), self.acc.at[k], self.own).start()
-
-        many(half, one)
-        many(half, mine)
-
-    def held(self, s):
-        return pl.ds(self.n >> (s + 1), self.n >> (s + 1))
-
-    def wait(self, sem, s):
-        ref = self.got.at[self.held(s)]
-        pltpu.make_async_copy(ref, ref, sem.at[s]).wait()
-
-    def add(self, s):
+    def sizes(self):
+        one = math.prod(self.mine.shape[1:]) * 2
+        return [one * (self.n >> (i + 1)) for i in range(len(self.order))]
+
+    def side(self, s, keep):
+        hi, lo = halves(self.order, s)
+        bit = bit_of(self.me, self.order[s])
+        which = bit if keep else 1 - bit
         if s == 0:
-            pltpu.make_async_copy(self.acc, self.acc, self.own).wait()
-        self.wait(self.recv, s)
-        count = self.n >> (s + 1)
-
-        def one(k):
-            total = self.acc[k].astype(F32) + self.got[count + k].astype(F32)
-            self.acc[k] = total.astype(BF16)
-
-        many(count, one)
-
-    def step(self, s):
-        self.add(s - 1)
-        part = self.acc.at[self.held(s)]
-        pltpu.make_async_remote_copy(
-            src_ref=part,
-            dst_ref=self.got.at[self.held(s)],
+            view = self.src.reshape((hi, 2, lo) + self.src.shape[1:])
+            return view.at[:, which, :, self.rows]
+        held = self.got[s - 1]
+        return held.reshape((hi, 2, lo) + held.shape[1:]).at[:, which]
+
+    def there(self, ref, s):
+        hi, lo = halves(self.order, s)
+        return ref.reshape((hi, lo) + ref.shape[1:])
+
+    def send_copy(self, s):
+        return pltpu.make_async_remote_copy(
+            src_ref=self.side(s, False),
+            dst_ref=self.there(self.got[s], s),
             send_sem=self.send.at[s],
             recv_sem=self.recv.at[s],
             device_id=(partner(self.me, self.order[s]),),
             device_id_type=MESH,
-        ).start()
-
-    def finish(self, out):
-        last = len(self.order) - 1
-        self.wait(self.recv, last)
-        out[self.rows, :] = self.acc[0].astype(F32) + self.got[1].astype(F32)
-        for s in range(last + 1):
-            self.wait(self.send, s)
+        )
+
+    def own_copy(self):
+        return pltpu.make_async_copy(self.side(0, True), self.there(self.mine, 0), self.own)
+
+    def add(self, s):
+        self.send_copy(s).wait_recv()
+        got = self.got[s]
+        if s == 0:
+            self.own_copy().wait()
+
+            def first(k, c):
+                got[k] = (got[k].astype(F32) + self.mine[k].astype(F32)).astype(BF16)
+                return c
+
+            lax.fori_loop(0, got.shape[0], first, 0)
+            return
+        hi, lo = halves(self.order, s)
+        held = self.got[s - 1]
+        bit = bit_of(self.me, self.order[s])
+
+        def one(k, c):
+            for i in range(lo):
+                to, at = k * lo + i, (k * 2 + bit) * lo + i
+                got[to] = (got[to].astype(F32) + held[at].astype(F32)).astype(BF16)
+            return c
+
+        if s < len(self.order) - 1:
+            lax.fori_loop(0, hi, one, 0)
+        else:
+            self.out[self.rows, :] = got[0].astype(F32) + held[bit].astype(F32)
+
+    def step(self, s):
+        if s > 0:
+            self.add(s - 1)
+        if s < len(self.order):
+            self.send_copy(s).start()
+        if s == 0:
+            self.own_copy().start()
+        if s == len(self.order):
+            for i in range(s):
+                self.send_copy(i).wait_send()
 
 
 ANY = pl.BlockSpec(memory_space=pl.ANY)
@@ -196,37 +196,75 @@
     return pltpu.CompilerParams(collective_id=cid, has_side_effects=True, vmem_limit_bytes=VMEM_CAP)
 
 
-def gather_all(n, shards):
-    count = len(shards)
-    stages = n.bit_length() - 1
+RATES = {1: 1 / 350e3, 2: 2 / 90e3, 4: 2 / 90e3, 8: 2 / 90e3, 16: 4 / 90e3}
+STAGE = 2.5
+
+
+def schedule(parts, last, spots):
+    link = [{1: 0, 2: 1, 4: 2}.get(bit, 3) for bit in range(1 << last)]
+    free, ready, at = [0.0] * 4, [0.0] * len(parts), [0] * len(parts)
+    plan = []
+    for now in spots:
+        due = []
+        for p, (bits, sizes) in enumerate(parts):
+            if at[p] <= last and ready[p] <= now:
+                due.append((p, at[p]))
+                if at[p] < last:
+                    bit = bits[at[p]]
+                    begin = max(now, free[link[bit]])
+                    free[link[bit]] = begin + sizes[at[p]] * RATES.get(bit, 4 / 90e3)
+                    ready[p] = free[link[bit]] + STAGE
+                at[p] += 1
+        plan.append(due)
+    plan.append([(p, i) for i in range(last + 1) for p in range(len(parts)) if at[p] <= i])
+    return plan
+
+
+class Timed:
+    def __init__(self, n, parts, spots=None):
+        self.parts = parts
+        self.last = n.bit_length() - 1
+        self.ticks = self.last + 1
+        self.plan = [[(p, t) for p in range(len(parts))] for t in range(self.ticks)]
+        if spots is not None:
+            self.plan = schedule([(p.order, p.sizes()) for p in parts], self.last, spots)
+            self.ticks = len(self.plan)
+
+    def tick(self, t):
+        for p, i in self.plan[t]:
+            self.parts[p].step(i)
+
+
+ALL = slice(None)
+
+
+def pieces(wide, count, rows=False):
+    size = wide // count
+    cuts = [pl.ds(i * size, size) for i in range(count)]
+    return [(c, ALL) if rows else (ALL, c) for c in cuts]
+
+
+def gathers(n, srcs, dsts, layout, sems, spots=None):
+    send, recv, own = sems
     orders = bit_orders(n)
-
-    def kernel(*refs):
-        srcs, dsts, (send, recv, own) = refs[:count], refs[count : 2 * count], refs[2 * count :]
-        greet(n)
-        plans = [
-            Gather(n, srcs[i], dsts[i], orders[i % 2], send.at[i], recv.at[i], own.at[i]) for i in range(count)
-        ]
-        for g in plans:
-            g.start()
-        for s in range(1, stages):
-            for g in plans:
-                g.step(s)
-        for g in plans:
-            g.finish()
-
-    return pl.pallas_call(
-        kernel,
-        out_shape=[jax.ShapeDtypeStruct((n,) + w.shape, w.dtype) for w in shards],
-        in_specs=[ANY] * count,
-        out_specs=[ANY] * count,
-        scratch_shapes=[
-            pltpu.SemaphoreType.DMA((count, stages)), pltpu.SemaphoreType.DMA((count, stages)),
-            pltpu.SemaphoreType.DMA((count,)),
+    return Timed(
+        n,
+        [
+            Gather(srcs[a], dsts[a], parts[0], parts[-1], orders[i % 2], send.at[i], recv.at[i], own.at[i])
+            for i, (a, *parts) in enumerate(layout)
         ],
-        compiler_params=remote(0),
-        name="gather",
-    )(*shards)
+        spots,
+    )
+
+
+def gather_sems(n, layout):
+    stages, count = n.bit_length() - 1, len(layout)
+    dma = pltpu.SemaphoreType.DMA
+    return [dma((count, stages)), dma((count, stages)), dma((count,))]
+
+
+def gathered(n, shards):
+    return [jax.ShapeDtypeStruct((2,) * (n.bit_length() - 1) + w.shape, w.dtype) for w in shards]
 
 
 def split_rows(rows, parts):
@@ -235,41 +273,52 @@
     return [(a, b - a) for a, b in zip(cuts, cuts[1:]) if b > a]
 
 
+def scatters(n, cuts, srcs, outs, refs, spots=None):
+    total, stages = len(cuts), n.bit_length() - 1
+    accs, gots, (send, recv, own) = refs[:total], refs[total:-3], refs[-3:]
+    gots = [gots[stages * j : stages * (j + 1)] for j in range(total)]
+    orders = bit_orders(n)
+    return Timed(
+        n,
+        [
+            Scatter(n, srcs[i], a, outs[i], accs[j], gots[j], orders[j % 2], send.at[j], recv.at[j], own.at[j])
+            for j, (i, a, r) in enumerate(cuts)
+        ],
+        spots,
+    )
+
+
+def scatter_cuts(packed, parts):
+    return [(i, a, r) for i, w in enumerate(packed) for a, r in split_rows(w.shape[1], parts)]
+
+
+def scatter_scratch(n, cuts, packed):
+    total, stages = len(cuts), n.bit_length() - 1
+    dma = pltpu.SemaphoreType.DMA
+    bufs = [(r, packed[i].shape[2]) for i, a, r in cuts]
+    return (
+        [pltpu.VMEM((n // 2,) + b, BF16) for b in bufs]
+        + [pltpu.VMEM((n >> (s + 1),) + b, BF16) for b in bufs for s in range(stages)]
+        + [dma((total, stages)), dma((total, stages)), dma((total,))]
+    )
+
+
 def scatter_all(n, cid, packed, parts):
-    stages = n.bit_length() - 1
-    orders = bit_orders(n)
-    cuts = [(i, a, r) for i, w in enumerate(packed) for a, r in split_rows(w.shape[1], parts)]
+    cuts = scatter_cuts(packed, parts)
     count = len(packed)
-    total = len(cuts)
 
     def kernel(*refs):
-        srcs, outs, rest = refs[:count], refs[count : 2 * count], refs[2 * count :]
-        accs, gots, (send, recv, own) = rest[:total], rest[total : 2 * total], rest[2 * total :]
         greet(n)
-        plans = [
-            Scatter(n, srcs[i], a, accs[j], gots[j], orders[j % 2], send.at[j], recv.at[j], own.at[j])
-            for j, (i, a, r) in enumerate(cuts)
-        ]
-        for p in plans:
-            p.start()
-        for s in range(1, stages):
-            for p in plans:
-                p.step(s)
-        for p, (i, a, r) in zip(plans, cuts):
-            p.finish(outs[i])
-
-    bufs = [(r, packed[i].shape[2]) for i, a, r in cuts]
+        plan = scatters(n, cuts, refs[:count], refs[count : 2 * count], refs[2 * count :])
+        for t in range(plan.ticks):
+            plan.tick(t)
+
     return pl.pallas_call(
         kernel,
         out_shape=[jax.ShapeDtypeStruct(w.shape[1:], F32) for w in packed],
         in_specs=[ANY] * count,
         out_specs=[pl.BlockSpec(memory_space=pltpu.VMEM)] * count,
-        scratch_shapes=[pltpu.VMEM((n // 2,) + b, BF16) for b in bufs]
-        + [pltpu.VMEM((n,) + b, BF16) for b in bufs]
-        + [
-            pltpu.SemaphoreType.DMA((total, stages)), pltpu.SemaphoreType.DMA((total, stages)),
-            pltpu.SemaphoreType.DMA((total,)),
-        ],
+        scratch_shapes=scatter_scratch(n, cuts, packed),
         compiler_params=remote(cid),
         name="scatter",
     )(*packed)
@@ -282,12 +331,16 @@
 
 
 def fill_expander(e_ref):
-    shape = e_ref.shape
-    half = shape[1] // KERNEL
-    row = lax.broadcasted_iota(jnp.int32, shape, 0) % 72
-    col = lax.broadcasted_iota(jnp.int32, shape, 1)
-    want = (col // half) * 8 + (col % half) // 64
-    e_ref[...] = jnp.where(row == want, 1.0, 0.0).astype(BF16)
+    half = e_ref.shape[1] // KERNEL
+    shape = (72, 128)
+    row = lax.broadcasted_iota(jnp.int32, shape, 0)
+    upper = jnp.where(lanes(shape) >= 64, 1, 0)
+    for o in range(KERNEL):
+        for j in range(half // 128):
+            one = jnp.where(row == upper + (o * 8 + 2 * j), 1.0, 0.0).astype(BF16)
+            cols = pl.ds(o * half + j * 128, 128)
+            e_ref[0:72, cols] = one
+            e_ref[72:144, cols] = one
 
 
 def mask_rows(segb_ref, r0, rows):
@@ -301,10 +354,13 @@
 def fill_segments(seg_ref, segb_ref, vt_ref):
     t = seg_ref.shape[-1]
     row = seg_ref[...]
-    wide = jnp.broadcast_to(row, (128, t))
-    segb_ref[0:8, :] = jnp.full((8, 128), -1.0, F32)
-    segb_ref[t + 8 : t + 16, :] = jnp.full((8, 128), -1.0, F32)
-    segb_ref[8 : t + 8, :] = wide.T
+    if segb_ref is not None:
+        wide = jnp.broadcast_to(row, (128, t))
+        segb_ref[0:8, :] = jnp.full((8, 128), -1.0, F32)
+        segb_ref[t + 8 : t + 16, :] = jnp.full((8, 128), -1.0, F32)
+        segb_ref[8 : t + 8, :] = wide.T
+    if vt_ref is None:
+        return
     tall = jnp.broadcast_to(row, (8, t))
     pos = lanes((8, t))
     for o in range(KERNEL):
@@ -314,7 +370,7 @@
         vt_ref[o] = jnp.where(inside & (moved == tall), 1.0, 0.0)
 
 
-def masked_tiles(t, body):
+def masked_tiles(t, body, between=None):
     full = SEG_MOST // 128
 
     def inner(i, c):
@@ -322,6 +378,8 @@
         return c
 
     lax.fori_loop(1, full - 1, inner, 0)
+    if between is not None:
+        between()
 
     def edge(i, c):
         idx = jnp.where(i == 0, 0, i + full - 2)
@@ -331,48 +389,132 @@
     lax.fori_loop(0, t // 128 - full + 2, edge, 0)
 
 
+def piece_rows(d):
+    small = PIECE // 2
+    row = lax.broadcasted_iota(jnp.int32, (d, d // 2), 0)
+    col = lanes((1, d // 2))
+    return jnp.where(row == col + col // small * small, 1.0, 0.0).astype(BF16)
+
+
 def unpack_small(sm_ref, wd_ref, wk_ref):
     d = sm_ref.shape[0]
-    for j in range(d // 128):
-        rows = pl.ds(j * 128, 128)
-        wd_ref[:, rows] = sm_ref[rows, 0:128].astype(F32).T[0:24, :]
-    row = lax.broadcasted_iota(jnp.int32, (d, d // 2), 0)
-    col = lax.broadcasted_iota(jnp.int32, (d, d // 2), 1)
-    piece = row % PIECE
-    pick = jnp.where((piece < PIECE // 2) & (row // PIECE * (PIECE // 2) + piece == col), 1.0, 0.0).astype(BF16)
-    wk_ref[...] = mm(sm_ref[:, 128:256], pick, TN)[0:72, :].astype(BF16)
-
-
-def kernel_a(
-    s_ref, x_ref, cot_ref, seg_ref, wp_ref, sm_ref, wpt_ref,
-    xr_ref, cotr_ref, q_ref, k_ref, v_ref, c_ref, depth_ref, span_ref, mixed_ref, taps_ref, conv_ref, wd_ref, wk_ref,
-    raw, xs, segb, vt, cs, lt, e_ref, texp,
-):
+    parts = [sm_ref[j * 128 : (j + 1) * 128, :].T for j in range(d // 128)]
+    tall = jnp.concatenate(parts, 1)
+    wd_ref[...] = tall[0:24, :]
+    wk_ref[...] = mm(tall[32:104, :].astype(BF16), piece_rows(d), NN).astype(BF16)
+
+
+def front_layout(d, half):
+    cols = pieces(2 * d, 4)
+    rest = [(1, (ALL, pl.ds(0, 128))), (1, (ALL, pl.ds(128, half - 128)))]
+    return [(0, cols[0]), (0, cols[1]), (2, (ALL, ALL)), (0, cols[2]), (0, cols[3])] + rest
+
+
+def kernel_front(n, layout, *refs):
+    s_ref, x_ref, cot_ref = refs[:3]
+    if layout:
+        sm_src, wp_src, wpt_src = refs[3:6]
+        xr_ref, cotr_ref, wd_ref, wk_ref, wp_far, wpt_far = refs[6:12]
+        raw, sm, *sems = refs[12:]
+        plan = gathers(n, (wp_src, wpt_src, sm_src), (wp_far, wpt_far, sm), layout, sems)
+    else:
+        sm_src = refs[3]
+        xr_ref, cotr_ref, wd_ref, wk_ref = refs[4:8]
+        raw, sm = refs[8:]
+        plan = None
     t, d = x_ref.shape[1:]
-    half = d // 2
     nch = d // 128
     b = pl.program_id(0)
     s = s_ref[b]
-
-    @pl.when(b == 0)
-    def _():
-        fill_expander(e_ref)
-        unpack_small(sm_ref, wd_ref, wk_ref)
-        xs[:, 0:8, :] = jnp.zeros((nch, 8, 128), F32)
-        xs[:, t + 8 : t + 16, :] = jnp.zeros((nch, 8, 128), F32)
-        cs[:, 0:8, :] = jnp.zeros((nch // 2, 8, 128), F32)
-        cs[:, t + 8 : t + 16, :] = jnp.zeros((nch // 2, 8, 128), F32)
-
-    fill_segments(seg_ref, segb, vt)
+    end = pl.num_programs(0) - 1
+    point(b == 0, lambda: greet(n), plan, 0)
     for src, dst in ((cot_ref, cotr_ref), (x_ref, xr_ref)):
         for j in range(nch):
             col = pl.ds(j * 128, 128)
             raw[0:t, :] = src[0, :, col].astype(F32)
             raw[t : t + 128, :] = src[0, 0:128, col].astype(F32)
-            moved = raw[pl.ds(s, t), :]
-            if dst is xr_ref:
-                xs[j, 8 : t + 8, :] = moved
-            dst[0, :, col] = moved.astype(BF16)
+            dst[0, :, col] = raw[pl.ds(s, t), :].astype(BF16)
+
+    point(b == 0, None, plan, 1)
+
+    @pl.when(b == end)
+    def _():
+        if plan is not None:
+            for i in range(2, plan.ticks):
+                plan.tick(i)
+            unpack_small(sm.reshape(d, 128), wd_ref, wk_ref)
+        else:
+            unpack_small(sm_src, wd_ref, wk_ref)
+
+
+def stage_front(n, s, x, cot, small, wp, wpt, own):
+    mb, t, d = x.shape
+    half = d // 2
+    sds = jax.ShapeDtypeStruct
+    layout = front_layout(d, half) if own else []
+    more = [wp, wpt] if own else []
+    out = [((mb, t, d), BF16)] * 2
+    return pl.pallas_call(
+        partial(kernel_front, n, layout),
+        out_shape=[sds(*o) for o in out] + [sds((24, d), F32), sds((72, half), BF16)] + gathered(n, more),
+        grid_spec=pltpu.PrefetchScalarGridSpec(
+            num_scalar_prefetch=1,
+            grid=(mb,),
+            in_specs=[per_block(t, d), per_block(t, d), ANY if own else whole(*small.shape)] + [ANY] * len(more),
+            out_specs=[per_block(t, d)] * 2 + [whole(24, d), whole(72, half)] + [ANY] * len(more),
+            scratch_shapes=[
+                pltpu.VMEM((t + 128, 128), F32),
+                pltpu.VMEM((2,) * (n.bit_length() - 1) + (PIECE, 128) if own else (8, 128), F32),
+            ]
+            + (gather_sems(n, layout) if own else []),
+        ),
+        compiler_params=params(1, 0 if own else None),
+        name="front",
+    )(s, x, cot, small, *more)
+
+
+A_SPOTS = [block + at for block in (0.0, 16.5) for at in (0.0, 3.0, 6.0, 7.4, 8.6, 11.0, 12.3, 13.6)]
+
+
+def kernel_a(n, layout, count, *refs):
+    seg_ref, xr_ref, wp_ref, wd_ref, wpt_ref, wk_ref = refs[:6]
+    srcs, refs = refs[6 : 6 + count], refs[6 + count :]
+    q_ref, k_ref, v_ref, c_ref, depth_ref, span_ref, mixed_ref, taps_ref, conv_ref = refs[:9]
+    dsts, refs = refs[9 : 9 + count], refs[9 + count :]
+    xs, segb, vt, cs, lt, e_ref, texp, *sems = refs
+    plan = gathers(n, srcs, dsts, layout, sems, A_SPOTS) if count else None
+    t, d = xr_ref.shape[1:]
+    half = d // 2
+    nch = d // 128
+    b = pl.program_id(0)
+    end = pl.num_programs(0) - 1
+    if plan is not None:
+        @pl.when(b == 0)
+        def _():
+            greet(n)
+
+    def spot(i, loop, every):
+        for at in range(3):
+            for block in range(2):
+                point((b == block) & (i == at * every), None, plan, 8 * block + 2 + 3 * loop + at)
+
+    def early(at):
+        for block in range(2):
+            point(b == block, None, plan, 8 * block + at)
+
+    early(0)
+
+    @pl.when(b == 0)
+    def _():
+        fill_expander(e_ref)
+        cs[:, 0:8, :] = jnp.zeros((nch // 2, 8, 128), F32)
+        cs[:, t + 8 : t + 16, :] = jnp.zeros((nch // 2, 8, 128), F32)
+        xs[:, 0:8, :] = jnp.zeros((nch, 8, 128), F32)
+        xs[:, t + 8 : t + 16, :] = jnp.zeros((nch, 8, 128), F32)
+
+    fill_segments(seg_ref, segb, vt)
+    for j in range(nch):
+        xs[j, 8 : t + 8, :] = xr_ref[0, :, pl.ds(j * 128, 128)].astype(F32)
 
     def depth_tile(r0, masked):
         masks = mask_rows(segb, r0, 128) if masked else None
@@ -385,9 +527,10 @@
                 acc = part if acc is None else acc + part
             depth_ref[0, pl.ds(r0, 128), pl.ds(j * 128, 128)] = acc.astype(BF16)
 
-    masked_tiles(t, depth_tile)
+    masked_tiles(t, depth_tile, lambda: early(1))
 
     def proj_tile(i, carry):
+        spot(i, 0, 1)
         r0 = pl.multiple_of(i * 384, 128)
         rows = pl.ds(r0, 384)
         merged = mm(xr_ref[0, rows, :], wp_ref[...]).astype(BF16)
@@ -423,6 +566,7 @@
         lt[o * 8 : o * 8 + 8, :] = tap * vt[o]
 
     def conv_tile(i, carry):
+        spot(i, 1, 3)
         r0 = pl.multiple_of(i * 128, 128)
         rows = pl.ds(r0, 128)
         texp[...] = expand_taps(lt[:, rows], e_ref)
@@ -435,6 +579,7 @@
         return carry
 
     lax.fori_loop(0, t // 128, conv_tile, 0)
+    point(b == end, None, plan, len(A_SPOTS))
 
 
 def whole(*shape):
@@ -445,44 +590,59 @@
     return pl.BlockSpec((1,) + shape, lambda b, *_: (b,) + (0,) * len(shape))
 
 
-def params(n):
-    return pltpu.CompilerParams(dimension_semantics=("arbitrary",) * n, vmem_limit_bytes=VMEM_CAP)
-
-
-def stage_a(s, x, cot, segr, wp, sm, wpt):
-    mb, t, d = x.shape
+def params(n, cid=None):
+    more = {} if cid is None else {"collective_id": cid, "has_side_effects": True}
+    return pltpu.CompilerParams(dimension_semantics=("arbitrary",) * n, vmem_limit_bytes=VMEM_CAP, **more)
+
+
+def point(when, first, plan, s):
+    if plan is None or not plan.plan[s]:
+        return
+
+    @pl.when(when)
+    def _():
+        if first is not None:
+            first()
+        plan.tick(s)
+
+
+def stage_a(n, segr, xr, wp, wd, wpt, wk, more):
+    mb, t, d = xr.shape
     half = d // 2
     sds = jax.ShapeDtypeStruct
     out = [
-        ((t, d), BF16), ((t, d), BF16), ((t, half), BF16), ((t, half), BF16), ((t, half), BF16), ((t, half), BF16),
-        ((t, d), BF16), ((t, half), F32), ((t, half), BF16), ((72, t), F32), ((t, half), BF16),
+        ((t, half), BF16), ((t, half), BF16), ((t, half), BF16), ((t, half), BF16), ((t, d), BF16),
+        ((t, half), F32), ((t, half), BF16), ((72, t), F32), ((t, half), BF16),
     ]
+    layout, far = [], []
+    if more:
+        hid = more[1].shape[1] // 2
+        layout = [(0, p) for p in pieces(d, 2)] + [(1, p) for p in pieces(hid, 2)]
+        layout = [layout[i] for i in (2, 3, 0, 1)]
+        far = [more[0], jax.ShapeDtypeStruct((more[1].shape[0], hid), BF16)]
     return pl.pallas_call(
-        kernel_a,
-        out_shape=[sds((mb,) + sh, dt) for sh, dt in out] + [sds((24, d), F32), sds((72, half), BF16)],
-        grid_spec=pltpu.PrefetchScalarGridSpec(
-            num_scalar_prefetch=1,
-            grid=(mb,),
-            in_specs=[
-                per_block(t, d), per_block(t, d),
-                pl.BlockSpec((pl.Squeezed(), 1, t), lambda b, *_: (b, 0, 0)),
-                whole(*wp.shape), whole(*sm.shape), whole(*wpt.shape),
-            ],
-            out_specs=[per_block(*sh) for sh, _ in out] + [whole(24, d), whole(72, half)],
-            scratch_shapes=[
-                pltpu.VMEM((t + 128, 128), F32),
-                pltpu.VMEM((d // 128, t + 16, 128), F32),
-                pltpu.VMEM((t + 16, 128), F32),
-                pltpu.VMEM((KERNEL, 8, t), F32),
-                pltpu.VMEM((half // 128, t + 16, 128), F32),
-                pltpu.VMEM((72, t), F32),
-                pltpu.VMEM((144, KERNEL * half), BF16),
-                pltpu.VMEM((128, KERNEL * half), F32),
-            ],
-        ),
-        compiler_params=params(1),
+        partial(kernel_a, n, layout, len(more)),
+        out_shape=[sds((mb,) + sh, dt) for sh, dt in out] + gathered(n, far),
+        grid=(mb,),
+        in_specs=[
+            pl.BlockSpec((pl.Squeezed(), 1, t), lambda b: (b, 0, 0)),
+            per_block(t, d), whole(*wp.shape), whole(*wd.shape), whole(*wpt.shape), whole(*wk.shape),
+        ]
+        + [ANY] * len(more),
+        out_specs=[per_block(*sh) for sh, _ in out] + [ANY] * len(more),
+        scratch_shapes=[
+            pltpu.VMEM((d // 128, t + 16, 128), F32),
+            pltpu.VMEM((t + 16, 128), F32),
+            pltpu.VMEM((KERNEL, 8, t), F32),
+            pltpu.VMEM((half // 128, t + 16, 128), F32),
+            pltpu.VMEM((72, t), F32),
+            pltpu.VMEM((144, KERNEL * half), BF16),
+            pltpu.VMEM((128, KERNEL * half), F32),
+        ]
+        + (gather_sems(n, layout) if more else []),
+        compiler_params=params(1, 2 if more else None),
         name="mix_fwd",
-    )(s, x, cot, segr, wp, sm, wpt)
+    )(segr, xr, wp, wd, wpt, wk, *more)
 
 
 QT = 256
@@ -495,7 +655,29 @@
     return jnp.where(hot & inside, 1.0, 0.0), jnp.where(inside & ~hot, -1e30, 0.0)
 
 
-def kernel_b(segt_ref, q_ref, k_ref, v_ref, ctx_ref, lse_ref):
+def tile_points(n, plan, spots, i, tiles):
+    if plan is None:
+        return
+    step = pl.program_id(0) * pl.num_programs(1) + pl.program_id(1)
+    for t in range(len(spots)):
+        point((step == t // tiles) & (i == t % tiles), (lambda: greet(n)) if t == 0 else None, plan, t)
+
+
+def end_points(plan):
+    if plan is None:
+        return
+    last = (pl.program_id(0) == pl.num_programs(0) - 1) & (pl.program_id(1) == pl.num_programs(1) - 1)
+    point(last, None, plan, plan.ticks - 1)
+
+
+B_SPOTS = [1.46 * i for i in range(24)]
+
+
+def kernel_b(n, layout, count, *refs):
+    segt_ref, q_ref, k_ref, v_ref = refs[:4]
+    srcs, (ctx_ref, lse_ref) = refs[4 : 4 + count], refs[4 + count : 6 + count]
+    dsts, sems = refs[6 + count : 6 + 2 * count], refs[6 + 2 * count :]
+    plan = gathers(n, srcs, dsts, layout, sems, B_SPOTS) if count else None
     t = q_ref.shape[1]
     tail = t - SEG_MOST
     low_half = lanes((1, 128)) < 64
@@ -517,6 +699,7 @@
     vs = (jnp.where(low_half, v, one_b), jnp.where(low_half, one_b, v))
 
     def tile(i, carry):
+        tile_points(n, plan, B_SPOTS, i, SEG_MOST // QT)
         rows = pl.ds(pl.multiple_of(i * QT, QT), QT)
         q = q_ref[0, rows, :] * 0.125
         zero = jnp.zeros((), BF16)
@@ -542,6 +725,7 @@
             )
         )
     finish(rows, [o[0] for o in outs], [o[1] for o in outs])
+    end_points(plan)
 
 
 def pair(t):
@@ -549,21 +733,30 @@
 
 
 def seg_tail(tail):
-    return pl.BlockSpec((pl.Squeezed(), 1, tail), lambda b, *_: (b, 0, 0))
-
-
-def stage_b(segt, q, k, v):
+    return pl.BlockSpec((pl.Squeezed(), 1, tail), lambda b, *_: (b, 0, SEG_MOST // tail))
+
+
+def stage_b(n, segt, q, k, v, more):
     mb, t, half = q.shape
     sds = jax.ShapeDtypeStruct
+    layout, far = [], []
+    if more:
+        hid = more[0].shape[1] // 2
+        cols = pieces(hid, 2)
+        wide = [(0, (ALL, pl.ds(hid + i * (hid // 2), hid // 2)), p) for i, p in enumerate(cols)]
+        tall = [(1, p) for p in pieces(more[1].shape[0], 4, True)]
+        layout = tall[:2] + wide + tall[2:]
+        far = [jax.ShapeDtypeStruct((more[0].shape[0], hid), BF16), more[1]]
     return pl.pallas_call(
-        kernel_b,
-        out_shape=[sds((mb, t, half), BF16), sds((mb, t, half), F32)],
+        partial(kernel_b, n, layout, len(more)),
+        out_shape=[sds((mb, t, half), BF16), sds((mb, t, half), F32)] + gathered(n, far),
         grid=(mb, half // 128),
-        in_specs=[seg_tail(t - SEG_MOST), pair(t), pair(t), pair(t)],
-        out_specs=[pair(t), pair(t)],
-        compiler_params=params(2),
+        in_specs=[seg_tail(t - SEG_MOST), pair(t), pair(t), pair(t)] + [ANY] * len(more),
+        out_specs=[pair(t), pair(t)] + [ANY] * len(more),
+        scratch_shapes=gather_sems(n, layout) if more else [],
+        compiler_params=params(2, 3 if more else None),
         name="att_fwd",
-    )(segt, q, k, v)
+    )(segt, q, k, v, *more)
 
 
 ROWS = 384
@@ -582,13 +775,9 @@
 
 
 def gelu_both(x):
-    z = jnp.abs(x) * 0.7071067811865476
-    r = 1.0 / (1.0 + 0.3275911 * z)
-    e = jnp.exp(-0.5 * (x * x))
-    poly = r * (0.254829592 + r * (-0.284496736 + r * (1.421413741 + r * (-1.453152027 + r * 1.061405429))))
-    tail = 0.5 * (poly * e)
-    cdf = jnp.where(x < 0, tail, 1.0 - tail)
-    return x * cdf, cdf + x * (e * 0.3989422804014327)
+    cdf = 0.5 + 0.5 * lax.erf(x * 0.7071067811865476)
+    bell = jnp.exp(x * (x * -0.5))
+    return x * cdf, cdf + x * (bell * 0.3989422804014327)
 
 
 def col_sum(v):
@@ -596,9 +785,9 @@
 
 
 def kernel_c(
-    ctx_ref, conv_ref, x_ref, cot_ref, wo_ref, wi_ref, wdn_ref, ln_ref,
+    ctx_ref, conv_ref, x_ref, cot_ref, wo_ref, wia_ref, wib_ref, wdn_ref, ln_ref,
     out_ref, dres_ref, dctx_ref, dconv_ref, gf_ref, gs_ref,
-    joined, act, slope, dinner, go_ref, gi_ref, gd_ref,
+    joined, act, slope, dinner, go_ref, gi_ref, gd_ref, wi_ref,
 ):
     first = (pl.program_id(0) == 0) & (pl.program_id(1) == 0)
     last = (pl.program_id(0) == pl.num_programs(0) - 1) & (pl.program_id(1) == pl.num_programs(1) - 1)
@@ -608,6 +797,8 @@
 
     @pl.when(first)
     def _():
+        wi_ref[:, 0 : hid // 2] = wia_ref[...]
+        wi_ref[:, hid // 2 :] = wib_ref[...]
         go_ref[...] = jnp.zeros_like(go_ref)
         gi_ref[...] = jnp.zeros_like(gi_ref)
         gd_ref[...] = jnp.zeros_like(gd_ref)
@@ -682,10 +873,10 @@
         lax.fori_loop(0, n // step, emit_down, 0)
 
 
-def stage_c(n, ctx, conv, x, cot, wo, wi, wdn, ln):
+def stage_c(n, ctx, conv, x, cot, wo, wi_a, wi_b, wdn, ln):
     mb, t, d = x.shape
     half = d // 2
-    hid = wi.shape[1]
+    hid = 2 * wi_a.shape[1]
     packed = (d * d + d * hid + 2 * hid * half) // (n * half)
     sds = jax.ShapeDtypeStruct
 
@@ -701,7 +892,7 @@
         grid=(mb, t // ROWS),
         in_specs=[
             tile(half), tile(half), tile(d), tile(d),
-            whole(*wo.shape), whole(*wi.shape), whole(*wdn.shape), whole(*ln.shape),
+            whole(*wo.shape), whole(*wi_a.shape), whole(*wi_b.shape), whole(*wdn.shape), whole(*ln.shape),
         ],
         out_specs=[
             tile(d), tile(d), tile(half), tile(half),
@@ -715,16 +906,25 @@
             pltpu.VMEM((d, d), F32),
             pltpu.VMEM((d, hid), F32),
             pltpu.VMEM((half, 2 * hid), F32),
+            pltpu.VMEM((d, hid), BF16),
         ],
         compiler_params=params(2),
         name="ffn",
-    )(ctx, conv, x, cot, wo, wi, wdn, ln)
+    )(ctx, conv, x, cot, wo, wi_a, wi_b, wdn, ln)
 
 
 KT = 256
-
-
-def kernel_d(segt_ref, q_ref, k_ref, v_ref, ctx_ref, lse_ref, do_ref, dq_ref, dk_ref, dv_ref, qa, da, dqt):
+D_SPOTS = [1.98 * i for i in range(24)]
+
+
+def kernel_d(n, cuts, *refs):
+    count = 1 if cuts else 0
+    segt_ref, q_ref, k_ref, v_ref, ctx_ref, lse_ref, do_ref = refs[:7]
+    srcs, refs = refs[7 : 7 + count], refs[7 + count :]
+    dq_ref, dk_ref, dv_ref = refs[:3]
+    outs, refs = refs[3 : 3 + count], refs[3 + count :]
+    qa, da, dqt, *rest = refs
+    plan = scatters(n, cuts, srcs, outs, rest, D_SPOTS) if count else None
     t = q_ref.shape[1]
     tail = t - SEG_MOST
     lane = lanes((1, 128))
@@ -770,6 +970,7 @@
     main = pl.ds(0, SEG_MOST)
 
     def tile(i, carry):
+        tile_points(n, plan, D_SPOTS, i, SEG_MOST // KT)
         rows = pl.ds(pl.multiple_of(i * KT, KT), KT)
         halves = []
         for h in range(2):
@@ -795,32 +996,67 @@
     for ref, i in ((dk_ref, 0), (dv_ref, 1)):
         ref[0, rows, :] = jnp.where(low_half, halves[0][i], halves[1][i]).astype(BF16)
     dq_ref[0, rows, :] = jnp.where(low_half, halves[0][2], halves[1][2]) * 0.125
-
-
-def stage_d(segt, q, k, v, ctx, lse, dctx):
+    end_points(plan)
+
+
+def stage_d(n, segt, q, k, v, ctx, lse, dctx, more):
     mb, t, half = q.shape
+    cuts = scatter_cuts(more, 4)
     sds = jax.ShapeDtypeStruct
     return pl.pallas_call(
-        kernel_d,
-        out_shape=[sds((mb, t, half), F32), sds((mb, t, half), BF16), sds((mb, t, half), BF16)],
+        partial(kernel_d, n, cuts),
+        out_shape=[sds((mb, t, half), F32), sds((mb, t, half), BF16), sds((mb, t, half), BF16)]
+        + [sds(w.shape[1:], F32) for w in more],
         grid=(mb, half // 128),
-        in_specs=[seg_tail(t - SEG_MOST)] + [pair(t)] * 6,
-        out_specs=[pair(t)] * 3,
+        in_specs=[seg_tail(t - SEG_MOST)] + [pair(t)] * 6 + [ANY] * len(more),
+        out_specs=[pair(t)] * 3 + [whole(*w.shape[1:]) for w in more],
         scratch_shapes=[
             pltpu.VMEM((2, t, 128), BF16), pltpu.VMEM((2, t, 128), BF16), pltpu.VMEM((128, SEG_MOST), F32),
-        ],
-        compiler_params=params(2),
+        ]
+        + (scatter_scratch(n, cuts, more) if more else []),
+        compiler_params=params(2, 4 if more else None),
         name="att_bwd",
-    )(segt, q, k, v, ctx, lse, dctx)
+    )(segt, q, k, v, ctx, lse, dctx, *more)
 
 
 def kernel_e(
-    s_ref, seg_ref, x_ref, out_ref_in, dres_ref, dconv_ref, dq_ref, dk_ref, dv_ref,
-    q_ref, c_ref, depth_ref, span_ref, mixed_ref, taps_ref, wp_ref, wd_ref, wpt_ref, wk_ref, gs_ref,
-    gx_ref, out_ref, gm_ref,
+    s_ref, seg_ref, c_far, dconv_far, taps_far, mixed_far, q_far, dq_far, span_far, dk_far, dv_far, depth_far,
+    x_far, dres_far, outr_far, wp_ref, wd_ref, wpt_ref, wk_ref, gs_ref,
+    gx_far, out_far, gm_ref,
     pad, xs, segb, vt, dcs, dts, e_ref, er_ref, texp, dlt, rt, dm, dl, gacc, gp_ref, gpt_ref, gk_ref, small,
+    c_ref, dconv_ref, taps_ref, mixed_ref, q_ref, dq_ref, span_ref, dk_ref, dv_ref, depth_ref,
+    x_ref, dres_ref, out_ref_in, gx_ref, out_ref, in_sem, out_sem,
 ):
     t, d = x_ref.shape[1:]
+    far = (
+        c_far, dconv_far, taps_far, mixed_far, q_far, dq_far, span_far, dk_far, dv_far, depth_far,
+        x_far, dres_far, outr_far,
+    )
+    near = (
+        c_ref, dconv_ref, taps_ref, mixed_ref, q_ref, dq_ref, span_ref, dk_ref, dv_ref, depth_ref,
+        x_ref, dres_ref, out_ref_in,
+    )
+
+    def fetch(i, block):
+        return pltpu.make_async_copy(far[i].at[pl.ds(block, 1)], near[i], in_sem.at[i])
+
+    def arrived(*which):
+        for i in which:
+            fetch(i, b).wait()
+
+    def done_with(*which):
+        @pl.when(b + 1 < pl.num_programs(0))
+        def _():
+            for i in which:
+                fetch(i, b + 1).start()
+
+    def put_back(j, block):
+        cols = pl.ds(j * 128, 128)
+        return [
+            pltpu.make_async_copy(src.at[:, :, cols], dst.at[pl.ds(block, 1), :, cols], out_sem.at[k, j])
+            for k, (src, dst) in enumerate(((gx_ref, gx_far), (out_ref, out_far)))
+        ]
+
     half = d // 2
     nch = d // 128
     b = pl.program_id(0)
@@ -828,11 +1064,15 @@
 
     @pl.when(b == 0)
     def _():
+        for i in range(len(far)):
+            fetch(i, 0).start()
         fill_expander(e_ref)
-        row = lax.broadcasted_iota(jnp.int32, er_ref.shape, 0)
-        col = lax.broadcasted_iota(jnp.int32, er_ref.shape, 1)
-        head = ((row % 768) % half) // 64
-        er_ref[...] = jnp.where(col == (row // 768) * 8 + head, 1.0, 0.0).astype(BF16)
+        col = lanes((128, 128))
+        upper = jnp.where(lax.broadcasted_iota(jnp.int32, (128, 128), 0) >= 64, 1, 0)
+        for o in range(KERNEL):
+            for j in range(half // 128):
+                one = jnp.where(col == upper + (o * 8 + 2 * j), 1.0, 0.0).astype(BF16)
+                er_ref[pl.ds(o * half + j * 128, 128), :] = one
         for ref in (xs, dts, dcs):
             n = ref.shape[0]
             ref[:, 0:8, :] = jnp.zeros((n, 8, 128), F32)
@@ -843,30 +1083,31 @@
         gacc[...] = jnp.zeros_like(gacc)
 
     fill_segments(seg_ref, segb, vt)
+    arrived(0, 1)
     cw = xs
     for j in range(nch // 2):
         cols = pl.ds(j * 128, 128)
         cw[j, 8 : t + 8, :] = c_ref[0, :, cols].astype(F32)
         dcs[j, 8 : t + 8, :] = dconv_ref[0, :, cols]
+    done_with(0, 1)
 
     def dtap_tile(i, carry):
         r0 = pl.multiple_of(i * 128, 128)
         rows = pl.ds(r0, 128)
         acc = None
         for o in range(KERNEL):
-            his, los = [], []
-            for j in range(nch // 2):
-                prod = cw[j, pl.ds(8 + r0 + o - REACH, 128), :] * dcs[j, pl.ds(8 + r0, 128), :]
-                hi, lo = split2(prod)
-                his.append(hi)
-                los.append(lo)
-            part = mm(jnp.concatenate(his + los, 1), er_ref[o * 768 : (o + 1) * 768, :])
+            prods = [
+                (cw[j, pl.ds(8 + r0 + o - REACH, 128), :] * dcs[j, pl.ds(8 + r0, 128), :]).astype(BF16)
+                for j in range(nch // 2)
+            ]
+            part = mm(jnp.concatenate(prods, 1), er_ref[o * half : (o + 1) * half, :])
             acc = part if acc is None else acc + part
         dlt[:, rows] = acc.T[0:72, :]
         return carry
 
     lax.fori_loop(0, t // 128, dtap_tile, 0)
 
+    arrived(2)
     taps = [taps_ref[0, o * 8 : o * 8 + 8, :] for o in range(KERNEL)]
     dtaps = [dlt[o * 8 : o * 8 + 8, :] * vt[o] for o in range(KERNEL)]
     mean = taps[0] * dtaps[0]
@@ -877,6 +1118,9 @@
         tv = taps[o] * vt[o]
         move = (o - REACH) % t
         rt[o * 8 : o * 8 + 8, :] = pltpu.roll(tv, move, 1) if move else tv
+
+    done_with(2)
+    arrived(*range(3, 10))
 
     def point_tile(i, carry):
         r0 = pl.multiple_of(i * 384, 128)
@@ -895,6 +1139,7 @@
         return carry
 
     lax.fori_loop(0, t // 384, point_tile, 0)
+    done_with(*range(3, 10))
 
     def dc_tile(i, carry):
         r0 = pl.multiple_of(i * 128, 128)
@@ -910,6 +1155,7 @@
 
     lax.fori_loop(0, t // 128, dc_tile, 0)
 
+    arrived(10, 11)
     for j in range(nch):
         xs[j, 8 : t + 8, :] = x_ref[0, :, pl.ds(j * 128, 128)].astype(F32)
 
@@ -923,6 +1169,8 @@
         return carry
 
     lax.fori_loop(0, t // 384, proj_tile, 0)
+
+    done_with(10, 11)
 
     def depth_tile(r0, masked):
         masks = mask_rows(segb, r0, 128) if masked else None
@@ -943,6 +1191,14 @@
 
     masked_tiles(t, depth_tile)
 
+    arrived(12)
+
+    @pl.when(b > 0)
+    def _():
+        for j in range(nch):
+            for copy in put_back(j, b - 1):
+                copy.wait()
+
     for j in range(nch):
         cols = pl.ds(j * 128, 128)
         pad[j, pl.ds(t, 128), :] = pad[j, 0:128, :]
@@ -956,6 +1212,9 @@
         pad[j, pl.ds(t, 128), :] = pad[j, 0:128, :]
         out_ref[0, 0:128, cols] = pad[j, first, :].astype(BF16)
         out_ref[0, 128:, cols] = pad[j, pl.ds(128 - s, t - 128), :].astype(BF16)
+        for copy in put_back(j, b):
+            copy.start()
+    done_with(12)
 
     @pl.when(b == pl.num_programs(0) - 1)
     def _():
@@ -969,11 +1228,7 @@
         col = lax.broadcasted_iota(jnp.int32, (128, 72), 1)
         order = jnp.where((row < HEADS * KERNEL) & (row % KERNEL * 8 + row // KERNEL == col), 1.0, 0.0).astype(BF16)
         gk = mm(order, gk_ref[...].astype(BF16)).astype(BF16)
-        row = lax.broadcasted_iota(jnp.int32, (half, d), 0)
-        col = lax.broadcasted_iota(jnp.int32, (half, d), 1)
-        piece = col % PIECE
-        put = jnp.where((piece < PIECE // 2) & (col // PIECE * (PIECE // 2) + piece == row), 1.0, 0.0).astype(BF16)
-        gk = mm(gk, put)
+        gk = mm(gk, piece_rows(d), NT)
         for j in range(nch):
             cols = pl.ds(j * 128, 128)
             pad[0, cols, :] = small[:, cols].T
@@ -988,6 +1243,9 @@
             return c
 
         lax.fori_loop(0, n, emit, 0)
+        for j in range(nch):
+            for copy in put_back(j, b):
+                copy.wait()
 
 
 def stage_e(n, s, segr, x, out_r, dres, dconv, dq, dk, dv, q, c, depth, span, mixed, taps, wp, wd, wpt, wk, gs):
@@ -996,9 +1254,7 @@
     packed = (d * 2 * d + d * half) // (n * half) + d // n
     sds = jax.ShapeDtypeStruct
 
-    def slow(*shape):
-        return pl.BlockSpec((1,) + shape, lambda b, *_: (b,) + (0,) * len(shape), pipeline_mode=pl.Buffered(1))
-
+    blocks = (c, dconv, taps, mixed, q, dq, span, dk, dv, depth, x, dres, out_r)
     return pl.pallas_call(
         kernel_e,
         out_shape=[
@@ -1008,10 +1264,9 @@
             num_scalar_prefetch=1,
             grid=(mb,),
             in_specs=[pl.BlockSpec((pl.Squeezed(), 1, t), lambda b, *_: (b, 0, 0))]
-            + [slow(t, d), slow(t, d), slow(t, d), slow(t, half), slow(t, half), slow(t, half), slow(t, half)]
-            + [slow(t, half), slow(t, half), slow(t, d), slow(t, half), slow(t, half), slow(72, t)]
+            + [ANY] * len(blocks)
             + [whole(*w.shape) for w in (wp, wd, wpt, wk, gs)],
-            out_specs=[slow(t, d), slow(t, d), whole(n, packed, half)],
+            out_specs=[ANY, ANY, whole(n, packed, half)],
             scratch_shapes=[
                 pltpu.VMEM((d // 128, t + 128, 128), F32),
                 pltpu.VMEM((d // 128, t + 16, 128), F32),
@@ -1020,7 +1275,7 @@
                 pltpu.VMEM((half // 128, t + 16, 128), F32),
                 pltpu.VMEM((d // 128, t + 16, 128), F32),
                 pltpu.VMEM((144, KERNEL * half), BF16),
-                pltpu.VMEM((KERNEL * 768, 128), BF16),
+                pltpu.VMEM((KERNEL * half, 128), BF16),
                 pltpu.VMEM((128, KERNEL * half), F32),
                 pltpu.VMEM((72, t), F32),
                 pltpu.VMEM((72, t), F32),
@@ -1031,33 +1286,59 @@
                 pltpu.VMEM(wpt.shape, F32),
                 pltpu.VMEM((72, half), F32),
                 pltpu.VMEM((128, d), F32),
+            ]
+            + [pltpu.VMEM((1,) + v.shape[1:], v.dtype) for v in blocks]
+            + [
+                pltpu.VMEM((1, t, d), F32),
+                pltpu.VMEM((1, t, d), BF16),
+                pltpu.SemaphoreType.DMA((len(blocks),)),
+                pltpu.SemaphoreType.DMA((2, d // 128)),
             ],
         ),
         compiler_params=params(1),
         name="mix_bwd",
-    )(s, segr, x, out_r, dres, dconv, dq, dk, dv, q, c, depth, span, mixed, taps, wp, wd, wpt, wk, gs)
-
-
-def rolled_segments(segments):
+    )(s, segr, *blocks, wp, wd, wpt, wk, gs)
+
+
+def prep_kernel(seg_ref, wd_ref, wk_ref, norm_ref, s_ref, segr_ref, small_ref, flip):
+    mb, t = seg_ref.shape
+    span = t - SEG_MOST + 1
+    pos = lanes((1, t))
+    for b in range(mb):
+        row = seg_ref[b : b + 1, :].astype(F32)
+        later = pltpu.roll(jnp.broadcast_to(row, (8, t)), t - (SEG_MOST - 1), 1)
+        hit = (later[0:1, :] == row) & (pos < span)
+        s = jnp.sum(jnp.where(hit, pos.astype(F32), 0.0)).astype(jnp.int32)
+        s_ref[b] = s
+        segr_ref[b] = pltpu.roll(jnp.broadcast_to(row, (8, t)), t - s, 1)[0:1, :]
+    flip[...] = jnp.zeros_like(flip)
+    rows = wd_ref.shape[0]
+    flip[0:4, 0:rows] = norm_ref[...].astype(F32)
+    small_ref[...] = jnp.zeros_like(small_ref)
+    small_ref[:, 0:KERNEL] = wd_ref[...].astype(F32)
+    small_ref[:, 16:20] = flip[...].T[0:rows, 0:4]
+    row = lax.broadcasted_iota(jnp.int32, (HEADS * KERNEL, 8 * KERNEL), 0)
+    col = lanes((HEADS * KERNEL, 8 * KERNEL))
+    order = jnp.where(row % KERNEL * 8 + row // KERNEL == col, 1.0, 0.0).astype(BF16)
+    heads = mm(wk_ref[...], order)
+    small = PIECE // 2
+    for p in range(rows // PIECE):
+        small_ref[p * PIECE : p * PIECE + small, 32 : 32 + 8 * KERNEL] = heads[p * small : (p + 1) * small, :]
+
+
+def prep(segments, w_depth, w_kernel, norms):
     mb, t = segments.shape
-    span = t - SEG_MOST + 1
-    hit = segments[:, :span] == segments[:, SEG_MOST - 1 :]
-    s = jnp.sum(jnp.where(hit, jnp.arange(span, dtype=jnp.int32)[None, :], 0), 1).astype(jnp.int32)
-    twice = jnp.concatenate([segments, segments[:, : t - SEG_MOST]], 1).astype(F32)
-    rows = [lax.dynamic_slice(twice[b], (s[b],), (t,)) for b in range(mb)]
-    return s, jnp.stack(rows)[:, None, :]
-
-
-def pack_small(w_depth, w_kernel, g1, b1, g2, b2):
     rows = w_depth.shape[0]
-    units = rows // PIECE
-    heads = w_kernel.reshape(units, PIECE // 2, HEADS, KERNEL).transpose(0, 1, 3, 2)
-    heads = jnp.pad(heads, ((0, 0), (0, PIECE // 2), (0, 0), (0, 8 - HEADS))).reshape(rows, 8 * KERNEL)
-    norms = jnp.stack([g1, b1, g2, b2], 1)
-    gap = jnp.zeros((rows, 16 - KERNEL), BF16)
-    return jnp.concatenate(
-        [w_depth, gap, norms, jnp.zeros((rows, 128 - 20), BF16), heads, jnp.zeros((rows, 128 - 8 * KERNEL), BF16)], 1
-    )
+    sds = jax.ShapeDtypeStruct
+    vmem = pl.BlockSpec(memory_space=pltpu.VMEM)
+    return pl.pallas_call(
+        prep_kernel,
+        out_shape=[sds((mb,), jnp.int32), sds((mb, 1, t), F32), sds((rows, 128), F32)],
+        in_specs=[vmem] * 4,
+        out_specs=[pl.BlockSpec(memory_space=pltpu.SMEM), vmem, vmem],
+        scratch_shapes=[pltpu.VMEM((128, -(-rows // 128) * 128), F32)],
+        name="prep",
+    )(segments, w_depth, w_kernel, norms)
 
 
 def finish_kernel(f_ref, m_ref, gp_ref, gdep_ref, gpt_ref, gk_ref, go_ref, gi_ref, gd_ref, gs_ref):
@@ -1117,34 +1398,40 @@
     return [lax.psum_scatter(g, "tok", scatter_dimension=0, tiled=True) for g in grads]
 
 
+def rows_of(w):
+    return w.reshape(-1, w.shape[-1])
+
+
 def shards(n, tokens, segments, cotangent, w_proj, w_depth, w_point, w_kernel, w_out, g1, b1, w_in, w_down, g2, b2):
     d = tokens.shape[-1]
     hid = w_in.shape[1]
     units = d // PIECE
     own = n == units
+    norms = [g1, b1, g2, b2]
     if own:
-        small = pack_small(w_depth, w_kernel, g1, b1, g2, b2)
-        full = gather_all(n, [w_proj, w_in, small, w_down, w_point, w_out])
-        wp, wi, sm, wdn, wpt, wo = [w.reshape(-1, w.shape[2]) for w in full]
+        more_a, more_b = [w_out, w_in], [w_in, w_down]
     else:
-        given = [w_proj, w_in, w_down, w_point, w_out, w_depth, w_kernel, g1, b1, g2, b2]
-        wp, wi, wdn, wpt, wo, *rest = [lax.all_gather(w, "tok", axis=0, tiled=True) for w in given]
-        sm = pack_small(*rest)
-    s, segr = rolled_segments(segments[:, 0])
-    segt = segr[:, :, SEG_MOST:]
-    xr, cotr, q, k, v, c, depth, span, mixed, taps, conv, wd_rows, wk_rows = stage_a(
-        s, tokens, cotangent, segr, wp, sm, wpt
-    )
-    ctx, lse = stage_b(segt, q, k, v)
-    out_r, dres, dctx, dconv, gf, g_small = stage_c(units, ctx, conv, xr, cotr, wo, wi, wdn, wd_rows)
-    dq, dk, dv = stage_d(segt, q, k, v, ctx, lse, dctx)
+        given = [w_proj, w_in, w_down, w_point, w_out, w_depth, w_kernel] + norms
+        wp, wi, wdn, wpt, wo, w_depth, w_kernel, *norms = [lax.all_gather(w, "tok", axis=0, tiled=True) for w in given]
+        more_a = more_b = []
+    s, segr, small = prep(segments[:, 0], w_depth, w_kernel, jnp.stack(norms))
+    xr, cotr, wd_rows, wk_rows, *got = stage_front(n, s, tokens, cotangent, small, w_proj, w_point, own)
+    if own:
+        wp, wpt = (rows_of(w) for w in got)
+    q, k, v, c, depth, span, mixed, taps, conv, *got_a = stage_a(n, segr, xr, wp, wd_rows, wpt, wk_rows, more_a)
+    ctx, lse, *got_b = stage_b(n, segr, q, k, v, more_b)
+    if own:
+        wo, wi_a, wi_b, wdn = (rows_of(w) for w in got_a + got_b)
+    else:
+        wi_a, wi_b = jnp.split(wi, 2, 1)
+    out_r, dres, dctx, dconv, gf, g_small = stage_c(units, ctx, conv, xr, cotr, wo, wi_a, wi_b, wdn, wd_rows)
+    dq, dk, dv, *sums = stage_d(n, segr, q, k, v, ctx, lse, dctx, [gf] if own else [])
     gx, out, gm = stage_e(
         units, s, segr, xr, out_r, dres, dconv, dq, dk, dv, q, c, depth, span, mixed, taps, wp, wd_rows, wpt, wk_rows,
         g_small,
     )
     if own:
-        f, m = scatter_all(n, 1, [gf, gm], 2)
-        sums = finish(n, d, hid, f, m)
+        sums = finish(n, d, hid, sums[0], scatter_all(n, 1, [gm], 6)[0])
     else:
         sums = native_sums(gf, gm, d, hid)
     g_proj, g_depth, g_point, g_kernel, g_out, g_in, g_down, g_vec = sums

time: 460 us -> 358 us (0.78); the launches traced: 454 us -> 357 us
  Pallas kernels: 438 us -> 349 us
  local copies, waits for them, and re-layouts: 10.4 us -> 5.64 us
    pallas_call x1, Pallas kernels: 67.7 us -> 31.8 us  [scatter_all(): pl.pallas_call(kernel, out_shape=[jax.ShapeDtypeStruct(w.shape[1:], F32)...]
    pallas_call x1, Pallas kernels: 97.1 us -> 62.4 us  [stage_e(): pl.pallas_call(kernel_e, out_shape=[sds((mb, t, d), F32), sds((mb, t, d),...]
    pallas_call x1, Pallas kernels: 87.8 us -> 75 us  [stage_c(): pl.pallas_call(kernel_c, out_shape=[sds((mb, t, d), BF16), sds((mb, t, d)...]
    pallas_call x4 -> x5, Pallas kernels: 184 us -> 178 us  [the longest x1 58 us: stage_d(): pl.pallas_call(partial(kernel_d, n, cuts), out_shape=[sds((mb, t, half),...]
where the time goes in v4:
time: 358 us; the launch traced here: 357 us
  Pallas kernels  349 us (97%)
  local copies, waits for them, and re-layouts  5.64 us (2%)
    pallas_call x1, Pallas kernels, stage_c(): pl.pallas_call(kernel_c, out_shape=[sds((mb, t, d), BF16), sds((mb, t, d)...  75 us
    pallas_call x1, Pallas kernels, stage_e(): pl.pallas_call(kernel_e, out_shape=[sds((mb, t, d), F32), sds((mb, t, d),...  62.4 us
    pallas_call x1, Pallas kernels, stage_d(): pl.pallas_call(partial(kernel_d, n, cuts), out_shape=[sds((mb, t, half),...  58 us
    pallas_call x1, Pallas kernels, stage_b(): pl.pallas_call(partial(kernel_b, n, layout, len(more)), out_shape=[sds((m...  42.9 us
    pallas_call x1, Pallas kernels, stage_a(): pl.pallas_call(partial(kernel_a, n, layout, len(more)), out_shape=[sds((m...  39.8 us
    pallas_call x1, Pallas kernels, stage_front(): pl.pallas_call(partial(kernel_front, n, layout), out_shape=[sds(*o) for o...  36 us
    pallas_call x1, Pallas kernels, scatter_all(): pl.pallas_call(kernel, out_shape=[jax.ShapeDtypeStruct(w.shape[1:], F32)...  31.8 us

profile of v4, /device:TPU:0, one launch (start us, length us, event | category | flops | bytes accessed | tf_op | source)
XLA Modules:
  0.0 357.1 jit_solution(7188215324826499524)
XLA Ops:
  0.6 1.3 pad_maximum_fusion.norm_ref
  1.9 1.4 copy.29.wd_ref
  3.3 1.3 copy.33
  4.6 1.7 prep.1
  6.3 36.0 %front.1 = (bf16[2,1152,768]{2,1,0:T(8,128)(2,1)}, bf16[2,1152,768]{2,1,0:T(8,128)(2,1)}, f32[24,768]{1,0:T(8,128)}, bf16[72,384]{1,0:T(8,128)(2,1)}, bf16[2,2,2...) custom-call(s32[2]{0:T(128)} %get-tuple-element.58.refs_0_.s_ref, ...), custom_call_target="tpu_custom_call" | custom-call | tf_op jit(solution)/shard_map/front/pallas_call | solution.py:457
  42.4 39.8 %mix_fwd.1 = (bf16[2,1152,384]{2,1,0:T(8,128)(2,1)}, bf16[2,1152,384]{2,1,0:T(8,128)(2,1)}, bf16[2,1152,384]{2,1,0:T(8,128)(2,1)}, bf16[2,1152,384]{2,1,0:T(8,12...) custom-call(f32[2,1,1152]{2,1,0:T(1,128)} %get-tuple-element.59.refs, ...), custom_call_target="tpu_custom_call" | custom-call | tf_op jit(solution)/shard_map/mix_fwd/pallas_call | solution.py:623
  82.1 42.9 %att_fwd.1 = (bf16[2,1152,384]{2,1,0:T(8,128)(2,1)}, f32[2,1152,384]{2,1,0:T(8,128)}, bf16[2,2,2,2,2,24,768]{6,5,4,3,2,1,0:T(8,128)(2,1)}, bf16[2,2,2,2,2,96,384]{6,5,4,3,2,1,0:T(8,128)(2,1)}) custom-call(f32[2,1,1152]{2,1,0:T(1,128)} %get-tuple-element.59.refs_0_.seg_ref, bf16[2,1152,384]{2,1,0:T(8,128)(2,1)} %get-tuple-element.67.refs_1_.q_far, ...), custom_call_target="tpu_custom_call" | custom-call | tf_op jit(solution)/shard_map/att_fwd/pallas_call | solution.py:750
  125.0 75.0 %ffn.1 = (bf16[2,1152,768]{2,1,0:T(8,128)(2,1)}, f32[2,1152,768]{2,1,0:T(8,128)}, bf16[2,1152,384]{2,1,0:T(8,128)(2,1)}, f32[2,1152,384]{2,1,0:T(8,128)}, bf16[3...) custom-call(bf16[2,1152,384]{2,1,0:T(8,128)(2,1)} %get-tuple-element.70.ctx_ref.refs_4_, ...), custom_call_target="tpu_custom_call" | custom-call | tf_op jit(solution)/shard_map/ffn/pallas_call | solution.py:886
  200.1 58.0 %att_bwd.1 = (f32[2,1152,384]{2,1,0:T(8,128)}, bf16[2,1152,384]{2,1,0:T(8,128)(2,1)}, bf16[2,1152,384]{2,1,0:T(8,128)(2,1)}, f32[240,384]{1,0:T(8,128)}) custom-call(f32[2,1,1152]{2,1,0:T(1,128)} %get-tuple-element.59.refs_0_.seg_ref, bf16[2,1152,384]{2,1,0:T(8,128)(2,1)} %get-tuple-element.67.refs_1_.q_far, ...), custom_call_target="tpu_custom_call" | custom-call | tf_op jit(solution)/shard_map/att_bwd/pallas_call | solution.py:1006
  258.1 62.4 %mix_bwd.1 = (f32[2,1152,768]{2,1,0:T(8,128)}, bf16[2,1152,768]{2,1,0:T(8,128)(2,1)}, bf16[32,144,384]{2,1,0:T(8,128)(2,1)}) custom-call(s32[2]{0:T(128)} %get-tuple-element.58.refs_0_.s_ref, f32[2,1,1152]{2,1,0:T(1,128)} %get-tuple-element.59.refs_0_.seg_ref, bf16[2,1152,384]{2,1,0:T(8,128)(2,1)} %get-tuple-element.66.c_far, ...), custom_call_target="tpu_custom_call" | custom-call | tf_op jit(solution)/shard_map/mix_bwd/pallas_call | solution.py:1258
  320.5 31.8 %scatter.1.m_ref = f32[144,384]{1,0:T(8,128)} custom-call(bf16[32,144,384]{2,1,0:T(8,128)(2,1)} %get-tuple-element.94.refs_0_), custom_call_target="tpu_custom_call" | custom-call | tf_op jit(solution)/shard_map/scatter/pallas_call | solution.py:316
  352.3 1.9 finish.1
  354.1 1.6 slice_reduce_fusion
  355.7 1.4 copy.30

commit v5 on v4

--- a/solution.py
+++ b/solution.py
@@ -196,11 +196,13 @@
     return pltpu.CompilerParams(collective_id=cid, has_side_effects=True, vmem_limit_bytes=VMEM_CAP)
 
 
-RATES = {1: 1 / 350e3, 2: 2 / 90e3, 4: 2 / 90e3, 8: 2 / 90e3, 16: 4 / 90e3}
-STAGE = 2.5
-
-
-def schedule(parts, last, spots):
+GATHER_PACE = (2.5, 90e3)
+SCATTER_PACE = (2.2, 95e3)
+
+
+def schedule(parts, last, spots, pace):
+    stage, rate = pace
+    cost = {1: 1 / (4 * rate), 2: 2 / rate, 4: 2 / rate, 8: 2 / rate}
     link = [{1: 0, 2: 1, 4: 2}.get(bit, 3) for bit in range(1 << last)]
     free, ready, at = [0.0] * 4, [0.0] * len(parts), [0] * len(parts)
     plan = []
@@ -212,8 +214,8 @@
                 if at[p] < last:
                     bit = bits[at[p]]
                     begin = max(now, free[link[bit]])
-                    free[link[bit]] = begin + sizes[at[p]] * RATES.get(bit, 4 / 90e3)
-                    ready[p] = free[link[bit]] + STAGE
+                    free[link[bit]] = begin + sizes[at[p]] * cost.get(bit, 4 / rate)
+                    ready[p] = free[link[bit]] + stage
                 at[p] += 1
         plan.append(due)
     plan.append([(p, i) for i in range(last + 1) for p in range(len(parts)) if at[p] <= i])
@@ -221,13 +223,13 @@
 
 
 class Timed:
-    def __init__(self, n, parts, spots=None):
+    def __init__(self, n, parts, spots, pace):
         self.parts = parts
         self.last = n.bit_length() - 1
         self.ticks = self.last + 1
         self.plan = [[(p, t) for p in range(len(parts))] for t in range(self.ticks)]
         if spots is not None:
-            self.plan = schedule([(p.order, p.sizes()) for p in parts], self.last, spots)
+            self.plan = schedule([(p.order, p.sizes()) for p in parts], self.last, spots, pace)
             self.ticks = len(self.plan)
 
     def tick(self, t):
@@ -254,6 +256,7 @@
             for i, (a, *parts) in enumerate(layout)
         ],
         spots,
+        GATHER_PACE,
     )
 
 
@@ -285,6 +288,7 @@
             for j, (i, a, r) in enumerate(cuts)
         ],
         spots,
+        SCATTER_PACE,
     )
 
 
@@ -645,7 +649,7 @@
     )(segr, xr, wp, wd, wpt, wk, *more)
 
 
-QT = 256
+QT = 1024
 
 
 def seg_codes(segb, first):
@@ -655,12 +659,13 @@
     return jnp.where(hot & inside, 1.0, 0.0), jnp.where(inside & ~hot, -1e30, 0.0)
 
 
-def tile_points(n, plan, spots, i, tiles):
+def tile_points(n, plan, spots, i, tiles, h=0, heads=2):
     if plan is None:
         return
     step = pl.program_id(0) * pl.num_programs(1) + pl.program_id(1)
-    for t in range(len(spots)):
-        point((step == t // tiles) & (i == t % tiles), (lambda: greet(n)) if t == 0 else None, plan, t)
+    for t in range(h, len(spots), heads):
+        at = t // heads
+        point((step == at // tiles) & (i == at % tiles), (lambda: greet(n)) if t == 0 else None, plan, t)
 
 
 def end_points(plan):
@@ -670,7 +675,7 @@
     point(last, None, plan, plan.ticks - 1)
 
 
-B_SPOTS = [1.46 * i for i in range(24)]
+B_SPOTS = [5.0 * i for i in range(6)]
 
 
 def kernel_b(n, layout, count, *refs):
@@ -699,11 +704,12 @@
     vs = (jnp.where(low_half, v, one_b), jnp.where(low_half, one_b, v))
 
     def tile(i, carry):
-        tile_points(n, plan, B_SPOTS, i, SEG_MOST // QT)
         rows = pl.ds(pl.multiple_of(i * QT, QT), QT)
         q = q_ref[0, rows, :] * 0.125
         zero = jnp.zeros((), BF16)
-        outs = [one(jnp.where(low_half, q, zero), k, vs[0]), one(jnp.where(low_half, zero, q), k, vs[1])]
+        tile_points(n, plan, B_SPOTS, i, SEG_MOST // QT, heads=1)
+        outs = [one(jnp.where(low_half, q, zero), k, vs[0])]
+        outs.append(one(jnp.where(low_half, zero, q), k, vs[1]))
         finish(rows, [o[0] for o in outs], [o[1] for o in outs])
         return carry
 
@@ -913,8 +919,8 @@
     )(ctx, conv, x, cot, wo, wi_a, wi_b, wdn, ln)
 
 
-KT = 256
-D_SPOTS = [1.98 * i for i in range(24)]
+KT = 512
+D_SPOTS = [1.9 * i for i in range(24)]
 
 
 def kernel_d(n, cuts, *refs):
@@ -970,10 +976,10 @@
     main = pl.ds(0, SEG_MOST)
 
     def tile(i, carry):
-        tile_points(n, plan, D_SPOTS, i, SEG_MOST // KT)
         rows = pl.ds(pl.multiple_of(i * KT, KT), KT)
         halves = []
         for h in range(2):
+            tile_points(n, plan, D_SPOTS, i, SEG_MOST // KT, h)
             ds, dk, dv, k = run(rows, main, h, None)
             part = mm(k[:, 64 * h : 64 * h + 64], ds, TN)
             dqt[64 * h : 64 * h + 64, :] = jnp.where(i == 0, part, dqt[64 * h : 64 * h + 64, :] + part)
@@ -1312,18 +1318,15 @@
         s_ref[b] = s
         segr_ref[b] = pltpu.roll(jnp.broadcast_to(row, (8, t)), t - s, 1)[0:1, :]
     flip[...] = jnp.zeros_like(flip)
-    rows = wd_ref.shape[0]
-    flip[0:4, 0:rows] = norm_ref[...].astype(F32)
-    small_ref[...] = jnp.zeros_like(small_ref)
-    small_ref[:, 0:KERNEL] = wd_ref[...].astype(F32)
-    small_ref[:, 16:20] = flip[...].T[0:rows, 0:4]
-    row = lax.broadcasted_iota(jnp.int32, (HEADS * KERNEL, 8 * KERNEL), 0)
-    col = lanes((HEADS * KERNEL, 8 * KERNEL))
-    order = jnp.where(row % KERNEL * 8 + row // KERNEL == col, 1.0, 0.0).astype(BF16)
-    heads = mm(wk_ref[...], order)
-    small = PIECE // 2
-    for p in range(rows // PIECE):
-        small_ref[p * PIECE : p * PIECE + small, 32 : 32 + 8 * KERNEL] = heads[p * small : (p + 1) * small, :]
+    rows = wd_ref.shape[1]
+    flip[0:KERNEL, 0:rows] = wd_ref[...].astype(F32)
+    flip[16:20, 0:rows] = norm_ref[...].astype(F32)
+    row = lax.broadcasted_iota(jnp.int32, (8 * KERNEL, HEADS * KERNEL), 0)
+    col = lanes((8 * KERNEL, HEADS * KERNEL))
+    order = jnp.where(col % KERNEL * 8 + col // KERNEL == row, 1.0, 0.0).astype(BF16)
+    heads = mm(order, wk_ref[...]).astype(BF16)
+    flip[32 : 32 + 8 * KERNEL, 0:rows] = mm(heads, piece_rows(rows), NT)
+    small_ref[...] = flip[...].T[0:rows, :]
 
 
 def prep(segments, w_depth, w_kernel, norms):
@@ -1338,10 +1341,10 @@
         out_specs=[pl.BlockSpec(memory_space=pltpu.SMEM), vmem, vmem],
         scratch_shapes=[pltpu.VMEM((128, -(-rows // 128) * 128), F32)],
         name="prep",
-    )(segments, w_depth, w_kernel, norms)
-
-
-def finish_kernel(f_ref, m_ref, gp_ref, gdep_ref, gpt_ref, gk_ref, go_ref, gi_ref, gd_ref, gs_ref):
+    )(segments, w_depth.T, w_kernel.T, norms)
+
+
+def finish_kernel(f_ref, m_ref, gp_ref, gdep_ref, gpt_ref, gk_ref, go_ref, gi_ref, gd_ref, gs_ref, flip):
     half = f_ref.shape[1]
     rows = gp_ref.shape[0]
     tall = gd_ref.shape[0]
@@ -1355,10 +1358,12 @@
     for j in range(wide):
         gp_ref[:, j * half : (j + 1) * half] = m_ref[j * rows : (j + 1) * rows, :]
     gpt_ref[...] = m_ref[wide * rows : (wide + 1) * rows, :]
-    small = m_ref[(wide + 1) * rows : (wide + 2) * rows, 0:256]
-    gdep_ref[...] = small[:, 0:KERNEL]
-    gk_ref[...] = small[0 : rows // 2, 128 : 128 + HEADS * KERNEL]
-    gs_ref[...] = small[:, 16:24]
+    flip[...] = jnp.zeros_like(flip)
+    flip[0:rows, :] = m_ref[(wide + 1) * rows : (wide + 2) * rows, 0:256]
+    first = flip[:, 0:128].T
+    gdep_ref[...] = first[0:KERNEL, 0:rows]
+    gs_ref[...] = first[16:24, 0:rows]
+    gk_ref[...] = flip[:, 128:256].T[0 : HEADS * KERNEL, 0 : rows // 2]
 
 
 def finish(n, d, hid, f, m):
@@ -1368,9 +1373,10 @@
     return pl.pallas_call(
         finish_kernel,
         out_shape=[
-            sds((rows, 2 * d), F32), sds((rows, KERNEL), F32), sds((rows, half), F32), sds((half // n, HEADS * KERNEL), F32),
-            sds((rows, d), F32), sds((rows, hid), F32), sds((2 * hid // n, half), F32), sds((rows, 8), F32),
+            sds((rows, 2 * d), F32), sds((KERNEL, rows), F32), sds((rows, half), F32), sds((HEADS * KERNEL, half // n), F32),
+            sds((rows, d), F32), sds((rows, hid), F32), sds((2 * hid // n, half), F32), sds((8, rows), F32),
         ],
+        scratch_shapes=[pltpu.VMEM((128, 256), F32)],
         name="finish",
     )(f, m)
 
@@ -1432,6 +1438,7 @@
     )
     if own:
         sums = finish(n, d, hid, sums[0], scatter_all(n, 1, [gm], 6)[0])
+        sums = [v.T if i in (1, 3, 7) else v for i, v in enumerate(sums)]
     else:
         sums = native_sums(gf, gm, d, hid)
     g_proj, g_depth, g_point, g_kernel, g_out, g_in, g_down, g_vec = sums

time: 358 us -> 343 us (0.958)
  Pallas kernels: 349 us -> 335 us
    pallas_call x1, Pallas kernels: 42.9 us -> 33.3 us  [stage_b(): pl.pallas_call(partial(kernel_b, n, layout, len(more)), out_shape=[sds((m...]
    pallas_call x1, Pallas kernels: 58 us -> 54.2 us  [stage_d(): pl.pallas_call(partial(kernel_d, n, cuts), out_shape=[sds((mb, t, half),...]
where the time goes in v5:
time: 343 us
  Pallas kernels  335 us (98%)
  local copies, waits for them, and re-layouts  5.47 us (2%)
    pallas_call x1, Pallas kernels, stage_c(): pl.pallas_call(kernel_c, out_shape=[sds((mb, t, d), BF16), sds((mb, t, d)...  75 us
    pallas_call x1, Pallas kernels, stage_e(): pl.pallas_call(kernel_e, out_shape=[sds((mb, t, d), F32), sds((mb, t, d),...  62.4 us
    pallas_call x1, Pallas kernels, stage_d(): pl.pallas_call(partial(kernel_d, n, cuts), out_shape=[sds((mb, t, half),...  54.2 us
    pallas_call x1, Pallas kernels, stage_a(): pl.pallas_call(partial(kernel_a, n, layout, len(more)), out_shape=[sds((m...  39.8 us
    pallas_call x1, Pallas kernels, stage_front(): pl.pallas_call(partial(kernel_front, n, layout), out_shape=[sds(*o) for o...  36 us
    pallas_call x1, Pallas kernels, stage_b(): pl.pallas_call(partial(kernel_b, n, layout, len(more)), out_shape=[sds((m...  33.3 us
    pallas_call x1, Pallas kernels, scatter_all(): pl.pallas_call(kernel, out_shape=[jax.ShapeDtypeStruct(w.shape[1:], F32)...  31.1 us

profile of v5, /device:TPU:0, one launch (start us, length us, event | category | flops | bytes accessed | tf_op | source)
XLA Modules:
  0.0 342.9 jit_solution(8269671156350178232)
XLA Ops:
  0.6 1.3 pad_maximum_fusion.norm_ref
  1.9 1.3 copy.31
  3.2 1.4 copy.27
  4.6 1.7 prep.1
  6.3 36.0 %front.1 = (bf16[2,1152,768]{2,1,0:T(8,128)(2,1)}, bf16[2,1152,768]{2,1,0:T(8,128)(2,1)}, f32[24,768]{1,0:T(8,128)}, bf16[72,384]{1,0:T(8,128)(2,1)}, bf16[2,2,2...) custom-call(s32[2]{0:T(128)} %get-tuple-element.58.refs_0_.s_ref, ...), custom_call_target="tpu_custom_call" | custom-call | tf_op jit(solution)/shard_map/front/pallas_call | solution.py:461
  42.3 39.8 %mix_fwd.1 = (bf16[2,1152,384]{2,1,0:T(8,128)(2,1)}, bf16[2,1152,384]{2,1,0:T(8,128)(2,1)}, bf16[2,1152,384]{2,1,0:T(8,128)(2,1)}, bf16[2,1152,384]{2,1,0:T(8,12...) custom-call(f32[2,1,1152]{2,1,0:T(1,128)} %get-tuple-element.59.refs, ...), custom_call_target="tpu_custom_call" | custom-call | tf_op jit(solution)/shard_map/mix_fwd/pallas_call | solution.py:627
  82.1 33.3 %att_fwd.1 = (bf16[2,1152,384]{2,1,0:T(8,128)(2,1)}, f32[2,1152,384]{2,1,0:T(8,128)}, bf16[2,2,2,2,2,24,768]{6,5,4,3,2,1,0:T(8,128)(2,1)}, bf16[2,2,2,2,2,96,384]{6,5,4,3,2,1,0:T(8,128)(2,1)}) custom-call(f32[2,1,1152]{2,1,0:T(1,128)} %get-tuple-element.59.refs_0_.seg_ref, bf16[2,1152,384]{2,1,0:T(8,128)(2,1)} %get-tuple-element.67.refs_1_.q_far, ...), custom_call_target="tpu_custom_call" | custom-call | tf_op jit(solution)/shard_map/att_fwd/pallas_call | solution.py:756
  115.5 75.0 %ffn.1 = (bf16[2,1152,768]{2,1,0:T(8,128)(2,1)}, f32[2,1152,768]{2,1,0:T(8,128)}, bf16[2,1152,384]{2,1,0:T(8,128)(2,1)}, f32[2,1152,384]{2,1,0:T(8,128)}, bf16[3...) custom-call(bf16[2,1152,384]{2,1,0:T(8,128)(2,1)} %get-tuple-element.70.ctx_ref.refs_4_, ...), custom_call_target="tpu_custom_call" | custom-call | tf_op jit(solution)/shard_map/ffn/pallas_call | solution.py:892
  190.5 54.2 %att_bwd.1 = (f32[2,1152,384]{2,1,0:T(8,128)}, bf16[2,1152,384]{2,1,0:T(8,128)(2,1)}, bf16[2,1152,384]{2,1,0:T(8,128)(2,1)}, f32[240,384]{1,0:T(8,128)}) custom-call(f32[2,1,1152]{2,1,0:T(1,128)} %get-tuple-element.59.refs_0_.seg_ref, bf16[2,1152,384]{2,1,0:T(8,128)(2,1)} %get-tuple-element.67.refs_1_.q_far, ...), custom_call_target="tpu_custom_call" | custom-call | tf_op jit(solution)/shard_map/att_bwd/pallas_call | solution.py:1012
  244.7 62.4 %mix_bwd.1 = (f32[2,1152,768]{2,1,0:T(8,128)}, bf16[2,1152,768]{2,1,0:T(8,128)(2,1)}, bf16[32,144,384]{2,1,0:T(8,128)(2,1)}) custom-call(s32[2]{0:T(128)} %get-tuple-element.58.refs_0_.s_ref, f32[2,1,1152]{2,1,0:T(1,128)} %get-tuple-element.59.refs_0_.seg_ref, bf16[2,1152,384]{2,1,0:T(8,128)(2,1)} %get-tuple-element.66.c_far, ...), custom_call_target="tpu_custom_call" | custom-call | tf_op jit(solution)/shard_map/mix_bwd/pallas_call | solution.py:1264
  307.1 31.1 %scatter.1.m_ref = f32[144,384]{1,0:T(8,128)} custom-call(bf16[32,144,384]{2,1,0:T(8,128)(2,1)} %get-tuple-element.94.refs_0_), custom_call_target="tpu_custom_call" | custom-call | tf_op jit(solution)/shard_map/scatter/pallas_call | solution.py:320
  338.2 1.9 finish.1
  340.1 1.4 slice_bitcast_fusion
  341.5 1.4 copy.28

commit v6 on v5

--- a/solution.py
+++ b/solution.py
@@ -409,9 +409,9 @@
 
 
 def front_layout(d, half):
-    cols = pieces(2 * d, 4)
+    cols = pieces(2 * d, 6)
     rest = [(1, (ALL, pl.ds(0, 128))), (1, (ALL, pl.ds(128, half - 128)))]
-    return [(0, cols[0]), (0, cols[1]), (2, (ALL, ALL)), (0, cols[2]), (0, cols[3])] + rest
+    return [(0, cols[0]), (0, cols[1]), (2, (ALL, ALL))] + [(0, c) for c in cols[2:]] + rest
 
 
 def kernel_front(n, layout, *refs):

time: 343 us -> 344 us (level)
  no operation moved by 1% of the time
where the time goes in v6:
time: 344 us; the launch traced here: 343 us
  Pallas kernels  336 us (98%)
  local copies, waits for them, and re-layouts  5.47 us (2%)
    pallas_call x1, Pallas kernels, stage_c(): pl.pallas_call(kernel_c, out_shape=[sds((mb, t, d), BF16), sds((mb, t, d)...  75 us
    pallas_call x1, Pallas kernels, stage_e(): pl.pallas_call(kernel_e, out_shape=[sds((mb, t, d), F32), sds((mb, t, d),...  62.4 us
    pallas_call x1, Pallas kernels, stage_d(): pl.pallas_call(partial(kernel_d, n, cuts), out_shape=[sds((mb, t, half),...  53.9 us
    pallas_call x1, Pallas kernels, stage_a(): pl.pallas_call(partial(kernel_a, n, layout, len(more)), out_shape=[sds((m...  39.5 us
    pallas_call x1, Pallas kernels, stage_front(): pl.pallas_call(partial(kernel_front, n, layout), out_shape=[sds(*o) for o...  36.1 us
    pallas_call x1, Pallas kernels, stage_b(): pl.pallas_call(partial(kernel_b, n, layout, len(more)), out_shape=[sds((m...  33.4 us
    pallas_call x1, Pallas kernels, scatter_all(): pl.pallas_call(kernel, out_shape=[jax.ShapeDtypeStruct(w.shape[1:], F32)...  31.8 us

profile of v6, /device:TPU:0, one launch (start us, length us, event | category | flops | bytes accessed | tf_op | source)
XLA Modules:
  0.0 343.2 jit_solution(16982060689629036930)
XLA Ops:
  0.6 1.3 pad_maximum_fusion.norm_ref
  1.9 1.3 copy.31
  3.2 1.4 copy.27
  4.6 1.7 prep.1
  6.3 36.1 %front.1 = (bf16[2,1152,768]{2,1,0:T(8,128)(2,1)}, bf16[2,1152,768]{2,1,0:T(8,128)(2,1)}, f32[24,768]{1,0:T(8,128)}, bf16[72,384]{1,0:T(8,128)(2,1)}, bf16[2,2,2...) custom-call(s32[2]{0:T(128)} %get-tuple-element.58.refs_0_.s_ref, ...), custom_call_target="tpu_custom_call" | custom-call | tf_op jit(solution)/shard_map/front/pallas_call | solution.py:461
  42.4 39.5 %mix_fwd.1 = (bf16[2,1152,384]{2,1,0:T(8,128)(2,1)}, bf16[2,1152,384]{2,1,0:T(8,128)(2,1)}, bf16[2,1152,384]{2,1,0:T(8,128)(2,1)}, bf16[2,1152,384]{2,1,0:T(8,12...) custom-call(f32[2,1,1152]{2,1,0:T(1,128)} %get-tuple-element.59.refs, ...), custom_call_target="tpu_custom_call" | custom-call | tf_op jit(solution)/shard_map/mix_fwd/pallas_call | solution.py:627
  81.9 33.4 %att_fwd.1 = (bf16[2,1152,384]{2,1,0:T(8,128)(2,1)}, f32[2,1152,384]{2,1,0:T(8,128)}, bf16[2,2,2,2,2,24,768]{6,5,4,3,2,1,0:T(8,128)(2,1)}, bf16[2,2,2,2,2,96,384]{6,5,4,3,2,1,0:T(8,128)(2,1)}) custom-call(f32[2,1,1152]{2,1,0:T(1,128)} %get-tuple-element.59.refs_0_.seg_ref, bf16[2,1152,384]{2,1,0:T(8,128)(2,1)} %get-tuple-element.67.refs_1_.q_far, ...), custom_call_target="tpu_custom_call" | custom-call | tf_op jit(solution)/shard_map/att_fwd/pallas_call | solution.py:756
  115.3 75.0 %ffn.1 = (bf16[2,1152,768]{2,1,0:T(8,128)(2,1)}, f32[2,1152,768]{2,1,0:T(8,128)}, bf16[2,1152,384]{2,1,0:T(8,128)(2,1)}, f32[2,1152,384]{2,1,0:T(8,128)}, bf16[3...) custom-call(bf16[2,1152,384]{2,1,0:T(8,128)(2,1)} %get-tuple-element.70.ctx_ref.refs_4_, ...), custom_call_target="tpu_custom_call" | custom-call | tf_op jit(solution)/shard_map/ffn/pallas_call | solution.py:892
  190.4 53.9 %att_bwd.1 = (f32[2,1152,384]{2,1,0:T(8,128)}, bf16[2,1152,384]{2,1,0:T(8,128)(2,1)}, bf16[2,1152,384]{2,1,0:T(8,128)(2,1)}, f32[240,384]{1,0:T(8,128)}) custom-call(f32[2,1,1152]{2,1,0:T(1,128)} %get-tuple-element.59.refs_0_.seg_ref, bf16[2,1152,384]{2,1,0:T(8,128)(2,1)} %get-tuple-element.67.refs_1_.q_far, ...), custom_call_target="tpu_custom_call" | custom-call | tf_op jit(solution)/shard_map/att_bwd/pallas_call | solution.py:1012
  244.3 62.4 %mix_bwd.1 = (f32[2,1152,768]{2,1,0:T(8,128)}, bf16[2,1152,768]{2,1,0:T(8,128)(2,1)}, bf16[32,144,384]{2,1,0:T(8,128)(2,1)}) custom-call(s32[2]{0:T(128)} %get-tuple-element.58.refs_0_.s_ref, f32[2,1,1152]{2,1,0:T(1,128)} %get-tuple-element.59.refs_0_.seg_ref, bf16[2,1152,384]{2,1,0:T(8,128)(2,1)} %get-tuple-element.66.c_far, ...), custom_call_target="tpu_custom_call" | custom-call | tf_op jit(solution)/shard_map/mix_bwd/pallas_call | solution.py:1264
  306.7 31.8 %scatter.1.m_ref = f32[144,384]{1,0:T(8,128)} custom-call(bf16[32,144,384]{2,1,0:T(8,128)(2,1)} %get-tuple-element.94.refs_0_), custom_call_target="tpu_custom_call" | custom-call | tf_op jit(solution)/shard_map/scatter/pallas_call | solution.py:320
  338.5 1.9 finish.1
  340.4 1.4 slice_bitcast_fusion
  341.7 1.4 copy.28
